TPU v7x, 512 devices: a whole 4x8x8 slice. The times are simulated.
512 devices in a mesh: tm: 16 (over y_lo, x, core), space: 32 (over y_hi, z).
Axes of the slice: x: 4, y: 8 (y_hi: 4, y_lo: 2; y = y_hi * 2 + y_lo), z: 8, core: 2. Of those that a mesh axis runs over, the one named last changes fastest.
Arguments:
- rhs_nodes: bfloat16 [16, 384, 4096], P('tm', None, 'space'), may hold values from -6 to 6
- rhs_arrow: float32 [384, 512], replicated, may hold values from -6 to 6
- coupling: bfloat16 [16, 4096, 4096], P('tm', 'space'), may hold values from -0.25 to 0.25
- pattern: int32 [16, 32, 32], P('tm', 'space'), may hold values 0 or 1
- pivot_inverse: bfloat16 [16, 4096, 4096], P('tm', 'space'), may hold values from -0.09375 to 0.09375
- arrow_factor: bfloat16 [16, 512, 4096], P('tm', None, 'space'), may hold values from -0.09375 to 0.09375
- tip_inverse: bfloat16 [512, 512], replicated, may hold values from -0.25 to 0.25
Outputs:
- solved: bfloat16 [16, 384, 4096], P('tm', None, 'space')
- arrow_solved: float32 [384, 512], replicated
All inputs are finite; a program needn't handle non-finite values. No bound on the sum of `pattern` on one device may be relied on, other than what follows from the above.
Results may differ from a plain program's by a relative error of at most 0.015.
Values may be sent and summed in bfloat16 or wider, within the bound.
No kernel may reach another device: no remote copies, remote signals or barrier semaphores. Data moves between devices by JAX's collectives and lax.ppermute only.
A program may use at most 64 MiB of HBM per device.

v0:
```python
import jax
import jax.numpy as jnp
from jax import lax
from jax.sharding import PartitionSpec as P

TILE = 128


def shifted(value, axis, steps):
    count = lax.axis_size(axis)
    leading, last = (max(0, -steps), min(count, count - steps))
    return lax.ppermute(value, axis, [(source, source + steps) for source in range(leading, last)])


def per_device(rhs_nodes, rhs_arrow, coupling, pattern, pivot_inverse, arrow_factor, tip_inverse):
    local_steps, local_rows, node_count = coupling.shape
    rhs_count = rhs_nodes.shape[1]
    tile_rows = local_rows // TILE
    tile_cols = node_count // TILE
    weights = pattern.astype(jnp.bfloat16)[:, :, None, :, None]
    masked = (coupling.reshape(local_steps, tile_rows, TILE, tile_cols, TILE) * weights).reshape(
        local_steps, local_rows, node_count
    )
    pieces = 8
    width = rhs_count // pieces
    sections = lax.axis_size("tm")
    position = lax.axis_index("tm")
    rounds = sections + pieces - 1
    contract = (((1,), (1,)), ((), ()))

    def advance(step, gathered, start):
        linked = lax.dot_general(
            gathered, masked[step], contract, preferred_element_type=jnp.float32
        )
        source = lax.dynamic_slice_in_dim(rhs_nodes[step], start, width, 0)
        return (source.astype(jnp.float32) - linked).astype(jnp.bfloat16)

    def store(chain, step, fresh, start, valid):
        current = lax.dynamic_slice_in_dim(chain[step], start, width, 0)
        kept = jnp.where(valid, fresh, current)
        return chain.at[step].set(lax.dynamic_update_slice_in_dim(chain[step], kept, start, 0))

    def placement(turn):
        block = turn - position
        valid = (block >= 0) & (block < pieces)
        start = jnp.clip(block, 0, pieces - 1) * width
        return (valid, start)

    chain = jnp.zeros((local_steps, rhs_count, local_rows), jnp.bfloat16)

    def one_round(turn, state):
        incoming, chain = state
        valid, start = placement(turn)
        gathered = lax.all_gather(incoming, "space", axis=1, tiled=True)
        incoming = advance(0, gathered, start)
        chain = store(chain, 0, incoming, start, valid)
        incoming = shifted(incoming, "tm", 1)
        return (incoming, chain)

    initial = (jnp.zeros((width, local_rows), jnp.bfloat16), chain)
    final_state = lax.fori_loop(0, rounds, one_round, initial)
    chain = final_state[1]
    solved = jnp.einsum(
        "srm,sqm->srq",
        lax.all_gather(chain, "space", axis=2, tiled=True),
        pivot_inverse,
        preferred_element_type=jnp.float32,
    ).astype(jnp.bfloat16)
    terms = jnp.einsum("srq,saq->ra", chain, arrow_factor, preferred_element_type=jnp.float32)
    arrow_sum = lax.psum(terms, ("tm", "space"))
    rest = (rhs_arrow - arrow_sum).astype(jnp.bfloat16)
    arrow_solved = lax.dot_general(rest, tip_inverse, contract, preferred_element_type=jnp.float32)
    return (solved, arrow_solved)


def solution(mesh):
    placed = (
        P("tm", None, "space"),
        P(),
        P("tm", "space", None),
        P("tm", "space", None),
        P("tm", "space", None),
        P("tm", None, "space"),
        P(),
    )
    return jax.shard_map(
        per_device,
        mesh=mesh,
        in_specs=placed,
        out_specs=(P("tm", None, "space"), P()),
        check_vma=False,
    )
```

profile of v0, /device:TPU:1, one launch (start us, length us, event | category | flops | bytes accessed | tf_op | source)
XLA Modules:
  0.0 2308.5 jit_solution(15668588265883571039)
XLA Ops:
  8.8 1.4 copy.10
  10.5 1961.1 %while.19 = (s32[]{:T(128)}, bf16[48,128]{1,0:T(8,128)(2,1)S(1)}, bf16[1,384,128]{2,1,0:T(8,128)(2,1)S(1)}, s32[]{:T(128)}, bf16[1,384,128]{2,1,0:T(8,128)(2,1)}...) while((s32[]{:T(128)}, bf16[48,128]{1,0:T(8,128)(2,1)S(1)}, ...), condition=%wide.region_1.2_spmd, body=%wide.region_0.1_spmd.sunk | while | flops 50356236 | bytes 1970445 | solution.py:61
  10.5 77.0 %all_gather.16 = bf16[48,4096]{1,0:T(8,128)(2,1)S(1)} all-gather(bf16[48,128]{1,0:T(8,128)(2,1)S(1)} %get-tuple-element.266), channel_id=1, replica_groups=mesh['tm'=16,'space'=32] {'space'}, dimensions={1}, use_global_device_ids=true | all-gather | bytes 405504 | tf_op jit(solution)/shard_map/while/body/eval_jaxpr/all_gather | solution.py:54
  87.5 1.2 bitcast_dynamic-update-slice_fusion.2
  88.7 18.2 collective-permute-start
  107.7 64.0 %all_gather.16 = bf16[48,4096]{1,0:T(8,128)(2,1)S(1)} all-gather(bf16[48,128]{1,0:T(8,128)(2,1)S(1)} %get-tuple-element.266), channel_id=1, replica_groups=mesh['tm'=16,'space'=32] {'space'}, dimensions={1}, use_global_device_ids=true | all-gather | bytes 405504 | tf_op jit(solution)/shard_map/while/body/eval_jaxpr/all_gather | solution.py:54
  171.7 1.2 bitcast_dynamic-update-slice_fusion.2
  172.9 17.9 collective-permute-start
  191.6 66.1 %all_gather.16 = bf16[48,4096]{1,0:T(8,128)(2,1)S(1)} all-gather(bf16[48,128]{1,0:T(8,128)(2,1)S(1)} %get-tuple-element.266), channel_id=1, replica_groups=mesh['tm'=16,'space'=32] {'space'}, dimensions={1}, use_global_device_ids=true | all-gather | bytes 405504 | tf_op jit(solution)/shard_map/while/body/eval_jaxpr/all_gather | solution.py:54
  259.0 17.2 collective-permute-start
  276.9 63.8 %all_gather.16 = bf16[48,4096]{1,0:T(8,128)(2,1)S(1)} all-gather(bf16[48,128]{1,0:T(8,128)(2,1)S(1)} %get-tuple-element.266), channel_id=1, replica_groups=mesh['tm'=16,'space'=32] {'space'}, dimensions={1}, use_global_device_ids=true | all-gather | bytes 405504 | tf_op jit(solution)/shard_map/while/body/eval_jaxpr/all_gather | solution.py:54
  340.7 1.2 bitcast_dynamic-update-slice_fusion.2
  342.0 18.7 collective-permute-start
  361.5 64.8 %all_gather.16 = bf16[48,4096]{1,0:T(8,128)(2,1)S(1)} all-gather(bf16[48,128]{1,0:T(8,128)(2,1)S(1)} %get-tuple-element.266), channel_id=1, replica_groups=mesh['tm'=16,'space'=32] {'space'}, dimensions={1}, use_global_device_ids=true | all-gather | bytes 405504 | tf_op jit(solution)/shard_map/while/body/eval_jaxpr/all_gather | solution.py:54
  427.5 18.2 collective-permute-start
  446.6 64.0 %all_gather.16 = bf16[48,4096]{1,0:T(8,128)(2,1)S(1)} all-gather(bf16[48,128]{1,0:T(8,128)(2,1)S(1)} %get-tuple-element.266), channel_id=1, replica_groups=mesh['tm'=16,'space'=32] {'space'}, dimensions={1}, use_global_device_ids=true | all-gather | bytes 405504 | tf_op jit(solution)/shard_map/while/body/eval_jaxpr/all_gather | solution.py:54
  510.5 1.2 bitcast_dynamic-update-slice_fusion.2
  511.8 18.4 collective-permute-start
  531.0 65.5 %all_gather.16 = bf16[48,4096]{1,0:T(8,128)(2,1)S(1)} all-gather(bf16[48,128]{1,0:T(8,128)(2,1)S(1)} %get-tuple-element.266), channel_id=1, replica_groups=mesh['tm'=16,'space'=32] {'space'}, dimensions={1}, use_global_device_ids=true | all-gather | bytes 405504 | tf_op jit(solution)/shard_map/while/body/eval_jaxpr/all_gather | solution.py:54
  596.5 1.2 bitcast_dynamic-update-slice_fusion.2
  597.7 17.9 collective-permute-start
  616.4 63.5 %all_gather.16 = bf16[48,4096]{1,0:T(8,128)(2,1)S(1)} all-gather(bf16[48,128]{1,0:T(8,128)(2,1)S(1)} %get-tuple-element.266), channel_id=1, replica_groups=mesh['tm'=16,'space'=32] {'space'}, dimensions={1}, use_global_device_ids=true | all-gather | bytes 405504 | tf_op jit(solution)/shard_map/while/body/eval_jaxpr/all_gather | solution.py:54
  679.9 1.2 bitcast_dynamic-update-slice_fusion.2
  681.1 18.2 collective-permute-start
  700.1 65.1 %all_gather.16 = bf16[48,4096]{1,0:T(8,128)(2,1)S(1)} all-gather(bf16[48,128]{1,0:T(8,128)(2,1)S(1)} %get-tuple-element.266), channel_id=1, replica_groups=mesh['tm'=16,'space'=32] {'space'}, dimensions={1}, use_global_device_ids=true | all-gather | bytes 405504 | tf_op jit(solution)/shard_map/while/body/eval_jaxpr/all_gather | solution.py:54
  765.2 1.2 bitcast_dynamic-update-slice_fusion.2
  766.4 18.8 collective-permute-start
  786.1 63.6 %all_gather.16 = bf16[48,4096]{1,0:T(8,128)(2,1)S(1)} all-gather(bf16[48,128]{1,0:T(8,128)(2,1)S(1)} %get-tuple-element.266), channel_id=1, replica_groups=mesh['tm'=16,'space'=32] {'space'}, dimensions={1}, use_global_device_ids=true | all-gather | bytes 405504 | tf_op jit(solution)/shard_map/while/body/eval_jaxpr/all_gather | solution.py:54
  850.9 18.1 collective-permute-start
  869.9 65.2 %all_gather.16 = bf16[48,4096]{1,0:T(8,128)(2,1)S(1)} all-gather(bf16[48,128]{1,0:T(8,128)(2,1)S(1)} %get-tuple-element.266), channel_id=1, replica_groups=mesh['tm'=16,'space'=32] {'space'}, dimensions={1}, use_global_device_ids=true | all-gather | bytes 405504 | tf_op jit(solution)/shard_map/while/body/eval_jaxpr/all_gather | solution.py:54
  935.1 1.2 bitcast_dynamic-update-slice_fusion.2
  936.3 18.3 collective-permute-start
  955.4 63.9 %all_gather.16 = bf16[48,4096]{1,0:T(8,128)(2,1)S(1)} all-gather(bf16[48,128]{1,0:T(8,128)(2,1)S(1)} %get-tuple-element.266), channel_id=1, replica_groups=mesh['tm'=16,'space'=32] {'space'}, dimensions={1}, use_global_device_ids=true | all-gather | bytes 405504 | tf_op jit(solution)/shard_map/while/body/eval_jaxpr/all_gather | solution.py:54
  1020.5 18.0 collective-permute-start
  1039.3 65.8 %all_gather.16 = bf16[48,4096]{1,0:T(8,128)(2,1)S(1)} all-gather(bf16[48,128]{1,0:T(8,128)(2,1)S(1)} %get-tuple-element.266), channel_id=1, replica_groups=mesh['tm'=16,'space'=32] {'space'}, dimensions={1}, use_global_device_ids=true | all-gather | bytes 405504 | tf_op jit(solution)/shard_map/while/body/eval_jaxpr/all_gather | solution.py:54
  1105.2 1.2 bitcast_dynamic-update-slice_fusion.2
  1106.4 17.7 collective-permute-start
  1124.9 63.7 %all_gather.16 = bf16[48,4096]{1,0:T(8,128)(2,1)S(1)} all-gather(bf16[48,128]{1,0:T(8,128)(2,1)S(1)} %get-tuple-element.266), channel_id=1, replica_groups=mesh['tm'=16,'space'=32] {'space'}, dimensions={1}, use_global_device_ids=true | all-gather | bytes 405504 | tf_op jit(solution)/shard_map/while/body/eval_jaxpr/all_gather | solution.py:54
  1188.6 1.2 bitcast_dynamic-update-slice_fusion.2
  1189.8 18.0 collective-permute-start
  1208.6 65.1 %all_gather.16 = bf16[48,4096]{1,0:T(8,128)(2,1)S(1)} all-gather(bf16[48,128]{1,0:T(8,128)(2,1)S(1)} %get-tuple-element.266), channel_id=1, replica_groups=mesh['tm'=16,'space'=32] {'space'}, dimensions={1}, use_global_device_ids=true | all-gather | bytes 405504 | tf_op jit(solution)/shard_map/while/body/eval_jaxpr/all_gather | solution.py:54
  1273.7 1.2 bitcast_dynamic-update-slice_fusion.2
  1275.0 18.5 collective-permute-start
  1294.3 63.9 %all_gather.16 = bf16[48,4096]{1,0:T(8,128)(2,1)S(1)} all-gather(bf16[48,128]{1,0:T(8,128)(2,1)S(1)} %get-tuple-element.266), channel_id=1, replica_groups=mesh['tm'=16,'space'=32] {'space'}, dimensions={1}, use_global_device_ids=true | all-gather | bytes 405504 | tf_op jit(solution)/shard_map/while/body/eval_jaxpr/all_gather | solution.py:54
  1358.3 1.2 bitcast_dynamic-update-slice_fusion.2
  1359.5 17.9 collective-permute-start
  1378.3 65.0 %all_gather.16 = bf16[48,4096]{1,0:T(8,128)(2,1)S(1)} all-gather(bf16[48,128]{1,0:T(8,128)(2,1)S(1)} %get-tuple-element.266), channel_id=1, replica_groups=mesh['tm'=16,'space'=32] {'space'}, dimensions={1}, use_global_device_ids=true | all-gather | bytes 405504 | tf_op jit(solution)/shard_map/while/body/eval_jaxpr/all_gather | solution.py:54
  1444.5 18.3 collective-permute-start
  1463.6 64.0 %all_gather.16 = bf16[48,4096]{1,0:T(8,128)(2,1)S(1)} all-gather(bf16[48,128]{1,0:T(8,128)(2,1)S(1)} %get-tuple-element.266), channel_id=1, replica_groups=mesh['tm'=16,'space'=32] {'space'}, dimensions={1}, use_global_device_ids=true | all-gather | bytes 405504 | tf_op jit(solution)/shard_map/while/body/eval_jaxpr/all_gather | solution.py:54
  1527.6 1.2 bitcast_dynamic-update-slice_fusion.2
  1528.8 17.9 collective-permute-start
  1547.6 65.1 %all_gather.16 = bf16[48,4096]{1,0:T(8,128)(2,1)S(1)} all-gather(bf16[48,128]{1,0:T(8,128)(2,1)S(1)} %get-tuple-element.266), channel_id=1, replica_groups=mesh['tm'=16,'space'=32] {'space'}, dimensions={1}, use_global_device_ids=true | all-gather | bytes 405504 | tf_op jit(solution)/shard_map/while/body/eval_jaxpr/all_gather | solution.py:54
  1613.9 18.2 collective-permute-start
  1632.9 64.0 %all_gather.16 = bf16[48,4096]{1,0:T(8,128)(2,1)S(1)} all-gather(bf16[48,128]{1,0:T(8,128)(2,1)S(1)} %get-tuple-element.266), channel_id=1, replica_groups=mesh['tm'=16,'space'=32] {'space'}, dimensions={1}, use_global_device_ids=true | all-gather | bytes 405504 | tf_op jit(solution)/shard_map/while/body/eval_jaxpr/all_gather | solution.py:54
  1698.1 18.0 collective-permute-start
  1716.9 65.2 %all_gather.16 = bf16[48,4096]{1,0:T(8,128)(2,1)S(1)} all-gather(bf16[48,128]{1,0:T(8,128)(2,1)S(1)} %get-tuple-element.266), channel_id=1, replica_groups=mesh['tm'=16,'space'=32] {'space'}, dimensions={1}, use_global_device_ids=true | all-gather | bytes 405504 | tf_op jit(solution)/shard_map/while/body/eval_jaxpr/all_gather | solution.py:54
  1783.4 18.1 collective-permute-start
  1802.3 63.5 %all_gather.16 = bf16[48,4096]{1,0:T(8,128)(2,1)S(1)} all-gather(bf16[48,128]{1,0:T(8,128)(2,1)S(1)} %get-tuple-element.266), channel_id=1, replica_groups=mesh['tm'=16,'space'=32] {'space'}, dimensions={1}, use_global_device_ids=true | all-gather | bytes 405504 | tf_op jit(solution)/shard_map/while/body/eval_jaxpr/all_gather | solution.py:54
  1867.1 18.5 collective-permute-start
  1886.3 64.8 %all_gather.16 = bf16[48,4096]{1,0:T(8,128)(2,1)S(1)} all-gather(bf16[48,128]{1,0:T(8,128)(2,1)S(1)} %get-tuple-element.266), channel_id=1, replica_groups=mesh['tm'=16,'space'=32] {'space'}, dimensions={1}, use_global_device_ids=true | all-gather | bytes 405504 | tf_op jit(solution)/shard_map/while/body/eval_jaxpr/all_gather | solution.py:54
  1952.4 18.4 collective-permute-start
  1973.3 321.7 %all-reduce.2.cloned.1.call-done = f32[384,512]{1,0:T(8,128)} async-done(((f32[384,512]{1,0:T(8,128)}), f32[384,512]{1,0:T(8,128)}) %all-reduce.2.cloned.1.call-update) | async-done | bytes 786448 | tf_op jit(solution)/shard_map/psum | solution.py:70
  2295.0 2.6 fusion.12
  2297.6 3.5 fusion.8
  (74 shorter events, 33.6 us)
Async XLA Ops:
  8.0 2289.6 %copy-start = (bf16[1,128,4096]{2,1,0:T(8,128)(2,1)S(1)}, bf16[1,128,4096]{2,1,0:T(8,128)(2,1)}, u32[]{:S(2)}) copy-start(bf16[1,128,4096]{2,1,0:T(8,128)(2,1)} %param.15) | copy-start | bytes 3145732
  8.0 2287.0 %all-reduce.2.cloned.1.call-start = ((), (), s32[]{:S(2)}) async-start(), calls=%async_computation.1 | async-start | bytes 1572864 | tf_op jit(solution)/shard_map/psum | solution.py:70
  10.4 1961.1 %copy-start.3 = (bf16[1,512,128]{2,1,0:T(8,128)(2,1)S(1)}, bf16[1,512,128]{2,1,0:T(8,128)(2,1)}, u32[]{:S(2)}) copy-start(bf16[1,512,128]{2,1,0:T(8,128)(2,1)} %param.16) | copy-start | bytes 393220
  10.4 2284.6 %copy-start.2 = (f32[384,512]{1,0:T(8,128)S(1)}, f32[384,512]{1,0:T(8,128)}, u32[]{:S(2)}) copy-start(f32[384,512]{1,0:T(8,128)} %param.12) | copy-start | bytes 2359300
  88.7 19.0 collective-permute-start
  172.9 18.7 collective-permute-start
  259.0 18.0 collective-permute-start
  342.0 19.5 collective-permute-start
  427.5 19.1 collective-permute-start
  511.8 19.2 collective-permute-start
  597.7 18.7 collective-permute-start
  681.1 19.0 collective-permute-start
  766.4 19.6 collective-permute-start
  850.9 18.9 collective-permute-start
  936.3 19.1 collective-permute-start
  1020.5 18.8 collective-permute-start
  1106.4 18.5 collective-permute-start
  1189.8 18.8 collective-permute-start
  1275.0 19.4 collective-permute-start
  1359.5 18.7 collective-permute-start
  1444.5 19.1 collective-permute-start
  1528.8 18.7 collective-permute-start
  1613.9 19.0 collective-permute-start
  1698.1 18.8 collective-permute-start
  1783.4 18.9 collective-permute-start
  1867.1 19.3 collective-permute-start
  1952.4 19.2 collective-permute-start
  1971.6 1.2 copy-start.1
  1972.8 324.8 %all-gather.2.cloned.1.call-start = ((), (), s32[]{:S(2)}) async-start(), calls=%async_computation | async-start | bytes 3244032 | tf_op jit(solution)/shard_map/all_gather | solution.py:65
Sparse Core Ops, SparseCore 0:
  1972.9 322.0 all-reduce.1
Sparse Core Ops, SparseCore 1:
  1976.9 128.1 all-gather.1
where the time goes:
time: 2310 us
  blocking collectives  1500 us (65%)
  starting transfers between devices  417 us (18%)
  waiting for transfers between devices  341 us (15%)
  matrix products  35.6 us (2%)
    all_gather x23, blocking collectives, one_round(): gathered = lax.all_gather(incoming, 'space', axis=1, tiled=True)  1500 us
    ppermute x23, starting transfers between devices, shifted(): lax.ppermute(value, axis, [(source, source + steps) for source in range(l...  417 us
    psum x1, waiting for transfers between devices, per_device(): arrow_sum = lax.psum(terms, ('tm', 'space'))  322 us
  transfers between devices with their start and end apart: 25, of which 24 were waited for; matrix products, arithmetic and copies ran while one was open for 0% of the time, Pallas kernels for 0%

commit v1 on v0

v1 whole, which is shorter than its diff:
```python
import jax
import jax.numpy as jnp
from jax import lax
from jax.sharding import PartitionSpec as P

TILE = 128
CONTRACT = (((1,), (1,)), ((), ()))


def spread(value, axis):
    count = lax.axis_size(axis)
    copies = jnp.broadcast_to(value[None], (count, *value.shape))
    return lax.all_to_all(copies, axis, 0, 0)


def per_device(rhs_nodes, rhs_arrow, coupling, pattern, pivot_inverse, arrow_factor, tip_inverse):
    _, local_rows, node_count = coupling.shape
    rhs_count = rhs_nodes.shape[1]
    arrow_count = arrow_factor.shape[1]
    steps = lax.axis_size("tm")
    blocks = lax.axis_size("space")
    width = rhs_count // steps
    arrow_rows = arrow_count // blocks
    section = lax.axis_index("tm")
    block = lax.axis_index("space")

    weights = pattern.astype(jnp.bfloat16)[:, :, None, :, None]
    masked = (coupling.reshape(1, local_rows // TILE, TILE, node_count // TILE, TILE) * weights).reshape(
        1, local_rows, node_count
    )
    links = lax.all_gather(masked, "tm", axis=0, tiled=True)
    source = lax.all_to_all(rhs_nodes.reshape(steps, width, local_rows), "tm", 0, 0)
    arrows = lax.all_to_all(arrow_factor.reshape(blocks, arrow_rows, local_rows), "space", 0, 0)
    arrows = arrows.transpose(1, 0, 2).reshape(1, arrow_rows, node_count)
    outputs = lax.all_gather(jnp.concatenate([pivot_inverse, arrows], 1), "tm", axis=0, tiled=True)

    previous = jnp.zeros((width, node_count), jnp.bfloat16)
    history = []
    for step in range(steps):
        linked = lax.dot_general(previous, links[step], CONTRACT, preferred_element_type=jnp.float32)
        fresh = (source[step].astype(jnp.float32) - linked).astype(jnp.bfloat16)
        previous = spread(fresh, "space").transpose(1, 0, 2).reshape(width, node_count)
        history.append(previous)
    whole = jnp.stack(history)
    results = jnp.einsum("trm,tqm->trq", whole, outputs, preferred_element_type=jnp.float32)
    solved = results[:, :, :local_rows].astype(jnp.bfloat16)
    arrow_sum = jnp.sum(results[:, :, local_rows:], 0)

    own = lax.dynamic_slice(rhs_arrow, (section * width, block * arrow_rows), (width, arrow_rows))
    rest = spread((own - arrow_sum).astype(jnp.bfloat16), "space")
    rest = rest.transpose(1, 0, 2).reshape(width, arrow_count)
    rest = spread(rest, "tm").reshape(rhs_count, arrow_count)
    arrow_solved = lax.dot_general(rest, tip_inverse, CONTRACT, preferred_element_type=jnp.float32)
    solved = lax.all_to_all(solved, "tm", 0, 0).reshape(1, rhs_count, local_rows)
    return (solved, arrow_solved)


def solution(mesh):
    placed = (
        P("tm", None, "space"),
        P(),
        P("tm", "space", None),
        P("tm", "space", None),
        P("tm", "space", None),
        P("tm", None, "space"),
        P(),
    )
    return jax.shard_map(
        per_device,
        mesh=mesh,
        in_specs=placed,
        out_specs=(P("tm", None, "space"), P()),
        check_vma=False,
    )
```

time: 2310 us -> 507 us (0.22)
  blocking collectives: 1500 us -> 40.8 us
  starting transfers between devices: 417 us -> 108 us
  waiting for transfers between devices: 341 us -> 272 us
  local copies, waits for them, and re-layouts: 1.54 us -> 27.8 us
    all_gather x23 -> x0, blocking collectives: 1500 us -> none  [one_round(): gathered = lax.all_gather(incoming, 'space', axis=1, tiled=True)]
    ppermute x23 -> x0, starting transfers between devices: 417 us -> none  [shifted(): lax.ppermute(value, axis, [(source, source + steps) for source in range(l...]
    psum x1 -> x0, waiting for transfers between devices: 322 us -> none  [per_device(): arrow_sum = lax.psum(terms, ('tm', 'space'))]
    all_to_all x0 -> x19, waiting for transfers between devices: none -> 210 us  [the longest x18 204 us: spread(): return lax.all_to_all(copies, axis, 0, 0)]
    all_to_all x0 -> x19, starting transfers between devices: none -> 108 us  [the longest x18 83 us: spread(): return lax.all_to_all(copies, axis, 0, 0)]
    all_gather x1 -> x2, waiting for transfers between devices: 0.01 us -> 61.9 us  [the longest x1 61.9 us: per_device(): links = lax.all_gather(masked, 'tm', axis=0, tiled=True)]
    all_to_all x0 -> x2, blocking collectives: none -> 40.8 us  [the longest x1 27.8 us: per_device(): lax.all_to_all(arrow_factor.reshape(blocks, arrow_rows, local_rows), 'spa...]
  transfers between devices with their start and end apart: 25 -> 21, of which waited for: 24 -> 20; matrix products, arithmetic and copies ran while one was open for 0% -> 10% of each run, Pallas kernels for 0% -> 0%
where the time goes in v1:
time: 507 us; the launch traced here: 505 us
  waiting for transfers between devices  272 us (54%)
  starting transfers between devices  108 us (21%)
  blocking collectives  40.8 us (8%)
  matrix products  36.9 us (7%)
  local copies, waits for them, and re-layouts  27.8 us (5%)
  between operations  14.5 us (3%)
    all_to_all x18, waiting for transfers between devices, spread(): return lax.all_to_all(copies, axis, 0, 0)  204 us
    all_to_all x18, starting transfers between devices, spread(): return lax.all_to_all(copies, axis, 0, 0)  83 us
    all_gather x1, waiting for transfers between devices, per_device(): links = lax.all_gather(masked, 'tm', axis=0, tiled=True)  61.9 us
    all_to_all x1, blocking collectives, per_device(): lax.all_to_all(arrow_factor.reshape(blocks, arrow_rows, local_rows), 'spa...  27.8 us
    dot_general x16, matrix products, per_device(): lax.dot_general(previous, links[step], CONTRACT, preferred_element_type=j...  25.7 us
    all_to_all x1, starting transfers between devices, per_device(): lax.all_to_all(solved, 'tm', 0, 0).reshape(1, rhs_count, local_rows)  25.1 us
    all_to_all x1, blocking collectives, per_device(): lax.all_to_all(rhs_nodes.reshape(steps, width, local_rows), 'tm', 0, 0)  13.1 us
    broadcast_in_dim x18, local copies, waits for them, and re-layouts, spread(): copies = jnp.broadcast_to(value[None], (count, *value.shape))  12.4 us
  transfers between devices with their start and end apart: 21, of which 20 were waited for; matrix products, arithmetic and copies ran while one was open for 10% of the time, Pallas kernels for 0%

profile of v1, /device:TPU:1, one launch (start us, length us, event | category | flops | bytes accessed | tf_op | source)
XLA Modules:
  0.0 505.0 jit_solution(713358051471123098)
XLA Ops:
  7.2 0.8 convert_bitcast_fusion
  8.1 2.3 broadcast_multiply_fusion
  10.5 27.8 %all_to_all.105 = bf16[32,16,128]{2,1,0:T(8,128)(2,1)S(1)} all-to-all(bf16[32,16,128]{2,1,0:T(8,128)(2,1)S(1)} %bitcast.288), channel_id=1, replica_groups=mesh['tm'=16,'space'=32] {'space'}, dimensions={0} | all-to-all | bytes 262144 | tf_op jit(solution)/shard_map/all_to_all | solution.py:33
  38.4 1.1 pad_maximum_fusion
  39.5 13.1 %all_to_all.106 = bf16[16,24,128]{2,1,0:T(8,128)(2,1)S(1)} all-to-all(bf16[16,24,128]{2,1,0:T(8,128)(2,1)S(1)} %bitcast.289), channel_id=1, replica_groups=mesh['tm'=16,'space'=32] {'tm'}, dimensions={0} | all-to-all | bytes 196608 | tf_op jit(solution)/shard_map/all_to_all | solution.py:32
  52.6 61.9 %all-gather.3.cloned.1.call-done = bf16[16,128,4096]{2,1,0:T(8,128)(2,1)} async-done(((bf16[1,128,4096]{2,1,0:T(8,128)(2,1)}), bf16[16,128,4096]{2,1,0:T(8,128)(2,1)}) %all-gather.3.cloned.1.call-update) | async-done | bytes 16777232 | tf_op jit(solution)/shard_map/all_gather | solution.py:31
  114.5 1.6 fusion
  116.8 12.2 %all-to-all-start.1 = ((bf16[32,24,128]{2,1,0:T(8,128)(2,1)}), bf16[32,24,128]{2,1,0:T(8,128)(2,1)S(1)}, u32[]{:S(2)}, u32[]{:S(2)}) async-start(bf16[32,24,128]{2,1,0:T(8,128)(2,1)} %broadcast_in_dim.41), calls=%async_computation.1 | async-start | bytes 393216 | tf_op jit(solution)/shard_map/all_to_all | solution.py:13
  129.0 11.8 %all-to-all-done.1 = bf16[32,24,128]{2,1,0:T(8,128)(2,1)S(1)} async-done(((bf16[32,24,128]{2,1,0:T(8,128)(2,1)}), bf16[32,24,128]{2,1,0:T(8,128)(2,1)S(1)}, u32[]{:S(2)}, u32[]{:S(2)}) %all-to-all-start.1) | async-done | bytes 196640 | tf_op jit(solution)/shard_map/all_to_all | solution.py:13
  140.8 1.6 fusion.1
  143.2 5.3 %all-to-all-start.2 = ((bf16[32,24,128]{2,1,0:T(8,128)(2,1)}), bf16[32,24,128]{2,1,0:T(8,128)(2,1)S(1)}, u32[]{:S(2)}, u32[]{:S(2)}) async-start(bf16[32,24,128]{2,1,0:T(8,128)(2,1)} %broadcast_in_dim.42), calls=%async_computation.2 | async-start | bytes 393216 | tf_op jit(solution)/shard_map/all_to_all | solution.py:13
  149.3 12.8 %all-to-all-done.2 = bf16[32,24,128]{2,1,0:T(8,128)(2,1)S(1)} async-done(((bf16[32,24,128]{2,1,0:T(8,128)(2,1)}), bf16[32,24,128]{2,1,0:T(8,128)(2,1)S(1)}, u32[]{:S(2)}, u32[]{:S(2)}) %all-to-all-start.2) | async-done | bytes 196640 | tf_op jit(solution)/shard_map/all_to_all | solution.py:13
  162.3 1.6 fusion.2
  164.6 4.8 all-to-all-start.3
  170.1 12.8 %all-to-all-done.3 = bf16[32,24,128]{2,1,0:T(8,128)(2,1)S(1)} async-done(((bf16[32,24,128]{2,1,0:T(8,128)(2,1)}), bf16[32,24,128]{2,1,0:T(8,128)(2,1)S(1)}, u32[]{:S(2)}, u32[]{:S(2)}) %all-to-all-start.3) | async-done | bytes 196640 | tf_op jit(solution)/shard_map/all_to_all | solution.py:13
  183.1 1.6 fusion.3
  185.4 4.8 all-to-all-start.4
  191.0 12.2 %all-to-all-done.4 = bf16[32,24,128]{2,1,0:T(8,128)(2,1)S(1)} async-done(((bf16[32,24,128]{2,1,0:T(8,128)(2,1)}), bf16[32,24,128]{2,1,0:T(8,128)(2,1)S(1)}, u32[]{:S(2)}, u32[]{:S(2)}) %all-to-all-start.4) | async-done | bytes 196640 | tf_op jit(solution)/shard_map/all_to_all | solution.py:13
  203.3 1.6 fusion.4
  205.6 4.8 all-to-all-start.5
  211.2 12.4 %all-to-all-done.5 = bf16[32,24,128]{2,1,0:T(8,128)(2,1)S(1)} async-done(((bf16[32,24,128]{2,1,0:T(8,128)(2,1)}), bf16[32,24,128]{2,1,0:T(8,128)(2,1)S(1)}, u32[]{:S(2)}, u32[]{:S(2)}) %all-to-all-start.5) | async-done | bytes 196640 | tf_op jit(solution)/shard_map/all_to_all | solution.py:13
  223.7 1.6 fusion.5
  226.0 4.1 all-to-all-start.6
  230.9 12.4 %all-to-all-done.6 = bf16[32,24,128]{2,1,0:T(8,128)(2,1)S(1)} async-done(((bf16[32,24,128]{2,1,0:T(8,128)(2,1)}), bf16[32,24,128]{2,1,0:T(8,128)(2,1)S(1)}, u32[]{:S(2)}, u32[]{:S(2)}) %all-to-all-start.6) | async-done | bytes 196640 | tf_op jit(solution)/shard_map/all_to_all | solution.py:13
  243.4 1.6 fusion.6
  245.8 4.1 all-to-all-start.7
  250.6 11.1 %all-to-all-done.7 = bf16[32,24,128]{2,1,0:T(8,128)(2,1)S(1)} async-done(((bf16[32,24,128]{2,1,0:T(8,128)(2,1)}), bf16[32,24,128]{2,1,0:T(8,128)(2,1)S(1)}, u32[]{:S(2)}, u32[]{:S(2)}) %all-to-all-start.7) | async-done | bytes 196640 | tf_op jit(solution)/shard_map/all_to_all | solution.py:13
  261.7 1.6 fusion.7
  264.1 3.9 all-to-all-start.8
  268.6 11.1 %all-to-all-done.8 = bf16[32,24,128]{2,1,0:T(8,128)(2,1)S(1)} async-done(((bf16[32,24,128]{2,1,0:T(8,128)(2,1)}), bf16[32,24,128]{2,1,0:T(8,128)(2,1)S(1)}, u32[]{:S(2)}, u32[]{:S(2)}) %all-to-all-start.8) | async-done | bytes 196640 | tf_op jit(solution)/shard_map/all_to_all | solution.py:13
  279.9 1.6 fusion.8
  282.2 3.9 all-to-all-start.9
  286.8 11.0 %all-to-all-done.9 = bf16[32,24,128]{2,1,0:T(8,128)(2,1)S(1)} async-done(((bf16[32,24,128]{2,1,0:T(8,128)(2,1)}), bf16[32,24,128]{2,1,0:T(8,128)(2,1)S(1)}, u32[]{:S(2)}, u32[]{:S(2)}) %all-to-all-start.9) | async-done | bytes 196640 | tf_op jit(solution)/shard_map/all_to_all | solution.py:13
  297.9 1.6 fusion.9
  300.2 3.9 all-to-all-start.10
  304.8 11.1 %all-to-all-done.10 = bf16[32,24,128]{2,1,0:T(8,128)(2,1)S(1)} async-done(((bf16[32,24,128]{2,1,0:T(8,128)(2,1)}), bf16[32,24,128]{2,1,0:T(8,128)(2,1)S(1)}, u32[]{:S(2)}, u32[]{:S(2)}) %all-to-all-start.10) | async-done | bytes 196640 | tf_op jit(solution)/shard_map/all_to_all | solution.py:13
  316.0 1.6 fusion.10
  318.3 3.9 all-to-all-start.11
  322.9 11.0 %all-to-all-done.11 = bf16[32,24,128]{2,1,0:T(8,128)(2,1)S(1)} async-done(((bf16[32,24,128]{2,1,0:T(8,128)(2,1)}), bf16[32,24,128]{2,1,0:T(8,128)(2,1)S(1)}, u32[]{:S(2)}, u32[]{:S(2)}) %all-to-all-start.11) | async-done | bytes 196640 | tf_op jit(solution)/shard_map/all_to_all | solution.py:13
  334.0 1.6 fusion.11
  336.4 4.0 all-to-all-start.12
  341.1 10.9 %all-to-all-done.12 = bf16[32,24,128]{2,1,0:T(8,128)(2,1)S(1)} async-done(((bf16[32,24,128]{2,1,0:T(8,128)(2,1)}), bf16[32,24,128]{2,1,0:T(8,128)(2,1)S(1)}, u32[]{:S(2)}, u32[]{:S(2)}) %all-to-all-start.12) | async-done | bytes 196640 | tf_op jit(solution)/shard_map/all_to_all | solution.py:13
  352.1 1.6 fusion.12
  354.4 3.9 all-to-all-start.13
  359.0 11.0 %all-to-all-done.13 = bf16[32,24,128]{2,1,0:T(8,128)(2,1)S(1)} async-done(((bf16[32,24,128]{2,1,0:T(8,128)(2,1)}), bf16[32,24,128]{2,1,0:T(8,128)(2,1)S(1)}, u32[]{:S(2)}, u32[]{:S(2)}) %all-to-all-start.13) | async-done | bytes 196640 | tf_op jit(solution)/shard_map/all_to_all | solution.py:13
  370.2 1.6 fusion.13
  372.5 3.9 all-to-all-start.14
  377.1 11.2 %all-to-all-done.14 = bf16[32,24,128]{2,1,0:T(8,128)(2,1)S(1)} async-done(((bf16[32,24,128]{2,1,0:T(8,128)(2,1)}), bf16[32,24,128]{2,1,0:T(8,128)(2,1)S(1)}, u32[]{:S(2)}, u32[]{:S(2)}) %all-to-all-start.14) | async-done | bytes 196640 | tf_op jit(solution)/shard_map/all_to_all | solution.py:13
  388.4 1.6 fusion.14
  390.7 3.9 all-to-all-start.15
  395.3 11.2 %all-to-all-done.15 = bf16[32,24,128]{2,1,0:T(8,128)(2,1)S(1)} async-done(((bf16[32,24,128]{2,1,0:T(8,128)(2,1)}), bf16[32,24,128]{2,1,0:T(8,128)(2,1)S(1)}, u32[]{:S(2)}, u32[]{:S(2)}) %all-to-all-start.15) | async-done | bytes 196640 | tf_op jit(solution)/shard_map/all_to_all | solution.py:13
  406.6 1.6 fusion.15
  408.9 3.9 all-to-all-start.16
  413.5 11.2 %all-to-all-done.16 = bf16[32,24,128]{2,1,0:T(8,128)(2,1)S(1)} async-done(((bf16[32,24,128]{2,1,0:T(8,128)(2,1)}), bf16[32,24,128]{2,1,0:T(8,128)(2,1)S(1)}, u32[]{:S(2)}, u32[]{:S(2)}) %all-to-all-start.16) | async-done | bytes 196640 | tf_op jit(solution)/shard_map/all_to_all | solution.py:13
  425.5 9.9 %fusion.48 = f32[16,24,144]{2,1,0:T(8,128)S(1)} fusion(bf16[16,24,4096]{2,1,0:T(8,128)(2,1)} %constant_dynamic-update-slice_fusion, bf16[16,144,4096]{2,1,0:T(8,128)(2,1)} %all-gather.5.cloned.1.call-done), kind=kOutput, calls=%fused_computation.120 | convolution fusion | flops 452984832 | bytes 22241280 | tf_op jit(solution)/shard_map/trm,tqm->trq/dot_general | solution.py:45
  435.5 0.8 subtract_convert_fusion
  436.4 0.8 reshape.159
  437.2 3.9 all-to-all-start.19
  441.7 10.5 %all-to-all-done.19 = bf16[32,2,192]{2,1,0:T(2,128)(2,1)S(1)} async-done(((bf16[32,2,192]{2,1,0:T(2,128)(2,1)}), bf16[32,2,192]{2,1,0:T(2,128)(2,1)S(1)}, u32[]{:S(2)}, u32[]{:S(2)}) %all-to-all-start.19) | async-done | bytes 24608 | tf_op jit(solution)/shard_map/all_to_all | solution.py:13
  452.1 25.1 %all-to-all-start.18 = ((bf16[16,24,128]{2,1,0:T(8,128)(2,1)}), bf16[16,24,128]{2,1,0:T(8,128)(2,1)S(1)}, u32[]{:S(2)}, u32[]{:S(2)}) async-start(bf16[16,24,128]{2,1,0:T(8,128)(2,1)} %slice.253), calls=%async_computation.18 | async-start | bytes 196608 | tf_op jit(solution)/shard_map/all_to_all | solution.py:54
  477.4 5.6 %all-to-all-done.18 = bf16[16,24,128]{2,1,0:T(8,128)(2,1)S(1)} async-done(((bf16[16,24,128]{2,1,0:T(8,128)(2,1)}), bf16[16,24,128]{2,1,0:T(8,128)(2,1)S(1)}, u32[]{:S(2)}, u32[]{:S(2)}) %all-to-all-start.18) | async-done | bytes 98336 | tf_op jit(solution)/shard_map/all_to_all | solution.py:54
  483.8 3.9 all-to-all-start.20
  487.7 8.5 %all-to-all-done.20 = bf16[16,24,512]{2,1,0:T(8,128)(2,1)S(1)} async-done(((bf16[16,24,512]{2,1,0:T(8,128)(2,1)}), bf16[16,24,512]{2,1,0:T(8,128)(2,1)S(1)}, u32[]{:S(2)}, u32[]{:S(2)}) %all-to-all-start.20) | async-done | bytes 393248 | tf_op jit(solution)/shard_map/all_to_all | solution.py:13
  496.2 1.3 fusion.49
  (88 shorter events, 27.2 us)
Async XLA Ops:
  7.2 489.1 %copy-start = (bf16[512,512]{1,0:T(8,128)(2,1)S(1)}, bf16[512,512]{1,0:T(8,128)(2,1)}, u32[]{:S(2)}) copy-start(bf16[512,512]{1,0:T(8,128)(2,1)} %param.13) | copy-start | bytes 1572868
  7.2 3.3 copy-start.2
  7.2 31.2 %copy-start.1 = (bf16[1,128,4096]{2,1,0:T(8,128)(2,1)S(1)}, bf16[1,128,4096]{2,1,0:T(8,128)(2,1)}, u32[]{:S(2)}) copy-start(bf16[1,128,4096]{2,1,0:T(8,128)(2,1)} %param.11) | copy-start | bytes 3145732
  7.2 107.3 %all-gather.3.cloned.1.call-start = ((), (), s32[]{:S(2)}) async-start(), calls=%async_computation.21 | async-start | bytes 17825792 | tf_op jit(solution)/shard_map/all_gather | solution.py:31
  10.4 29.1 %copy-start.3 = (bf16[1,384,128]{2,1,0:T(8,128)(2,1)S(1)}, bf16[1,384,128]{2,1,0:T(8,128)(2,1)}, u32[]{:S(2)}) copy-start(bf16[1,384,128]{2,1,0:T(8,128)(2,1)} %param.7) | copy-start | bytes 294916
  10.4 415.1 %all-gather.5.cloned.1.call-start = ((), (), s32[]{:S(2)}) async-start(), calls=%async_computation.22 | async-start | bytes 20054016 | tf_op jit(solution)/shard_map/all_gather | solution.py:35
  116.8 24.0 %all-to-all-start.1 = ((bf16[32,24,128]{2,1,0:T(8,128)(2,1)}), bf16[32,24,128]{2,1,0:T(8,128)(2,1)S(1)}, u32[]{:S(2)}, u32[]{:S(2)}) async-start(bf16[32,24,128]{2,1,0:T(8,128)(2,1)} %broadcast_in_dim.41), calls=%async_computation.1 | async-start | bytes 393216 | tf_op jit(solution)/shard_map/all_to_all | solution.py:13
  143.2 19.0 %all-to-all-start.2 = ((bf16[32,24,128]{2,1,0:T(8,128)(2,1)}), bf16[32,24,128]{2,1,0:T(8,128)(2,1)S(1)}, u32[]{:S(2)}, u32[]{:S(2)}) async-start(bf16[32,24,128]{2,1,0:T(8,128)(2,1)} %broadcast_in_dim.42), calls=%async_computation.2 | async-start | bytes 393216 | tf_op jit(solution)/shard_map/all_to_all | solution.py:13
  164.6 18.3 %all-to-all-start.3 = ((bf16[32,24,128]{2,1,0:T(8,128)(2,1)}), bf16[32,24,128]{2,1,0:T(8,128)(2,1)S(1)}, u32[]{:S(2)}, u32[]{:S(2)}) async-start(bf16[32,24,128]{2,1,0:T(8,128)(2,1)} %broadcast_in_dim.43), calls=%async_computation.3 | async-start | bytes 393216 | tf_op jit(solution)/shard_map/all_to_all | solution.py:13
  185.4 17.8 %all-to-all-start.4 = ((bf16[32,24,128]{2,1,0:T(8,128)(2,1)}), bf16[32,24,128]{2,1,0:T(8,128)(2,1)S(1)}, u32[]{:S(2)}, u32[]{:S(2)}) async-start(bf16[32,24,128]{2,1,0:T(8,128)(2,1)} %broadcast_in_dim.44), calls=%async_computation.4 | async-start | bytes 393216 | tf_op jit(solution)/shard_map/all_to_all | solution.py:13
  205.6 17.9 %all-to-all-start.5 = ((bf16[32,24,128]{2,1,0:T(8,128)(2,1)}), bf16[32,24,128]{2,1,0:T(8,128)(2,1)S(1)}, u32[]{:S(2)}, u32[]{:S(2)}) async-start(bf16[32,24,128]{2,1,0:T(8,128)(2,1)} %broadcast_in_dim.45), calls=%async_computation.5 | async-start | bytes 393216 | tf_op jit(solution)/shard_map/all_to_all | solution.py:13
  226.0 17.3 %all-to-all-start.6 = ((bf16[32,24,128]{2,1,0:T(8,128)(2,1)}), bf16[32,24,128]{2,1,0:T(8,128)(2,1)S(1)}, u32[]{:S(2)}, u32[]{:S(2)}) async-start(bf16[32,24,128]{2,1,0:T(8,128)(2,1)} %broadcast_in_dim.46), calls=%async_computation.6 | async-start | bytes 393216 | tf_op jit(solution)/shard_map/all_to_all | solution.py:13
  245.8 15.9 %all-to-all-start.7 = ((bf16[32,24,128]{2,1,0:T(8,128)(2,1)}), bf16[32,24,128]{2,1,0:T(8,128)(2,1)S(1)}, u32[]{:S(2)}, u32[]{:S(2)}) async-start(bf16[32,24,128]{2,1,0:T(8,128)(2,1)} %broadcast_in_dim.47), calls=%async_computation.7 | async-start | bytes 393216 | tf_op jit(solution)/shard_map/all_to_all | solution.py:13
  264.1 15.7 %all-to-all-start.8 = ((bf16[32,24,128]{2,1,0:T(8,128)(2,1)}), bf16[32,24,128]{2,1,0:T(8,128)(2,1)S(1)}, u32[]{:S(2)}, u32[]{:S(2)}) async-start(bf16[32,24,128]{2,1,0:T(8,128)(2,1)} %broadcast_in_dim.48), calls=%async_computation.8 | async-start | bytes 393216 | tf_op jit(solution)/shard_map/all_to_all | solution.py:13
  282.2 15.6 %all-to-all-start.9 = ((bf16[32,24,128]{2,1,0:T(8,128)(2,1)}), bf16[32,24,128]{2,1,0:T(8,128)(2,1)S(1)}, u32[]{:S(2)}, u32[]{:S(2)}) async-start(bf16[32,24,128]{2,1,0:T(8,128)(2,1)} %broadcast_in_dim.49), calls=%async_computation.9 | async-start | bytes 393216 | tf_op jit(solution)/shard_map/all_to_all | solution.py:13
  300.2 15.6 %all-to-all-start.10 = ((bf16[32,24,128]{2,1,0:T(8,128)(2,1)}), bf16[32,24,128]{2,1,0:T(8,128)(2,1)S(1)}, u32[]{:S(2)}, u32[]{:S(2)}) async-start(bf16[32,24,128]{2,1,0:T(8,128)(2,1)} %broadcast_in_dim.50), calls=%async_computation.10 | async-start | bytes 393216 | tf_op jit(solution)/shard_map/all_to_all | solution.py:13
  318.3 15.6 %all-to-all-start.11 = ((bf16[32,24,128]{2,1,0:T(8,128)(2,1)}), bf16[32,24,128]{2,1,0:T(8,128)(2,1)S(1)}, u32[]{:S(2)}, u32[]{:S(2)}) async-start(bf16[32,24,128]{2,1,0:T(8,128)(2,1)} %broadcast_in_dim.51), calls=%async_computation.11 | async-start | bytes 393216 | tf_op jit(solution)/shard_map/all_to_all | solution.py:13
  336.4 15.6 %all-to-all-start.12 = ((bf16[32,24,128]{2,1,0:T(8,128)(2,1)}), bf16[32,24,128]{2,1,0:T(8,128)(2,1)S(1)}, u32[]{:S(2)}, u32[]{:S(2)}) async-start(bf16[32,24,128]{2,1,0:T(8,128)(2,1)} %broadcast_in_dim.52), calls=%async_computation.12 | async-start | bytes 393216 | tf_op jit(solution)/shard_map/all_to_all | solution.py:13
  354.4 15.6 %all-to-all-start.13 = ((bf16[32,24,128]{2,1,0:T(8,128)(2,1)}), bf16[32,24,128]{2,1,0:T(8,128)(2,1)S(1)}, u32[]{:S(2)}, u32[]{:S(2)}) async-start(bf16[32,24,128]{2,1,0:T(8,128)(2,1)} %broadcast_in_dim.53), calls=%async_computation.13 | async-start | bytes 393216 | tf_op jit(solution)/shard_map/all_to_all | solution.py:13
  372.5 15.8 %all-to-all-start.14 = ((bf16[32,24,128]{2,1,0:T(8,128)(2,1)}), bf16[32,24,128]{2,1,0:T(8,128)(2,1)S(1)}, u32[]{:S(2)}, u32[]{:S(2)}) async-start(bf16[32,24,128]{2,1,0:T(8,128)(2,1)} %broadcast_in_dim.54), calls=%async_computation.14 | async-start | bytes 393216 | tf_op jit(solution)/shard_map/all_to_all | solution.py:13
  390.7 15.7 %all-to-all-start.15 = ((bf16[32,24,128]{2,1,0:T(8,128)(2,1)}), bf16[32,24,128]{2,1,0:T(8,128)(2,1)S(1)}, u32[]{:S(2)}, u32[]{:S(2)}) async-start(bf16[32,24,128]{2,1,0:T(8,128)(2,1)} %broadcast_in_dim.55), calls=%async_computation.15 | async-start | bytes 393216 | tf_op jit(solution)/shard_map/all_to_all | solution.py:13
  408.9 15.8 %all-to-all-start.16 = ((bf16[32,24,128]{2,1,0:T(8,128)(2,1)}), bf16[32,24,128]{2,1,0:T(8,128)(2,1)S(1)}, u32[]{:S(2)}, u32[]{:S(2)}) async-start(bf16[32,24,128]{2,1,0:T(8,128)(2,1)} %broadcast_in_dim.56), calls=%async_computation.16 | async-start | bytes 393216 | tf_op jit(solution)/shard_map/all_to_all | solution.py:13
  437.2 15.0 %all-to-all-start.19 = ((bf16[32,2,192]{2,1,0:T(2,128)(2,1)}), bf16[32,2,192]{2,1,0:T(2,128)(2,1)S(1)}, u32[]{:S(2)}, u32[]{:S(2)}) async-start(bf16[32,2,192]{2,1,0:T(2,128)(2,1)} %reshape.159), calls=%async_computation.19 | async-start | bytes 65536 | tf_op jit(solution)/shard_map/all_to_all | solution.py:13
  452.1 30.9 %all-to-all-start.18 = ((bf16[16,24,128]{2,1,0:T(8,128)(2,1)}), bf16[16,24,128]{2,1,0:T(8,128)(2,1)S(1)}, u32[]{:S(2)}, u32[]{:S(2)}) async-start(bf16[16,24,128]{2,1,0:T(8,128)(2,1)} %slice.253), calls=%async_computation.18 | async-start | bytes 196608 | tf_op jit(solution)/shard_map/all_to_all | solution.py:54
  483.8 12.4 %all-to-all-start.20 = ((bf16[16,24,512]{2,1,0:T(8,128)(2,1)}), bf16[16,24,512]{2,1,0:T(8,128)(2,1)S(1)}, u32[]{:S(2)}, u32[]{:S(2)}) async-start(bf16[16,24,512]{2,1,0:T(8,128)(2,1)} %broadcast_in_dim.59), calls=%async_computation.20 | async-start | bytes 786432 | tf_op jit(solution)/shard_map/all_to_all | solution.py:13
Sparse Core Ops, SparseCore 0:
  10.5 103.9 all-gather.2
  116.6 130.0 all-gather.4

commit v2 on v1

v2 whole, which is shorter than its diff:
```python
import jax
import jax.numpy as jnp
import numpy as np
from jax import lax
from jax.sharding import Mesh
from jax.sharding import PartitionSpec as P

TILE = 128
CONTRACT = (((1,), (1,)), ((), ()))
AXES = ("yl", "x", "c", "yh", "z")
SIZES = (2, 4, 2, 4, 8)
DEAL = ("yl", "x")
COPY = ("c", "z")
CHAIN = ("yl", "x", "yh")
EARLY = 2


def spread(value, axis):
    count = lax.axis_size(axis)
    copies = jnp.broadcast_to(value[None], (count, *value.shape))
    return lax.all_to_all(copies, axis, 0, 0)


def reorder(rows, deal, piece):
    source = np.arange(TILE)
    upper, lower, blocks = 4, 8, deal
    one = jnp.arange(TILE) // piece
    low = jnp.arange(TILE) % piece
    hot = (
        (one[None, :, None, None] == jnp.arange(blocks)[None, None, :, None])
        & (jnp.arange(lower)[:, None, None, None] == one[None, None, None, :])
        & (low[None, :, None, None] == low[None, None, None, :])
    ).astype(jnp.bfloat16)
    del source
    moved = jnp.einsum(
        "ryzl,zlum->ruym",
        rows.reshape(rows.shape[0], upper, lower, TILE),
        hot,
        preferred_element_type=jnp.float32,
    )
    return moved.astype(jnp.bfloat16).reshape(rows.shape)


def per_device(rhs_nodes, rhs_arrow, coupling, pattern, pivot_inverse, arrow_factor, tip_inverse):
    _, local_rows, node_count = coupling.shape
    rhs_count = rhs_nodes.shape[1]
    arrow_count = arrow_factor.shape[1]
    deal, copies, group = (lax.axis_size(axes) for axes in (DEAL, COPY, CHAIN))
    cores, lower = lax.axis_size("c"), lax.axis_size("z")
    steps = deal * cores
    piece = local_rows // deal
    width = rhs_count // copies
    arrow_rows = arrow_count // group
    mine = lax.axis_index(COPY)

    weights = pattern.astype(jnp.bfloat16)[0, :, None, :, None]
    masked = (coupling.reshape(local_rows // TILE, TILE, node_count // TILE, TILE) * weights).reshape(
        local_rows, node_count
    )
    rows = jnp.concatenate([reorder(masked, deal, piece), rhs_nodes[0].T], 1)
    rows = lax.all_to_all(rows.reshape(deal, piece, -1), DEAL, 0, 0)
    early = spread(rows[:EARLY], COPY)
    late = lax.all_gather(rows[EARLY:], COPY, axis=0)
    out_rows = jnp.concatenate([reorder(pivot_inverse[0], deal, piece), arrow_factor[0].T], 1)
    out_rows = lax.all_to_all(out_rows.reshape(deal, piece, -1), DEAL, 0, 0)
    out_rows = lax.all_gather(out_rows, COPY, axis=0)

    def of_step(held, pair, core):
        return held.reshape(cores, lower, *held.shape[1:])[core, :, pair].reshape(local_rows, -1)

    def link_rows(step):
        pair, core = step // cores, step % cores
        return of_step(early, pair, core) if pair < EARLY else of_step(late, pair - EARLY, core)

    select = (jnp.arange(rhs_count)[None] == mine * width + jnp.arange(width)[:, None]).astype(jnp.bfloat16)
    previous = jnp.zeros((width, node_count), jnp.bfloat16)
    history, parts = [], []
    for step in range(steps):
        held = link_rows(step)
        source = lax.dot_general(select, held[:, node_count:], CONTRACT, preferred_element_type=jnp.float32)
        linked = lax.dot_general(previous, held[:, :node_count], CONTRACT, preferred_element_type=jnp.float32)
        fresh = (source - linked).astype(jnp.bfloat16)
        parts.append(fresh)
        previous = spread(fresh, CHAIN).transpose(1, 0, 2).reshape(width, node_count)
        history.append(previous)

    terms = jnp.zeros((arrow_count, width), jnp.float32)
    solved = []
    for step in range(steps):
        held = of_step(out_rows, step // cores, step % cores)
        terms = terms + lax.dot_general(
            held[:, node_count:], parts[step], (((0,), (1,)), ((), ())), preferred_element_type=jnp.float32
        )
        result = lax.dot_general(
            held[:, :node_count], history[step], CONTRACT, preferred_element_type=jnp.float32
        )
        solved.append(result.astype(jnp.bfloat16))

    place = lax.axis_index(CHAIN)
    own = lax.dynamic_slice(rhs_arrow, (mine * width, place * arrow_rows), (width, arrow_rows)).T
    terms = lax.all_to_all(terms.reshape(group, arrow_rows, width), CHAIN, 0, 0)
    rest = (own - jnp.sum(terms, 0)).astype(jnp.bfloat16)
    rest = spread(rest, CHAIN).reshape(arrow_count, width)
    rest = spread(rest, COPY)
    arrow_solved = jnp.einsum("gar,ba->grb", rest, tip_inverse, preferred_element_type=jnp.float32)
    arrow_solved = arrow_solved.reshape(rhs_count, arrow_count)

    solved = jnp.stack(solved).reshape(deal, cores, lower, piece, width)
    solved = solved.transpose(1, 2, 0, 3, 4).reshape(copies, deal, piece, width)
    solved = lax.all_to_all(solved, COPY, 0, 0).transpose(1, 0, 2, 3)
    solved = lax.all_to_all(solved, DEAL, 0, 0)
    solved = solved.transpose(1, 3, 0, 2).reshape(1, rhs_count, local_rows)
    return (solved, arrow_solved)


def solution(mesh):
    fine = Mesh(mesh.devices.reshape(SIZES), AXES)
    steps, nodes = ("yl", "x", "c"), ("yh", "z")
    placed = (
        P(steps, None, nodes),
        P(),
        P(steps, nodes, None),
        P(steps, nodes, None),
        P(steps, nodes, None),
        P(steps, None, nodes),
        P(),
    )
    return jax.shard_map(
        per_device,
        mesh=fine,
        in_specs=placed,
        out_specs=(P(steps, None, nodes), P()),
        check_vma=False,
    )
```

time: 507 us -> 584 us (1.15)
  blocking collectives: 40.8 us -> 219 us
  waiting for transfers between devices: 272 us -> 185 us
  starting transfers between devices: 108 us -> 82.2 us
  local copies, waits for them, and re-layouts: 27.8 us -> 50.8 us
  matrix products: 36.9 us -> 29.7 us
    all_to_all x2 -> x15, blocking collectives: 40.8 us -> 219 us  [the longest x13 186 us: spread(): return lax.all_to_all(copies, axis, 0, 0)]
    all_gather x2, waiting for transfers between devices: 61.9 us -> 0.04 us  [the longest x1 0.02 us: per_device(): late = lax.all_gather(rows[EARLY:], COPY, axis=0)]
    all_to_all x18 -> x6, starting transfers between devices: 83 us -> 44.2 us  [spread(): return lax.all_to_all(copies, axis, 0, 0)]
    all_to_all x18 -> x6, waiting for transfers between devices: 204 us -> 172 us  [spread(): return lax.all_to_all(copies, axis, 0, 0)]
    slice x1 -> x5, local copies, waits for them, and re-layouts: 0.66 us -> 22.1 us  [the longest x3 21.1 us: of_step(): held.reshape(cores, lower, *held.shape[1:])[core, :, pair]]
    all_to_all x1 -> x3, starting transfers between devices: 25.1 us -> 37.9 us  [the longest x1 25.2 us: per_device(): solved = lax.all_to_all(solved, COPY, 0, 0).transpose(1, 0, 2, 3)]
    all_to_all x1 -> x3, waiting for transfers between devices: 5.62 us -> 13.3 us  [the longest x1 5.04 us: per_device(): solved = lax.all_to_all(solved, COPY, 0, 0).transpose(1, 0, 2, 3)]
    dot_general x18 -> x67, matrix products: 36.9 us -> 29.7 us  [the longest x16 9.3 us: per_device(): lax.dot_general(held[:, :node_count], history[step], CONTRACT, preferred_...]
  transfers between devices with their start and end apart: 21 -> 11, of which waited for: 20 -> 7; matrix products, arithmetic and copies ran while one was open for 10% -> 12% of each run, Pallas kernels for 0% -> 0%
where the time goes in v2:
time: 584 us; the launch traced here: 583 us
  blocking collectives  219 us (38%)
  waiting for transfers between devices  185 us (32%)
  starting transfers between devices  82.2 us (14%)
  local copies, waits for them, and re-layouts  50.8 us (9%)
  matrix products  29.7 us (5%)
  between operations  14.8 us (3%)
    all_to_all x13, blocking collectives, spread(): return lax.all_to_all(copies, axis, 0, 0)  186 us
    all_to_all x6, waiting for transfers between devices, spread(): return lax.all_to_all(copies, axis, 0, 0)  172 us
    all_to_all x6, starting transfers between devices, spread(): return lax.all_to_all(copies, axis, 0, 0)  44.2 us
    all_to_all x1, starting transfers between devices, per_device(): solved = lax.all_to_all(solved, COPY, 0, 0).transpose(1, 0, 2, 3)  25.2 us
    slice x3, local copies, waits for them, and re-layouts, of_step(): held.reshape(cores, lower, *held.shape[1:])[core, :, pair]  21.1 us
    all_to_all x1, blocking collectives, per_device(): rows = lax.all_to_all(rows.reshape(deal, piece, -1), DEAL, 0, 0)  18.4 us
    all_to_all x1, blocking collectives, per_device(): out_rows = lax.all_to_all(out_rows.reshape(deal, piece, -1), DEAL, 0, 0)  14.9 us
    unnamed x118, local copies, waits for them, and re-layouts  12.3 us
  transfers between devices with their start and end apart: 11, of which 7 were waited for; matrix products, arithmetic and copies ran while one was open for 12% of the time, Pallas kernels for 0%

profile of v2, /device:TPU:1, one launch (start us, length us, event | category | flops | bytes accessed | tf_op | source)
XLA Modules:
  0.0 582.6 jit_solution(15395944658860814355)
XLA Ops:
  7.4 1.0 copy.100
  8.4 1.4 copy.147
  10.0 2.4 fusion.17
  12.4 1.9 copy.99
  14.3 0.8 concatenate.19
  15.2 18.4 %all_to_all.120 = bf16[8,16,4480]{2,1,0:T(8,128)(2,1)S(1)} all-to-all(bf16[8,16,4480]{2,1,0:T(8,128)(2,1)S(1)} %pad_maximum_fusion.1), channel_id=1, replica_groups=mesh['yl'=2,'x'=4,'c'=2,'yh'=4,'z'=8] {'yl','x'}, dimensions={0} | all-to-all | bytes 2293760 | tf_op jit(solution)/shard_map/all_to_all | solution.py:61
  33.7 1.0 slice.415
  35.5 1.3 fusion.14
  36.9 1.7 copy.96
  38.6 1.8 concatenate.16
  40.5 14.9 %all_to_all.121 = bf16[8,16,4608]{2,1,0:T(8,128)(2,1)} all-to-all(bf16[8,16,4608]{2,1,0:T(8,128)(2,1)S(1)} %pad_maximum_fusion), channel_id=1, replica_groups=mesh['yl'=2,'x'=4,'c'=2,'yh'=4,'z'=8] {'yl','x'}, dimensions={0} | all-to-all | bytes 2359296 | tf_op jit(solution)/shard_map/all_to_all | solution.py:65
  55.4 2.4 broadcast_in_dim.42
  57.9 19.4 %all-to-all-start.2 = ((bf16[16,2,16,4480]{3,2,1,0:T(8,128)(2,1)}), bf16[16,2,16,4480]{3,2,1,0:T(8,128)(2,1)}, u32[]{:S(2)}, u32[]{:S(2)}) async-start(bf16[16,2,16,4480]{3,2,1,0:T(8,128)(2,1)} %broadcast_in_dim.42), calls=%async_computation.2 | async-start | bytes 9175040 | tf_op jit(solution)/shard_map/all_to_all | solution.py:21
  77.2 146.0 %all-to-all-done.2 = bf16[16,2,16,4480]{3,2,1,0:T(8,128)(2,1)} async-done(((bf16[16,2,16,4480]{3,2,1,0:T(8,128)(2,1)}), bf16[16,2,16,4480]{3,2,1,0:T(8,128)(2,1)}, u32[]{:S(2)}, u32[]{:S(2)}) %all-to-all-start.2) | async-done | bytes 4587552 | tf_op jit(solution)/shard_map/all_to_all | solution.py:21
  223.2 2.6 fusion.238
  226.4 18.8 %all_to_all.122 = bf16[32,24,128]{2,1,0:T(8,128)(2,1)S(1)} all-to-all(bf16[32,24,128]{2,1,0:T(8,128)(2,1)S(1)} %broadcast_in_dim.44), channel_id=1, replica_groups=mesh['yl'=2,'x'=4,'c'=2,'yh'=4,'z'=8] {'yl','x','yh'}, dimensions={0} | all-to-all | bytes 393216 | tf_op jit(solution)/shard_map/all_to_all | solution.py:21
  245.8 14.3 %all_to_all.123 = bf16[32,24,128]{2,1,0:T(8,128)(2,1)S(1)} all-to-all(bf16[32,24,128]{2,1,0:T(8,128)(2,1)S(1)} %broadcast_in_dim.45), channel_id=1, replica_groups=mesh['yl'=2,'x'=4,'c'=2,'yh'=4,'z'=8] {'yl','x','yh'}, dimensions={0} | all-to-all | bytes 393216 | tf_op jit(solution)/shard_map/all_to_all | solution.py:21
  260.8 13.2 %all_to_all.124 = bf16[32,24,128]{2,1,0:T(8,128)(2,1)S(1)} all-to-all(bf16[32,24,128]{2,1,0:T(8,128)(2,1)S(1)} %broadcast_in_dim.46), channel_id=1, replica_groups=mesh['yl'=2,'x'=4,'c'=2,'yh'=4,'z'=8] {'yl','x','yh'}, dimensions={0} | all-to-all | bytes 393216 | tf_op jit(solution)/shard_map/all_to_all | solution.py:21
  274.5 0.7 broadcast_in_dim.47
  275.2 4.6 all-to-all-start.6
  279.9 9.8 %fusion.237 = (bf16[1,8,1,16,4480]{4,3,2,1,0:T(8,128)(2,1)S(1)}, bf16[1,8,1,16,4480]{4,3,2,1,0:T(8,128)(2,1)S(1)}, bf16[1,8,1,16,4480]{4,3,2,1,0:T(8,128)(2,1)},...) fusion(bf16[2,8,6,16,4480]{4,3,2,1,0:T(8,128)(2,1)} %bitcast.393), kind=kLoop, calls=%fused_computation.294 | loop fusion | bytes 27525120 | tf_op jit(solution)/shard_map/slice | solution.py:69
  289.7 1.8 fusion.101
  291.5 1.1 fusion.24
  292.6 18.6 %all_to_all.125 = bf16[32,24,128]{2,1,0:T(8,128)(2,1)S(1)} all-to-all(bf16[32,24,128]{2,1,0:T(8,128)(2,1)S(1)} %broadcast_in_dim.48), channel_id=1, replica_groups=mesh['yl'=2,'x'=4,'c'=2,'yh'=4,'z'=8] {'yl','x','yh'}, dimensions={0} | all-to-all | bytes 393216 | tf_op jit(solution)/shard_map/all_to_all | solution.py:21
  311.9 13.1 %all_to_all.126 = bf16[32,24,128]{2,1,0:T(8,128)(2,1)S(1)} all-to-all(bf16[32,24,128]{2,1,0:T(8,128)(2,1)S(1)} %broadcast_in_dim.49), channel_id=1, replica_groups=mesh['yl'=2,'x'=4,'c'=2,'yh'=4,'z'=8] {'yl','x','yh'}, dimensions={0} | all-to-all | bytes 393216 | tf_op jit(solution)/shard_map/all_to_all | solution.py:21
  325.6 13.3 %all_to_all.127 = bf16[32,24,128]{2,1,0:T(8,128)(2,1)S(1)} all-to-all(bf16[32,24,128]{2,1,0:T(8,128)(2,1)S(1)} %broadcast_in_dim.50), channel_id=1, replica_groups=mesh['yl'=2,'x'=4,'c'=2,'yh'=4,'z'=8] {'yl','x','yh'}, dimensions={0} | all-to-all | bytes 393216 | tf_op jit(solution)/shard_map/all_to_all | solution.py:21
  339.5 13.1 %all_to_all.128 = bf16[32,24,128]{2,1,0:T(8,128)(2,1)S(1)} all-to-all(bf16[32,24,128]{2,1,0:T(8,128)(2,1)S(1)} %broadcast_in_dim.51), channel_id=1, replica_groups=mesh['yl'=2,'x'=4,'c'=2,'yh'=4,'z'=8] {'yl','x','yh'}, dimensions={0} | all-to-all | bytes 393216 | tf_op jit(solution)/shard_map/all_to_all | solution.py:21
  353.2 13.1 %all_to_all.129 = bf16[32,24,128]{2,1,0:T(8,128)(2,1)S(1)} all-to-all(bf16[32,24,128]{2,1,0:T(8,128)(2,1)S(1)} %broadcast_in_dim.52), channel_id=1, replica_groups=mesh['yl'=2,'x'=4,'c'=2,'yh'=4,'z'=8] {'yl','x','yh'}, dimensions={0} | all-to-all | bytes 393216 | tf_op jit(solution)/shard_map/all_to_all | solution.py:21
  367.0 13.1 %all_to_all.130 = bf16[32,24,128]{2,1,0:T(8,128)(2,1)S(1)} all-to-all(bf16[32,24,128]{2,1,0:T(8,128)(2,1)S(1)} %broadcast_in_dim.53), channel_id=1, replica_groups=mesh['yl'=2,'x'=4,'c'=2,'yh'=4,'z'=8] {'yl','x','yh'}, dimensions={0} | all-to-all | bytes 393216 | tf_op jit(solution)/shard_map/all_to_all | solution.py:21
  380.7 13.7 %all_to_all.131 = bf16[32,24,128]{2,1,0:T(8,128)(2,1)S(1)} all-to-all(bf16[32,24,128]{2,1,0:T(8,128)(2,1)S(1)} %broadcast_in_dim.54), channel_id=1, replica_groups=mesh['yl'=2,'x'=4,'c'=2,'yh'=4,'z'=8] {'yl','x','yh'}, dimensions={0} | all-to-all | bytes 393216 | tf_op jit(solution)/shard_map/all_to_all | solution.py:21
  395.1 14.1 %all_to_all.132 = bf16[32,24,128]{2,1,0:T(8,128)(2,1)S(1)} all-to-all(bf16[32,24,128]{2,1,0:T(8,128)(2,1)S(1)} %broadcast_in_dim.55), channel_id=1, replica_groups=mesh['yl'=2,'x'=4,'c'=2,'yh'=4,'z'=8] {'yl','x','yh'}, dimensions={0} | all-to-all | bytes 393216 | tf_op jit(solution)/shard_map/all_to_all | solution.py:21
  409.8 14.2 %all_to_all.133 = bf16[32,24,128]{2,1,0:T(8,128)(2,1)S(1)} all-to-all(bf16[32,24,128]{2,1,0:T(8,128)(2,1)S(1)} %broadcast_in_dim.56), channel_id=1, replica_groups=mesh['yl'=2,'x'=4,'c'=2,'yh'=4,'z'=8] {'yl','x','yh'}, dimensions={0} | all-to-all | bytes 393216 | tf_op jit(solution)/shard_map/all_to_all | solution.py:21
  424.6 13.0 %all_to_all.134 = bf16[32,24,128]{2,1,0:T(8,128)(2,1)S(1)} all-to-all(bf16[32,24,128]{2,1,0:T(8,128)(2,1)S(1)} %broadcast_in_dim.57), channel_id=1, replica_groups=mesh['yl'=2,'x'=4,'c'=2,'yh'=4,'z'=8] {'yl','x','yh'}, dimensions={0} | all-to-all | bytes 393216 | tf_op jit(solution)/shard_map/all_to_all | solution.py:21
  438.3 0.7 broadcast_in_dim.58
  439.1 3.9 all-to-all-start.17
  442.9 0.8 dynamic_slice.3
  443.8 8.8 %all-to-all-done.17 = bf16[32,24,128]{2,1,0:T(8,128)(2,1)S(1)} async-done(((bf16[32,24,128]{2,1,0:T(8,128)(2,1)}), bf16[32,24,128]{2,1,0:T(8,128)(2,1)S(1)}, u32[]{:S(2)}, u32[]{:S(2)}) %all-to-all-start.17) | async-done | bytes 196640 | tf_op jit(solution)/shard_map/all_to_all | solution.py:21
  453.2 0.7 broadcast_in_dim.59
  453.9 4.6 all-to-all-start.18
  458.5 8.7 %fusion.236 = (bf16[1,8,1,16,4608]{4,3,2,1,0:T(8,128)(2,1)S(1)}, bf16[1,8,1,16,4608]{4,3,2,1,0:T(8,128)(2,1)S(1)}, bf16[1,8,1,16,4608]{4,3,2,1,0:T(8,128)(2,1)S(...) fusion(bf16[2,8,8,16,4608]{4,3,2,1,0:T(8,128)(2,1)} %bitcast.392), kind=kLoop, calls=%fused_computation.293 | loop fusion | bytes 37748736 | tf_op jit(solution)/shard_map/slice | solution.py:69
  467.2 1.0 fusion.199
  468.3 1.1 convolution_add_fusion.14
  472.9 1.4 fusion.43
  479.8 0.8 reshape.322
  480.7 1.0 fusion.65
  481.7 9.3 %all-to-all-start.21 = ((f32[32,1,384]{2,1,0:T(1,128)}), f32[32,1,384]{2,1,0:T(1,128)S(1)}, u32[]{:S(2)}, u32[]{:S(2)}) async-start(f32[32,1,384]{2,1,0:T(1,128)} %reshape.322), calls=%async_computation.21 | async-start | bytes 98304 | tf_op jit(solution)/shard_map/all_to_all | solution.py:101
  491.0 1.9 fusion.67
  492.9 1.4 reshape.296
  494.9 1.3 reshape.318
  496.2 3.3 all-to-all-done.21
  499.4 25.2 %all-to-all-start.19 = ((bf16[16,2,1536]{2,1,0:T(2,128)(2,1)}), bf16[16,2,1536]{2,1,0:T(2,128)(2,1)S(1)}, u32[]{:S(2)}, u32[]{:S(2)}) async-start(bf16[16,2,1536]{2,1,0:T(2,128)(2,1)} %reshape.318), calls=%async_computation.19 | async-start | bytes 196608 | tf_op jit(solution)/shard_map/all_to_all | solution.py:110
  525.2 0.8 reduce.4
  526.2 0.8 reshape.324
  527.0 5.0 all-to-all-done.19
  532.0 4.9 all-to-all-start.22
  537.7 1.3 reshape.320
  539.0 6.7 %all-to-all-done.22 = bf16[32,2,192]{2,1,0:T(2,128)(2,1)S(1)} async-done(((bf16[32,2,192]{2,1,0:T(2,128)(2,1)}), bf16[32,2,192]{2,1,0:T(2,128)(2,1)S(1)}, u32[]{:S(2)}, u32[]{:S(2)}) %all-to-all-start.22) | async-done | bytes 24608 | tf_op jit(solution)/shard_map/all_to_all | solution.py:21
  545.6 3.4 all-to-all-start.20
  549.2 5.0 all-to-all-done.20
  554.2 0.8 broadcast_in_dim.62
  555.0 6.9 %all-to-all-start.23 = ((bf16[16,512,24]{1,2,0:T(8,128)(2,1)}), bf16[16,512,24]{1,2,0:T(8,128)(2,1)S(1)}, u32[]{:S(2)}, u32[]{:S(2)}) async-start(bf16[16,512,24]{1,2,0:T(8,128)(2,1)} %broadcast_in_dim.62), calls=%async_computation.23 | async-start | bytes 786432 | tf_op jit(solution)/shard_map/all_to_all | solution.py:21
  563.3 0.8 copy.123
  564.1 10.3 %all-to-all-done.23 = bf16[16,512,24]{1,2,0:T(8,128)(2,1)S(1)} async-done(((bf16[16,512,24]{1,2,0:T(8,128)(2,1)}), bf16[16,512,24]{1,2,0:T(8,128)(2,1)S(1)}, u32[]{:S(2)}, u32[]{:S(2)}) %all-to-all-start.23) | async-done | bytes 393248 | tf_op jit(solution)/shard_map/all_to_all | solution.py:21
  574.4 1.3 fusion.119
  (210 shorter events, 23.4 us)
Async XLA Ops:
  7.2 567.2 %copy-start = (bf16[512,512]{1,0:T(8,128)(2,1)S(1)}, bf16[512,512]{1,0:T(8,128)(2,1)}, u32[]{:S(2)}) copy-start(bf16[512,512]{1,0:T(8,128)(2,1)} %param.13) | copy-start | bytes 1572868
  7.2 2.7 copy-start.51
  7.2 272.7 %all-gather.7.cloned.1.call-start = ((), (), s32[]{:S(2)}) async-start(), calls=%async_computation.25 | async-start | bytes 14622720 | tf_op jit(solution)/shard_map/all_gather | solution.py:63
  33.7 1.0 copy-start.35
  33.7 1.6 copy-start.12
  34.7 423.8 %all-gather.5.cloned.1.call-start = ((), (), s32[]{:S(2)}) async-start(), calls=%async_computation.24 | async-start | bytes 20054016 | tf_op jit(solution)/shard_map/all_gather | solution.py:66
  57.9 165.3 %all-to-all-start.2 = ((bf16[16,2,16,4480]{3,2,1,0:T(8,128)(2,1)}), bf16[16,2,16,4480]{3,2,1,0:T(8,128)(2,1)}, u32[]{:S(2)}, u32[]{:S(2)}) async-start(bf16[16,2,16,4480]{3,2,1,0:T(8,128)(2,1)} %broadcast_in_dim.42), calls=%async_computation.2 | async-start | bytes 9175040 | tf_op jit(solution)/shard_map/all_to_all | solution.py:21
  275.2 14.4 %all-to-all-start.6 = ((bf16[32,24,128]{2,1,0:T(8,128)(2,1)}), bf16[32,24,128]{2,1,0:T(8,128)(2,1)}, u32[]{:S(2)}, u32[]{:S(2)}) async-start(bf16[32,24,128]{2,1,0:T(8,128)(2,1)} %broadcast_in_dim.47), calls=%async_computation.6 | async-start | bytes 393216 | tf_op jit(solution)/shard_map/all_to_all | solution.py:21
  289.7 21.6 %copy-start.11 = (bf16[1,8,1,16,4480]{4,3,2,1,0:T(8,128)(2,1)S(1)}, bf16[1,8,1,16,4480]{4,3,2,1,0:T(8,128)(2,1)}, u32[]{:S(2)}) copy-start(bf16[1,8,1,16,4480]{4,3,2,1,0:T(8,128)(2,1)} %get-tuple-element.36) | copy-start | bytes 3440644
  292.6 32.4 %copy-start.10 = (bf16[1,8,1,16,4480]{4,3,2,1,0:T(8,128)(2,1)S(1)}, bf16[1,8,1,16,4480]{4,3,2,1,0:T(8,128)(2,1)}, u32[]{:S(2)}) copy-start(bf16[1,8,1,16,4480]{4,3,2,1,0:T(8,128)(2,1)} %get-tuple-element.35) | copy-start | bytes 3440644
  311.3 14.1 %copy-start.13 = (bf16[32,24,128]{2,1,0:T(8,128)(2,1)}, bf16[32,24,128]{2,1,0:T(8,128)(2,1)S(1)}, u32[]{:S(2)}) copy-start(bf16[32,24,128]{2,1,0:T(8,128)(2,1)S(1)} %all_to_all.125) | copy-start | bytes 589828
  311.9 27.0 %copy-start.9 = (bf16[1,8,1,16,4480]{4,3,2,1,0:T(8,128)(2,1)S(1)}, bf16[1,8,1,16,4480]{4,3,2,1,0:T(8,128)(2,1)}, u32[]{:S(2)}) copy-start(bf16[1,8,1,16,4480]{4,3,2,1,0:T(8,128)(2,1)} %get-tuple-element.34) | copy-start | bytes 3440644
  325.0 14.3 %copy-start.15 = (bf16[32,24,128]{2,1,0:T(8,128)(2,1)}, bf16[32,24,128]{2,1,0:T(8,128)(2,1)S(1)}, u32[]{:S(2)}) copy-start(bf16[32,24,128]{2,1,0:T(8,128)(2,1)S(1)} %all_to_all.126) | copy-start | bytes 589828
  325.6 27.0 %copy-start.8 = (bf16[1,8,1,16,4480]{4,3,2,1,0:T(8,128)(2,1)S(1)}, bf16[1,8,1,16,4480]{4,3,2,1,0:T(8,128)(2,1)}, u32[]{:S(2)}) copy-start(bf16[1,8,1,16,4480]{4,3,2,1,0:T(8,128)(2,1)} %get-tuple-element.33) | copy-start | bytes 3440644
  338.9 14.1 %copy-start.17 = (bf16[32,24,128]{2,1,0:T(8,128)(2,1)}, bf16[32,24,128]{2,1,0:T(8,128)(2,1)S(1)}, u32[]{:S(2)}) copy-start(bf16[32,24,128]{2,1,0:T(8,128)(2,1)S(1)} %all_to_all.127) | copy-start | bytes 589828
  339.5 26.8 %copy-start.7 = (bf16[1,8,1,16,4480]{4,3,2,1,0:T(8,128)(2,1)S(1)}, bf16[1,8,1,16,4480]{4,3,2,1,0:T(8,128)(2,1)}, u32[]{:S(2)}) copy-start(bf16[1,8,1,16,4480]{4,3,2,1,0:T(8,128)(2,1)} %get-tuple-element.32) | copy-start | bytes 3440644
  352.6 14.1 %copy-start.19 = (bf16[32,24,128]{2,1,0:T(8,128)(2,1)}, bf16[32,24,128]{2,1,0:T(8,128)(2,1)S(1)}, u32[]{:S(2)}) copy-start(bf16[32,24,128]{2,1,0:T(8,128)(2,1)S(1)} %all_to_all.128) | copy-start | bytes 589828
  353.2 26.9 %copy-start.6 = (bf16[1,8,1,16,4480]{4,3,2,1,0:T(8,128)(2,1)S(1)}, bf16[1,8,1,16,4480]{4,3,2,1,0:T(8,128)(2,1)}, u32[]{:S(2)}) copy-start(bf16[1,8,1,16,4480]{4,3,2,1,0:T(8,128)(2,1)} %get-tuple-element.31) | copy-start | bytes 3440644
  366.3 14.2 %copy-start.21 = (bf16[32,24,128]{2,1,0:T(8,128)(2,1)}, bf16[32,24,128]{2,1,0:T(8,128)(2,1)S(1)}, u32[]{:S(2)}) copy-start(bf16[32,24,128]{2,1,0:T(8,128)(2,1)S(1)} %all_to_all.129) | copy-start | bytes 589828
  366.9 27.5 %copy-start.37 = (bf16[24,128]{1,0:T(8,128)(2,1)}, bf16[24,128]{1,0:T(8,128)(2,1)S(1)}, u32[]{:S(2)}) copy-start(bf16[24,128]{1,0:T(8,128)(2,1)S(1)} %fusion.29) | copy-start | bytes 18436
  366.9 27.5 %copy-start.5 = (bf16[1,8,1,16,4480]{4,3,2,1,0:T(8,128)(2,1)S(1)}, bf16[1,8,1,16,4480]{4,3,2,1,0:T(8,128)(2,1)}, u32[]{:S(2)}) copy-start(bf16[1,8,1,16,4480]{4,3,2,1,0:T(8,128)(2,1)} %get-tuple-element.30) | copy-start | bytes 3440644
  380.1 14.7 %copy-start.23 = (bf16[32,24,128]{2,1,0:T(8,128)(2,1)}, bf16[32,24,128]{2,1,0:T(8,128)(2,1)S(1)}, u32[]{:S(2)}) copy-start(bf16[32,24,128]{2,1,0:T(8,128)(2,1)S(1)} %all_to_all.130) | copy-start | bytes 589828
  380.7 28.5 %copy-start.39 = (bf16[24,128]{1,0:T(8,128)(2,1)}, bf16[24,128]{1,0:T(8,128)(2,1)S(1)}, u32[]{:S(2)}) copy-start(bf16[24,128]{1,0:T(8,128)(2,1)S(1)} %fusion.30) | copy-start | bytes 18436
  380.7 28.4 %copy-start.4 = (bf16[1,8,1,16,4480]{4,3,2,1,0:T(8,128)(2,1)S(1)}, bf16[1,8,1,16,4480]{4,3,2,1,0:T(8,128)(2,1)}, u32[]{:S(2)}) copy-start(bf16[1,8,1,16,4480]{4,3,2,1,0:T(8,128)(2,1)} %get-tuple-element.29) | copy-start | bytes 3440644
  394.4 15.1 %copy-start.25 = (bf16[32,24,128]{2,1,0:T(8,128)(2,1)}, bf16[32,24,128]{2,1,0:T(8,128)(2,1)S(1)}, u32[]{:S(2)}) copy-start(bf16[32,24,128]{2,1,0:T(8,128)(2,1)S(1)} %all_to_all.131) | copy-start | bytes 589828
  395.0 29.0 %copy-start.41 = (bf16[24,128]{1,0:T(8,128)(2,1)}, bf16[24,128]{1,0:T(8,128)(2,1)S(1)}, u32[]{:S(2)}) copy-start(bf16[24,128]{1,0:T(8,128)(2,1)S(1)} %fusion.31) | copy-start | bytes 18436
  395.1 29.0 %copy-start.3 = (bf16[1,8,1,16,4480]{4,3,2,1,0:T(8,128)(2,1)S(1)}, bf16[1,8,1,16,4480]{4,3,2,1,0:T(8,128)(2,1)}, u32[]{:S(2)}) copy-start(bf16[1,8,1,16,4480]{4,3,2,1,0:T(8,128)(2,1)} %get-tuple-element.28) | copy-start | bytes 3440644
  409.2 15.2 %copy-start.27 = (bf16[32,24,128]{2,1,0:T(8,128)(2,1)}, bf16[32,24,128]{2,1,0:T(8,128)(2,1)S(1)}, u32[]{:S(2)}) copy-start(bf16[32,24,128]{2,1,0:T(8,128)(2,1)S(1)} %all_to_all.132) | copy-start | bytes 589828
  409.8 27.9 %copy-start.43 = (bf16[24,128]{1,0:T(8,128)(2,1)}, bf16[24,128]{1,0:T(8,128)(2,1)S(1)}, u32[]{:S(2)}) copy-start(bf16[24,128]{1,0:T(8,128)(2,1)S(1)} %fusion.32) | copy-start | bytes 18436
  424.0 14.0 %copy-start.31 = (bf16[32,24,128]{2,1,0:T(8,128)(2,1)}, bf16[32,24,128]{2,1,0:T(8,128)(2,1)S(1)}, u32[]{:S(2)}) copy-start(bf16[32,24,128]{2,1,0:T(8,128)(2,1)S(1)} %all_to_all.133) | copy-start | bytes 589828
  424.6 14.5 %copy-start.45 = (bf16[24,128]{1,0:T(8,128)(2,1)}, bf16[24,128]{1,0:T(8,128)(2,1)S(1)}, u32[]{:S(2)}) copy-start(bf16[24,128]{1,0:T(8,128)(2,1)S(1)} %fusion.33) | copy-start | bytes 18436
  437.7 0.7 copy-start.33
  438.3 15.5 %copy-start.47 = (bf16[24,128]{1,0:T(8,128)(2,1)}, bf16[24,128]{1,0:T(8,128)(2,1)S(1)}, u32[]{:S(2)}) copy-start(bf16[24,128]{1,0:T(8,128)(2,1)S(1)} %fusion.34) | copy-start | bytes 18436
  439.1 13.5 %all-to-all-start.17 = ((bf16[32,24,128]{2,1,0:T(8,128)(2,1)}), bf16[32,24,128]{2,1,0:T(8,128)(2,1)S(1)}, u32[]{:S(2)}, u32[]{:S(2)}) async-start(bf16[32,24,128]{2,1,0:T(8,128)(2,1)} %broadcast_in_dim.58), calls=%async_computation.17 | async-start | bytes 393216 | tf_op jit(solution)/shard_map/all_to_all | solution.py:21
  452.6 5.9 %copy-start.29 = (bf16[32,24,128]{2,1,0:T(8,128)(2,1)}, bf16[32,24,128]{2,1,0:T(8,128)(2,1)S(1)}, u32[]{:S(2)}) copy-start(bf16[32,24,128]{2,1,0:T(8,128)(2,1)S(1)} %all-to-all-done.17) | copy-start | bytes 589828
  453.2 5.4 copy-start.49
  453.9 27.8 %all-to-all-start.18 = ((bf16[32,24,128]{2,1,0:T(8,128)(2,1)}), bf16[32,24,128]{2,1,0:T(8,128)(2,1)}, u32[]{:S(2)}, u32[]{:S(2)}) async-start(bf16[32,24,128]{2,1,0:T(8,128)(2,1)} %broadcast_in_dim.59), calls=%async_computation.18 | async-start | bytes 393216 | tf_op jit(solution)/shard_map/all_to_all | solution.py:21
  467.2 3.1 copy-start.38
  467.2 3.2 copy-start.40
  468.3 2.3 copy-start.42
  469.3 1.4 copy-start.44
  469.5 1.4 copy-start.46
  469.6 1.4 copy-start.48
  469.7 1.4 copy-start.2
  470.7 1.4 copy-start.1
  472.5 1.8 copy-start.14
  472.9 1.8 copy-start.16
  474.3 0.9 copy-start.18
  474.7 1.0 copy-start.20
  475.2 0.9 copy-start.22
  475.7 0.9 copy-start.24
  476.2 0.9 copy-start.26
  476.6 0.9 copy-start.28
  477.1 0.9 copy-start.32
  477.6 0.9 copy-start.34
  478.1 1.5 copy-start.50
  478.5 2.2 copy-start.30
  478.9 0.7 copy-start.36
  481.7 17.8 %all-to-all-start.21 = ((f32[32,1,384]{2,1,0:T(1,128)}), f32[32,1,384]{2,1,0:T(1,128)S(1)}, u32[]{:S(2)}, u32[]{:S(2)}) async-start(f32[32,1,384]{2,1,0:T(1,128)} %reshape.322), calls=%async_computation.21 | async-start | bytes 98304 | tf_op jit(solution)/shard_map/all_to_all | solution.py:101
  499.4 32.6 %all-to-all-start.19 = ((bf16[16,2,1536]{2,1,0:T(2,128)(2,1)}), bf16[16,2,1536]{2,1,0:T(2,128)(2,1)S(1)}, u32[]{:S(2)}, u32[]{:S(2)}) async-start(bf16[16,2,1536]{2,1,0:T(2,128)(2,1)} %reshape.318), calls=%async_computation.19 | async-start | bytes 196608 | tf_op jit(solution)/shard_map/all_to_all | solution.py:110
  532.0 13.6 %all-to-all-start.22 = ((bf16[32,2,192]{2,1,0:T(2,128)(2,1)}), bf16[32,2,192]{2,1,0:T(2,128)(2,1)S(1)}, u32[]{:S(2)}, u32[]{:S(2)}) async-start(bf16[32,2,192]{2,1,0:T(2,128)(2,1)} %reshape.324), calls=%async_computation.22 | async-start | bytes 65536 | tf_op jit(solution)/shard_map/all_to_all | solution.py:21
  545.6 8.6 %all-to-all-start.20 = ((bf16[8,2,3072]{2,1,0:T(2,128)(2,1)}), bf16[8,2,3072]{2,1,0:T(2,128)(2,1)S(1)}, u32[]{:S(2)}, u32[]{:S(2)}) async-start(bf16[8,2,3072]{2,1,0:T(2,128)(2,1)} %reshape.320), calls=%async_computation.20 | async-start | bytes 196608 | tf_op jit(solution)/shard_map/all_to_all | solution.py:111
  555.0 19.4 %all-to-all-start.23 = ((bf16[16,512,24]{1,2,0:T(8,128)(2,1)}), bf16[16,512,24]{1,2,0:T(8,128)(2,1)S(1)}, u32[]{:S(2)}, u32[]{:S(2)}) async-start(bf16[16,512,24]{1,2,0:T(8,128)(2,1)} %broadcast_in_dim.62), calls=%async_computation.23 | async-start | bytes 786432 | tf_op jit(solution)/shard_map/all_to_all | solution.py:21
Sparse Core Ops, SparseCore 0:
  34.8 183.8 all-gather.6
  220.8 112.3 all-gather.4

commit v3 on v1

--- a/solution.py
+++ b/solution.py
@@ -5,6 +5,10 @@
 
 TILE = 128
 CONTRACT = (((1,), (1,)), ((), ()))
+
+
+def product(left, right):
+    return lax.dot_general(left, right, CONTRACT, preferred_element_type=jnp.float32)
 
 
 def spread(value, axis):
@@ -37,22 +41,25 @@
     previous = jnp.zeros((width, node_count), jnp.bfloat16)
     history = []
     for step in range(steps):
-        linked = lax.dot_general(previous, links[step], CONTRACT, preferred_element_type=jnp.float32)
+        linked = product(previous, links[step])
         fresh = (source[step].astype(jnp.float32) - linked).astype(jnp.bfloat16)
         previous = spread(fresh, "space").transpose(1, 0, 2).reshape(width, node_count)
         history.append(previous)
-    whole = jnp.stack(history)
-    results = jnp.einsum("trm,tqm->trq", whole, outputs, preferred_element_type=jnp.float32)
-    solved = results[:, :, :local_rows].astype(jnp.bfloat16)
-    arrow_sum = jnp.sum(results[:, :, local_rows:], 0)
+    solved = [product(history[step], outputs[step, :local_rows]).astype(jnp.bfloat16) for step in range(steps)]
+    terms = [product(outputs[step, local_rows:], history[step]) for step in range(steps)]
 
-    own = lax.dynamic_slice(rhs_arrow, (section * width, block * arrow_rows), (width, arrow_rows))
-    rest = spread((own - arrow_sum).astype(jnp.bfloat16), "space")
-    rest = rest.transpose(1, 0, 2).reshape(width, arrow_count)
-    rest = spread(rest, "tm").reshape(rhs_count, arrow_count)
-    arrow_solved = lax.dot_general(rest, tip_inverse, CONTRACT, preferred_element_type=jnp.float32)
-    solved = lax.all_to_all(solved, "tm", 0, 0).reshape(1, rhs_count, local_rows)
-    return (solved, arrow_solved)
+    own = lax.dynamic_slice(rhs_arrow, (section * width, block * arrow_rows), (width, arrow_rows)).T
+    rest = spread((own - sum(terms)).astype(jnp.bfloat16), "space").reshape(arrow_count, width).T
+    parts = arrow_count // TILE
+    rest = rest.reshape(width, parts, TILE).transpose(1, 0, 2).reshape(parts * width, TILE)
+    sent = jnp.stack([jnp.concatenate([value, rest], 0) for value in solved])
+    arrived = lax.all_to_all(sent, "tm", 0, 0)
+    rest = arrived[:, width:].reshape(steps, parts, width, TILE)
+    arrow_solved = sum(
+        product(rest[:, part].reshape(rhs_count, TILE), tip_inverse[:, part * TILE : (part + 1) * TILE])
+        for part in range(parts)
+    )
+    return (arrived[:, :width].reshape(1, rhs_count, local_rows), arrow_solved)
 
 
 def solution(mesh):

time: 507 us -> 500 us (0.986)
  blocking collectives: 40.8 us -> 233 us
  waiting for transfers between devices: 272 us -> 126 us
  starting transfers between devices: 108 us -> 38.8 us
  matrix products: 36.9 us -> 70.7 us
  local copies, waits for them, and re-layouts: 27.8 us -> 8.26 us
    all_to_all x0 -> x10, blocking collectives: none -> 191 us  [the longest x9 160 us: spread(): return lax.all_to_all(copies, axis, 0, 0)]
    all_to_all x18 -> x8, waiting for transfers between devices: 204 us -> 66 us  [spread(): return lax.all_to_all(copies, axis, 0, 0)]
    all_to_all x18 -> x8, starting transfers between devices: 83 us -> 38.7 us  [spread(): return lax.all_to_all(copies, axis, 0, 0)]
    dot_general x18 -> x52, matrix products: 36.9 us -> 70.7 us  [product(): lax.dot_general(left, right, CONTRACT, preferred_element_type=jnp.float32)]
    all_to_all x1 -> x0, starting transfers between devices: 25.1 us -> none  [per_device(): lax.all_to_all(solved, 'tm', 0, 0).reshape(1, rhs_count, local_rows)]
    unnamed x27 -> x5, local copies, waits for them, and re-layouts: 12 us -> 1.01 us
    broadcast_in_dim x18 -> x17, local copies, waits for them, and re-layouts: 12.4 us -> 5.48 us  [spread(): copies = jnp.broadcast_to(value[None], (count, *value.shape))]
    all_to_all x1 -> x0, waiting for transfers between devices: 5.62 us -> none  [per_device(): lax.all_to_all(solved, 'tm', 0, 0).reshape(1, rhs_count, local_rows)]
  transfers between devices with their start and end apart: 21 -> 10, of which waited for: 20 -> 8; matrix products, arithmetic and copies ran while one was open for 10% -> 13% of each run, Pallas kernels for 0% -> 0%
where the time goes in v3:
time: 500 us; the launch traced here: 497 us
  blocking collectives  233 us (47%)
  waiting for transfers between devices  126 us (25%)
  matrix products  70.7 us (14%)
  starting transfers between devices  38.8 us (8%)
  between operations  14.5 us (3%)
  local copies, waits for them, and re-layouts  8.26 us (2%)
  other arithmetic  5.48 us (1%)
    all_to_all x9, blocking collectives, spread(): return lax.all_to_all(copies, axis, 0, 0)  160 us
    dot_general x52, matrix products, product(): lax.dot_general(left, right, CONTRACT, preferred_element_type=jnp.float32)  70.7 us
    all_to_all x8, waiting for transfers between devices, spread(): return lax.all_to_all(copies, axis, 0, 0)  66 us
    all_gather x1, waiting for transfers between devices, per_device(): links = lax.all_gather(masked, 'tm', axis=0, tiled=True)  60.4 us
    all_to_all x8, starting transfers between devices, spread(): return lax.all_to_all(copies, axis, 0, 0)  38.7 us
    all_to_all x1, blocking collectives, per_device(): arrived = lax.all_to_all(sent, 'tm', 0, 0)  31.1 us
    all_to_all x1, blocking collectives, per_device(): lax.all_to_all(arrow_factor.reshape(blocks, arrow_rows, local_rows), 'spa...  28 us
    all_to_all x1, blocking collectives, per_device(): lax.all_to_all(rhs_nodes.reshape(steps, width, local_rows), 'tm', 0, 0)  13.3 us
  transfers between devices with their start and end apart: 10, of which 8 were waited for; matrix products, arithmetic and copies ran while one was open for 13% of the time, Pallas kernels for 0%

profile of v3, /device:TPU:1, one launch (start us, length us, event | category | flops | bytes accessed | tf_op | source)
XLA Modules:
  0.0 496.9 jit_solution(16811307133307203670)
XLA Ops:
  7.9 2.3 broadcast_multiply_fusion
  10.3 28.0 %all_to_all.100 = bf16[32,16,128]{2,1,0:T(8,128)(2,1)S(1)} all-to-all(bf16[32,16,128]{2,1,0:T(8,128)(2,1)} %bitcast.617), channel_id=1, replica_groups=mesh['tm'=16,'space'=32] {'space'}, dimensions={0} | all-to-all | bytes 262144 | tf_op jit(solution)/shard_map/all_to_all | solution.py:37
  38.4 2.4 pad_maximum_fusion
  40.8 13.3 %all_to_all.101 = bf16[16,24,128]{2,1,0:T(8,128)(2,1)S(1)} all-to-all(bf16[16,24,128]{2,1,0:T(8,128)(2,1)} %bitcast.618), channel_id=1, replica_groups=mesh['tm'=16,'space'=32] {'tm'}, dimensions={0} | all-to-all | bytes 196608 | tf_op jit(solution)/shard_map/all_to_all | solution.py:36
  54.1 60.4 %all-gather.3.cloned.1.call-done = bf16[16,128,4096]{2,1,0:T(8,128)(2,1)} async-done(((bf16[1,128,4096]{2,1,0:T(8,128)(2,1)}), bf16[16,128,4096]{2,1,0:T(8,128)(2,1)}) %all-gather.3.cloned.1.call-update) | async-done | bytes 16777232 | tf_op jit(solution)/shard_map/all_gather | solution.py:35
  114.5 1.6 fusion
  116.2 23.6 %all_to_all.102 = bf16[32,24,128]{2,1,0:T(8,128)(2,1)S(1)} all-to-all(bf16[32,24,128]{2,1,0:T(8,128)(2,1)S(1)} %broadcast_in_dim.37), channel_id=1, replica_groups=mesh['tm'=16,'space'=32] {'space'}, dimensions={0} | all-to-all | bytes 393216 | tf_op jit(solution)/shard_map/all_to_all | solution.py:17
  139.8 1.6 fusion.1
  141.4 18.9 %all_to_all.103 = bf16[32,24,128]{2,1,0:T(8,128)(2,1)S(1)} all-to-all(bf16[32,24,128]{2,1,0:T(8,128)(2,1)S(1)} %broadcast_in_dim.38), channel_id=1, replica_groups=mesh['tm'=16,'space'=32] {'space'}, dimensions={0} | all-to-all | bytes 393216 | tf_op jit(solution)/shard_map/all_to_all | solution.py:17
  160.4 1.6 fusion.2
  162.0 18.4 %all_to_all.104 = bf16[32,24,128]{2,1,0:T(8,128)(2,1)S(1)} all-to-all(bf16[32,24,128]{2,1,0:T(8,128)(2,1)S(1)} %broadcast_in_dim.39), channel_id=1, replica_groups=mesh['tm'=16,'space'=32] {'space'}, dimensions={0} | all-to-all | bytes 393216 | tf_op jit(solution)/shard_map/all_to_all | solution.py:17
  180.4 1.6 fusion.3
  182.1 17.9 %all_to_all.105 = bf16[32,24,128]{2,1,0:T(8,128)(2,1)S(1)} all-to-all(bf16[32,24,128]{2,1,0:T(8,128)(2,1)S(1)} %broadcast_in_dim.40), channel_id=1, replica_groups=mesh['tm'=16,'space'=32] {'space'}, dimensions={0} | all-to-all | bytes 393216 | tf_op jit(solution)/shard_map/all_to_all | solution.py:17
  200.0 1.6 fusion.4
  201.6 18.0 %all_to_all.106 = bf16[32,24,128]{2,1,0:T(8,128)(2,1)S(1)} all-to-all(bf16[32,24,128]{2,1,0:T(8,128)(2,1)S(1)} %broadcast_in_dim.41), channel_id=1, replica_groups=mesh['tm'=16,'space'=32] {'space'}, dimensions={0} | all-to-all | bytes 393216 | tf_op jit(solution)/shard_map/all_to_all | solution.py:17
  219.6 1.6 fusion.5
  221.3 17.3 %all_to_all.107 = bf16[32,24,128]{2,1,0:T(8,128)(2,1)S(1)} all-to-all(bf16[32,24,128]{2,1,0:T(8,128)(2,1)S(1)} %broadcast_in_dim.42), channel_id=1, replica_groups=mesh['tm'=16,'space'=32] {'space'}, dimensions={0} | all-to-all | bytes 393216 | tf_op jit(solution)/shard_map/all_to_all | solution.py:17
  238.6 1.6 fusion.6
  240.3 16.0 %all_to_all.108 = bf16[32,24,128]{2,1,0:T(8,128)(2,1)S(1)} all-to-all(bf16[32,24,128]{2,1,0:T(8,128)(2,1)S(1)} %broadcast_in_dim.43), channel_id=1, replica_groups=mesh['tm'=16,'space'=32] {'space'}, dimensions={0} | all-to-all | bytes 393216 | tf_op jit(solution)/shard_map/all_to_all | solution.py:17
  256.2 1.6 fusion.7
  257.9 15.1 %all_to_all.109 = bf16[32,24,128]{2,1,0:T(8,128)(2,1)S(1)} all-to-all(bf16[32,24,128]{2,1,0:T(8,128)(2,1)S(1)} %broadcast_in_dim.44), channel_id=1, replica_groups=mesh['tm'=16,'space'=32] {'space'}, dimensions={0} | all-to-all | bytes 393216 | tf_op jit(solution)/shard_map/all_to_all | solution.py:17
  273.0 1.6 fusion.8
  274.7 15.1 %all_to_all.110 = bf16[32,24,128]{2,1,0:T(8,128)(2,1)S(1)} all-to-all(bf16[32,24,128]{2,1,0:T(8,128)(2,1)S(1)} %broadcast_in_dim.45), channel_id=1, replica_groups=mesh['tm'=16,'space'=32] {'space'}, dimensions={0} | all-to-all | bytes 393216 | tf_op jit(solution)/shard_map/all_to_all | solution.py:17
  289.7 1.6 fusion.9
  292.1 3.9 all-to-all-start.11
  296.8 10.8 %all-to-all-done.11 = bf16[32,24,128]{2,1,0:T(8,128)(2,1)S(1)} async-done(((bf16[32,24,128]{2,1,0:T(8,128)(2,1)}), bf16[32,24,128]{2,1,0:T(8,128)(2,1)S(1)}, u32[]{:S(2)}, u32[]{:S(2)}) %all-to-all-start.11) | async-done | bytes 196640 | tf_op jit(solution)/shard_map/all_to_all | solution.py:17
  307.6 1.6 fusion.10
  309.9 4.0 all-to-all-start.12
  315.1 1.6 convolution_convert_fusion.15
  316.7 1.6 convolution_convert_fusion.14
  318.3 1.6 convolution_convert_fusion.13
  319.9 1.7 convolution_convert_fusion.12
  321.6 1.6 convolution_convert_fusion.11
  323.2 1.6 convolution_convert_fusion.10
  324.9 1.6 convolution_convert_fusion.9
  326.5 1.6 convolution_convert_fusion.8
  328.1 1.6 convolution_convert_fusion.7
  329.7 1.1 convolution_add_fusion.17
  339.5 1.6 convolution_convert_fusion.6
  341.1 1.6 fusion.11
  343.4 11.5 %all-to-all-start.13 = ((bf16[32,24,128]{2,1,0:T(8,128)(2,1)}), bf16[32,24,128]{2,1,0:T(8,128)(2,1)S(1)}, u32[]{:S(2)}, u32[]{:S(2)}) async-start(bf16[32,24,128]{2,1,0:T(8,128)(2,1)} %broadcast_in_dim.48), calls=%async_computation.13 | async-start | bytes 393216 | tf_op jit(solution)/shard_map/all_to_all | solution.py:17
  356.0 1.6 convolution_convert_fusion.5
  357.6 9.0 %all-to-all-done.13 = bf16[32,24,128]{2,1,0:T(8,128)(2,1)S(1)} async-done(((bf16[32,24,128]{2,1,0:T(8,128)(2,1)}), bf16[32,24,128]{2,1,0:T(8,128)(2,1)S(1)}, u32[]{:S(2)}, u32[]{:S(2)}) %all-to-all-start.13) | async-done | bytes 196640 | tf_op jit(solution)/shard_map/all_to_all | solution.py:17
  366.6 1.6 fusion.12
  368.9 3.9 all-to-all-start.14
  373.9 1.6 convolution_convert_fusion.4
  375.5 9.1 %all-to-all-done.14 = bf16[32,24,128]{2,1,0:T(8,128)(2,1)S(1)} async-done(((bf16[32,24,128]{2,1,0:T(8,128)(2,1)}), bf16[32,24,128]{2,1,0:T(8,128)(2,1)S(1)}, u32[]{:S(2)}, u32[]{:S(2)}) %all-to-all-start.14) | async-done | bytes 196640 | tf_op jit(solution)/shard_map/all_to_all | solution.py:17
  384.5 1.6 fusion.13
  386.9 3.9 all-to-all-start.15
  391.8 1.6 convolution_convert_fusion.3
  393.5 9.0 %all-to-all-done.15 = bf16[32,24,128]{2,1,0:T(8,128)(2,1)S(1)} async-done(((bf16[32,24,128]{2,1,0:T(8,128)(2,1)}), bf16[32,24,128]{2,1,0:T(8,128)(2,1)S(1)}, u32[]{:S(2)}, u32[]{:S(2)}) %all-to-all-start.15) | async-done | bytes 196640 | tf_op jit(solution)/shard_map/all_to_all | solution.py:17
  402.5 1.6 fusion.14
  404.8 3.9 all-to-all-start.16
  409.8 1.6 convolution_convert_fusion.2
  411.4 9.1 %all-to-all-done.16 = bf16[32,24,128]{2,1,0:T(8,128)(2,1)S(1)} async-done(((bf16[32,24,128]{2,1,0:T(8,128)(2,1)}), bf16[32,24,128]{2,1,0:T(8,128)(2,1)S(1)}, u32[]{:S(2)}, u32[]{:S(2)}) %all-to-all-start.16) | async-done | bytes 196640 | tf_op jit(solution)/shard_map/all_to_all | solution.py:17
  420.5 1.6 fusion.15
  422.9 3.9 all-to-all-start.17
  427.8 1.6 convolution_convert_fusion.1
  429.4 9.2 %all-to-all-done.17 = bf16[32,24,128]{2,1,0:T(8,128)(2,1)S(1)} async-done(((bf16[32,24,128]{2,1,0:T(8,128)(2,1)}), bf16[32,24,128]{2,1,0:T(8,128)(2,1)S(1)}, u32[]{:S(2)}, u32[]{:S(2)}) %all-to-all-start.17) | async-done | bytes 196640 | tf_op jit(solution)/shard_map/all_to_all | solution.py:17
  440.5 3.9 all-to-all-start.18
  444.4 1.6 convolution_convert_fusion
  446.0 9.8 %all-to-all-done.18 = bf16[32,2,192]{2,1,0:T(2,128)(2,1)S(1)} async-done(((bf16[32,2,192]{2,1,0:T(2,128)(2,1)}), bf16[32,2,192]{2,1,0:T(2,128)(2,1)S(1)}, u32[]{:S(2)}, u32[]{:S(2)}) %all-to-all-start.18) | async-done | bytes 24608 | tf_op jit(solution)/shard_map/all_to_all | solution.py:17
  456.3 31.1 %all_to_all.111 = bf16[16,120,128]{2,1,0:T(8,128)(2,1)S(1)} all-to-all(bf16[16,120,128]{2,1,0:T(8,128)(2,1)S(1)} %constant_dynamic-update-slice_fusion), channel_id=1, replica_groups=mesh['tm'=16,'space'=32] {'tm'}, dimensions={0} | all-to-all | bytes 983040 | tf_op jit(solution)/shard_map/all_to_all | solution.py:56
  488.2 1.1 convolution_add_fusion
  (73 shorter events, 26.1 us)
Async XLA Ops:
  7.2 107.4 %all-gather.3.cloned.1.call-start = ((), (), s32[]{:S(2)}) async-start(), calls=%async_computation.20 | async-start | bytes 17825792 | tf_op jit(solution)/shard_map/all_gather | solution.py:35
  10.3 303.7 %all-gather.5.cloned.1.call-start = ((), (), s32[]{:S(2)}) async-start(), calls=%async_computation.21 | async-start | bytes 20054016 | tf_op jit(solution)/shard_map/all_gather | solution.py:39
  292.1 15.5 %all-to-all-start.11 = ((bf16[32,24,128]{2,1,0:T(8,128)(2,1)}), bf16[32,24,128]{2,1,0:T(8,128)(2,1)S(1)}, u32[]{:S(2)}, u32[]{:S(2)}) async-start(bf16[32,24,128]{2,1,0:T(8,128)(2,1)} %broadcast_in_dim.46), calls=%async_computation.11 | async-start | bytes 393216 | tf_op jit(solution)/shard_map/all_to_all | solution.py:17
  309.9 31.2 %all-to-all-start.12 = ((bf16[32,24,128]{2,1,0:T(8,128)(2,1)}), bf16[32,24,128]{2,1,0:T(8,128)(2,1)S(1)}, u32[]{:S(2)}, u32[]{:S(2)}) async-start(bf16[32,24,128]{2,1,0:T(8,128)(2,1)} %broadcast_in_dim.47), calls=%async_computation.12 | async-start | bytes 393216 | tf_op jit(solution)/shard_map/all_to_all | solution.py:17
  319.9 167.5 %copy-start = (bf16[512,512]{1,0:T(8,128)(2,1)S(1)}, bf16[512,512]{1,0:T(8,128)(2,1)}, u32[]{:S(2)}) copy-start(bf16[512,512]{1,0:T(8,128)(2,1)} %param.13) | copy-start | bytes 1572868
  343.4 23.1 %all-to-all-start.13 = ((bf16[32,24,128]{2,1,0:T(8,128)(2,1)}), bf16[32,24,128]{2,1,0:T(8,128)(2,1)S(1)}, u32[]{:S(2)}, u32[]{:S(2)}) async-start(bf16[32,24,128]{2,1,0:T(8,128)(2,1)} %broadcast_in_dim.48), calls=%async_computation.13 | async-start | bytes 393216 | tf_op jit(solution)/shard_map/all_to_all | solution.py:17
  368.9 15.6 %all-to-all-start.14 = ((bf16[32,24,128]{2,1,0:T(8,128)(2,1)}), bf16[32,24,128]{2,1,0:T(8,128)(2,1)S(1)}, u32[]{:S(2)}, u32[]{:S(2)}) async-start(bf16[32,24,128]{2,1,0:T(8,128)(2,1)} %broadcast_in_dim.49), calls=%async_computation.14 | async-start | bytes 393216 | tf_op jit(solution)/shard_map/all_to_all | solution.py:17
  386.9 15.6 %all-to-all-start.15 = ((bf16[32,24,128]{2,1,0:T(8,128)(2,1)}), bf16[32,24,128]{2,1,0:T(8,128)(2,1)S(1)}, u32[]{:S(2)}, u32[]{:S(2)}) async-start(bf16[32,24,128]{2,1,0:T(8,128)(2,1)} %broadcast_in_dim.50), calls=%async_computation.15 | async-start | bytes 393216 | tf_op jit(solution)/shard_map/all_to_all | solution.py:17
  404.8 15.7 %all-to-all-start.16 = ((bf16[32,24,128]{2,1,0:T(8,128)(2,1)}), bf16[32,24,128]{2,1,0:T(8,128)(2,1)S(1)}, u32[]{:S(2)}, u32[]{:S(2)}) async-start(bf16[32,24,128]{2,1,0:T(8,128)(2,1)} %broadcast_in_dim.51), calls=%async_computation.16 | async-start | bytes 393216 | tf_op jit(solution)/shard_map/all_to_all | solution.py:17
  422.9 15.7 %all-to-all-start.17 = ((bf16[32,24,128]{2,1,0:T(8,128)(2,1)}), bf16[32,24,128]{2,1,0:T(8,128)(2,1)S(1)}, u32[]{:S(2)}, u32[]{:S(2)}) async-start(bf16[32,24,128]{2,1,0:T(8,128)(2,1)} %broadcast_in_dim.52), calls=%async_computation.17 | async-start | bytes 393216 | tf_op jit(solution)/shard_map/all_to_all | solution.py:17
  440.5 15.2 %all-to-all-start.18 = ((bf16[32,2,192]{2,1,0:T(2,128)(2,1)}), bf16[32,2,192]{2,1,0:T(2,128)(2,1)S(1)}, u32[]{:S(2)}, u32[]{:S(2)}) async-start(bf16[32,2,192]{2,1,0:T(2,128)(2,1)} %reshape.174), calls=%async_computation.18 | async-start | bytes 65536 | tf_op jit(solution)/shard_map/all_to_all | solution.py:17
Sparse Core Ops, SparseCore 0:
  10.4 104.0 all-gather.2
  116.7 129.4 all-gather.4

commit v4 on v3

--- a/solution.py
+++ b/solution.py
@@ -33,20 +33,27 @@
         1, local_rows, node_count
     )
     links = lax.all_gather(masked, "tm", axis=0, tiled=True)
-    source = lax.all_to_all(rhs_nodes.reshape(steps, width, local_rows), "tm", 0, 0)
+    initial = jnp.zeros((rhs_count, node_count), jnp.bfloat16)
+    entering = jnp.where(section == 0, product(initial, masked[0]), 0.0)
+    forcing = rhs_nodes[0].astype(jnp.float32) - entering
+    source = lax.all_to_all(forcing.astype(jnp.bfloat16).reshape(steps, width, local_rows), "tm", 0, 0)
     arrows = lax.all_to_all(arrow_factor.reshape(blocks, arrow_rows, local_rows), "space", 0, 0)
     arrows = arrows.transpose(1, 0, 2).reshape(1, arrow_rows, node_count)
     outputs = lax.all_gather(jnp.concatenate([pivot_inverse, arrows], 1), "tm", axis=0, tiled=True)
 
-    previous = jnp.zeros((width, node_count), jnp.bfloat16)
     history = []
+    fresh = source[0]
     for step in range(steps):
-        linked = product(previous, links[step])
-        fresh = (source[step].astype(jnp.float32) - linked).astype(jnp.bfloat16)
+        if step > 0:
+            linked = product(previous, lax.optimization_barrier(links[step]))
+            fresh = (source[step].astype(jnp.float32) - linked).astype(jnp.bfloat16)
         previous = spread(fresh, "space").transpose(1, 0, 2).reshape(width, node_count)
         history.append(previous)
-    solved = [product(history[step], outputs[step, :local_rows]).astype(jnp.bfloat16) for step in range(steps)]
-    terms = [product(outputs[step, local_rows:], history[step]) for step in range(steps)]
+    solved, terms = [], []
+    for step in range(steps):
+        held = lax.optimization_barrier(outputs[step])
+        solved.append(product(history[step], held[:local_rows]).astype(jnp.bfloat16))
+        terms.append(product(held[local_rows:], history[step]))
 
     own = lax.dynamic_slice(rhs_arrow, (section * width, block * arrow_rows), (width, arrow_rows)).T
     rest = spread((own - sum(terms)).astype(jnp.bfloat16), "space").reshape(arrow_count, width).T

time: 500 us -> 513 us (1.026)
  blocking collectives: 233 us -> 73 us
  waiting for transfers between devices: 126 us -> 233 us
  starting transfers between devices: 38.8 us -> 89.3 us
  local copies, waits for them, and re-layouts: 8.26 us -> 36.1 us
  matrix products: 70.7 us -> 60.5 us
    all_to_all x10 -> x1, blocking collectives: 174 us -> 13.1 us  [per_device(): lax.all_to_all(forcing.astype(jnp.bfloat16).reshape(steps, width, local_r...]
    all_to_all x8 -> x17, waiting for transfers between devices: 66 us -> 173 us  [spread(): return lax.all_to_all(copies, axis, 0, 0)]
    all_to_all x8 -> x17, starting transfers between devices: 38.7 us -> 89.2 us  [spread(): return lax.all_to_all(copies, axis, 0, 0)]
    squeeze x0 -> x2, local copies, waits for them, and re-layouts: none -> 19.9 us  [the longest x1 10.3 us: per_device(): linked = product(previous, lax.optimization_barrier(links[step]))]
    dot_general x52, matrix products: 70.7 us -> 60.5 us  [product(): lax.dot_general(left, right, CONTRACT, preferred_element_type=jnp.float32)]
    broadcast_in_dim x17 -> x18, local copies, waits for them, and re-layouts: 5.48 us -> 11.6 us  [spread(): copies = jnp.broadcast_to(value[None], (count, *value.shape))]
  transfers between devices with their start and end apart: 10 -> 19, of which waited for: 8 -> 16; matrix products, arithmetic and copies ran while one was open for 13% -> 17% of each run, Pallas kernels for 0% -> 0%
where the time goes in v4:
time: 513 us; the launch traced here: 510 us
  waiting for transfers between devices  233 us (45%)
  starting transfers between devices  89.3 us (17%)
  blocking collectives  73 us (14%)
  matrix products  60.5 us (12%)
  local copies, waits for them, and re-layouts  36.1 us (7%)
  between operations  14.7 us (3%)
    all_to_all x17, waiting for transfers between devices, spread(): return lax.all_to_all(copies, axis, 0, 0)  173 us
    all_to_all x17, starting transfers between devices, spread(): return lax.all_to_all(copies, axis, 0, 0)  89.2 us
    dot_general x52, matrix products, product(): lax.dot_general(left, right, CONTRACT, preferred_element_type=jnp.float32)  60.5 us
    all_gather x1, waiting for transfers between devices, per_device(): links = lax.all_gather(masked, 'tm', axis=0, tiled=True)  59.3 us
    all_to_all x1, blocking collectives, per_device(): arrived = lax.all_to_all(sent, 'tm', 0, 0)  32.1 us
    all_to_all x1, blocking collectives, per_device(): lax.all_to_all(arrow_factor.reshape(blocks, arrow_rows, local_rows), 'spa...  27.9 us
    all_to_all x1, blocking collectives, per_device(): lax.all_to_all(forcing.astype(jnp.bfloat16).reshape(steps, width, local_r...  13.1 us
    broadcast_in_dim x18, local copies, waits for them, and re-layouts, spread(): copies = jnp.broadcast_to(value[None], (count, *value.shape))  11.6 us
  transfers between devices with their start and end apart: 19, of which 16 were waited for; matrix products, arithmetic and copies ran while one was open for 17% of the time, Pallas kernels for 0%

profile of v4, /device:TPU:1, one launch (start us, length us, event | category | flops | bytes accessed | tf_op | source)
XLA Modules:
  0.0 510.4 jit_solution(2888120260583361793)
XLA Ops:
  7.9 2.3 broadcast_multiply_fusion
  10.3 27.9 %all_to_all.100 = bf16[32,16,128]{2,1,0:T(8,128)(2,1)S(1)} all-to-all(bf16[32,16,128]{2,1,0:T(8,128)(2,1)S(1)} %bitcast.553), channel_id=1, replica_groups=mesh['tm'=16,'space'=32] {'space'}, dimensions={0} | all-to-all | bytes 262144 | tf_op jit(solution)/shard_map/all_to_all | solution.py:40
  39.5 1.2 copy-done.3
  41.7 13.1 %all_to_all.101 = bf16[16,24,128]{2,1,0:T(8,128)(2,1)S(1)} all-to-all(bf16[16,24,128]{2,1,0:T(8,128)(2,1)S(1)} %bitcast.555), channel_id=1, replica_groups=mesh['tm'=16,'space'=32] {'tm'}, dimensions={0} | all-to-all | bytes 196608 | tf_op jit(solution)/shard_map/all_to_all | solution.py:39
  55.5 3.9 all-to-all-start.1
  59.4 59.3 %all-gather.5.cloned.1.call-done = bf16[16,128,4096]{2,1,0:T(8,128)(2,1)} async-done(((bf16[1,128,4096]{2,1,0:T(8,128)(2,1)}), bf16[16,128,4096]{2,1,0:T(8,128)(2,1)}) %all-gather.5.cloned.1.call-update) | async-done | bytes 16777232 | tf_op jit(solution)/shard_map/all_gather | solution.py:35
  118.7 10.3 %slice_bitcast_fusion.16 = (bf16[128,4096]{1,0:T(8,128)(2,1)S(1)}, bf16[128,4096]{1,0:T(8,128)(2,1)S(1)}, bf16[128,4096]{1,0:T(8,128)(2,1)S(1)}, bf16[128,4096]{...) fusion(bf16[16,128,4096]{2,1,0:T(8,128)(2,1)} %all-gather.5.clo, ...), kind=kLoop, calls=%fused_computation.103 | loop fusion | bytes 31457280 | tf_op jit(solution)/shard_map/squeeze | solution.py:48
  129.0 1.6 fusion.11
  131.4 11.4 %all-to-all-start.3 = ((bf16[32,24,128]{2,1,0:T(8,128)(2,1)}), bf16[32,24,128]{2,1,0:T(8,128)(2,1)S(1)}, u32[]{:S(2)}, u32[]{:S(2)}) async-start(bf16[32,24,128]{2,1,0:T(8,128)(2,1)} %broadcast_in_dim.46), calls=%async_computation.3 | async-start | bytes 393216 | tf_op jit(solution)/shard_map/all_to_all | solution.py:17
  142.7 14.4 %all-to-all-done.3 = bf16[32,24,128]{2,1,0:T(8,128)(2,1)S(1)} async-done(((bf16[32,24,128]{2,1,0:T(8,128)(2,1)}), bf16[32,24,128]{2,1,0:T(8,128)(2,1)S(1)}, u32[]{:S(2)}, u32[]{:S(2)}) %all-to-all-start.3) | async-done | bytes 196640 | tf_op jit(solution)/shard_map/all_to_all | solution.py:17
  157.1 1.7 fusion.12
  159.6 4.6 all-to-all-start.4
  164.2 13.7 %all-to-all-done.4 = bf16[32,24,128]{2,1,0:T(8,128)(2,1)} async-done(((bf16[32,24,128]{2,1,0:T(8,128)(2,1)}), bf16[32,24,128]{2,1,0:T(8,128)(2,1)}, u32[]{:S(2)}, u32[]{:S(2)}) %all-to-all-start.4) | async-done | bytes 196640 | tf_op jit(solution)/shard_map/all_to_all | solution.py:17
  177.9 1.6 fusion.13
  180.3 4.9 all-to-all-start.5
  185.2 13.0 %all-to-all-done.5 = bf16[32,24,128]{2,1,0:T(8,128)(2,1)} async-done(((bf16[32,24,128]{2,1,0:T(8,128)(2,1)}), bf16[32,24,128]{2,1,0:T(8,128)(2,1)}, u32[]{:S(2)}, u32[]{:S(2)}) %all-to-all-start.5) | async-done | bytes 196640 | tf_op jit(solution)/shard_map/all_to_all | solution.py:17
  198.2 1.6 fusion.14
  200.6 5.2 %all-to-all-start.6 = ((bf16[32,24,128]{2,1,0:T(8,128)(2,1)}), bf16[32,24,128]{2,1,0:T(8,128)(2,1)}, u32[]{:S(2)}, u32[]{:S(2)}) async-start(bf16[32,24,128]{2,1,0:T(8,128)(2,1)} %broadcast_in_dim.49), calls=%async_computation.6 | async-start | bytes 393216 | tf_op jit(solution)/shard_map/all_to_all | solution.py:17
  205.8 13.0 %all-to-all-done.6 = bf16[32,24,128]{2,1,0:T(8,128)(2,1)} async-done(((bf16[32,24,128]{2,1,0:T(8,128)(2,1)}), bf16[32,24,128]{2,1,0:T(8,128)(2,1)}, u32[]{:S(2)}, u32[]{:S(2)}) %all-to-all-start.6) | async-done | bytes 196640 | tf_op jit(solution)/shard_map/all_to_all | solution.py:17
  218.8 1.6 fusion.15
  221.2 4.6 all-to-all-start.7
  225.7 12.9 %all-to-all-done.7 = bf16[32,24,128]{2,1,0:T(8,128)(2,1)} async-done(((bf16[32,24,128]{2,1,0:T(8,128)(2,1)}), bf16[32,24,128]{2,1,0:T(8,128)(2,1)}, u32[]{:S(2)}, u32[]{:S(2)}) %all-to-all-start.7) | async-done | bytes 196640 | tf_op jit(solution)/shard_map/all_to_all | solution.py:17
  238.7 1.6 fusion.16
  241.0 4.6 all-to-all-start.8
  245.6 11.7 %all-to-all-done.8 = bf16[32,24,128]{2,1,0:T(8,128)(2,1)} async-done(((bf16[32,24,128]{2,1,0:T(8,128)(2,1)}), bf16[32,24,128]{2,1,0:T(8,128)(2,1)}, u32[]{:S(2)}, u32[]{:S(2)}) %all-to-all-start.8) | async-done | bytes 196640 | tf_op jit(solution)/shard_map/all_to_all | solution.py:17
  257.2 1.6 fusion.17
  259.6 4.6 all-to-all-start.9
  264.2 11.7 %all-to-all-done.9 = bf16[32,24,128]{2,1,0:T(8,128)(2,1)} async-done(((bf16[32,24,128]{2,1,0:T(8,128)(2,1)}), bf16[32,24,128]{2,1,0:T(8,128)(2,1)}, u32[]{:S(2)}, u32[]{:S(2)}) %all-to-all-start.9) | async-done | bytes 196640 | tf_op jit(solution)/shard_map/all_to_all | solution.py:17
  275.9 1.6 fusion.18
  278.3 4.6 all-to-all-start.10
  282.8 11.7 %all-to-all-done.10 = bf16[32,24,128]{2,1,0:T(8,128)(2,1)} async-done(((bf16[32,24,128]{2,1,0:T(8,128)(2,1)}), bf16[32,24,128]{2,1,0:T(8,128)(2,1)}, u32[]{:S(2)}, u32[]{:S(2)}) %all-to-all-start.10) | async-done | bytes 196640 | tf_op jit(solution)/shard_map/all_to_all | solution.py:17
  294.6 1.6 fusion.19
  296.9 4.6 all-to-all-start.11
  301.5 11.7 %all-to-all-done.11 = bf16[32,24,128]{2,1,0:T(8,128)(2,1)} async-done(((bf16[32,24,128]{2,1,0:T(8,128)(2,1)}), bf16[32,24,128]{2,1,0:T(8,128)(2,1)}, u32[]{:S(2)}, u32[]{:S(2)}) %all-to-all-start.11) | async-done | bytes 196640 | tf_op jit(solution)/shard_map/all_to_all | solution.py:17
  313.2 1.6 fusion.20
  315.6 4.6 all-to-all-start.12
  321.6 10.2 %all-to-all-done.12 = bf16[32,24,128]{2,1,0:T(8,128)(2,1)} async-done(((bf16[32,24,128]{2,1,0:T(8,128)(2,1)}), bf16[32,24,128]{2,1,0:T(8,128)(2,1)}, u32[]{:S(2)}, u32[]{:S(2)}) %all-to-all-start.12) | async-done | bytes 196640 | tf_op jit(solution)/shard_map/all_to_all | solution.py:17
  331.9 1.6 fusion.21
  334.2 4.8 all-to-all-start.13
  339.0 9.5 %slice_bitcast_fusion = (bf16[144,4096]{1,0:T(8,128)(2,1)}, bf16[144,4096]{1,0:T(8,128)(2,1)}, bf16[144,4096]{1,0:T(8,128)(2,1)}, bf16[144,4096]{1,0:T(8,128)(2,...) fusion(bf16[16,144,4096]{2,1,0:T(8,128)(2,1)} %all-gather.3.clo, ...), kind=kLoop, calls=%fused_computation.5 | loop fusion | bytes 37748736 | tf_op jit(solution)/shard_map/squeeze | solution.py:54
  349.7 1.3 convolution_convert_fusion.5
  351.0 1.3 convolution_convert_fusion.6
  352.4 1.9 convolution_convert_fusion.7
  354.3 1.9 convolution_convert_fusion.8
  357.4 1.3 convolution_convert_fusion.13
  359.8 1.3 convolution_convert_fusion.12
  362.3 1.3 convolution_convert_fusion.11
  364.7 1.3 convolution_convert_fusion.10
  372.7 1.3 convolution_convert_fusion.9
  374.0 1.6 fusion.22
  376.4 11.4 %all-to-all-start.14 = ((bf16[32,24,128]{2,1,0:T(8,128)(2,1)}), bf16[32,24,128]{2,1,0:T(8,128)(2,1)S(1)}, u32[]{:S(2)}, u32[]{:S(2)}) async-start(bf16[32,24,128]{2,1,0:T(8,128)(2,1)} %broadcast_in_dim.57), calls=%async_computation.14 | async-start | bytes 393216 | tf_op jit(solution)/shard_map/all_to_all | solution.py:17
  389.0 1.7 convolution_convert_fusion.4
  390.7 8.9 %all-to-all-done.14 = bf16[32,24,128]{2,1,0:T(8,128)(2,1)S(1)} async-done(((bf16[32,24,128]{2,1,0:T(8,128)(2,1)}), bf16[32,24,128]{2,1,0:T(8,128)(2,1)S(1)}, u32[]{:S(2)}, u32[]{:S(2)}) %all-to-all-start.14) | async-done | bytes 196640 | tf_op jit(solution)/shard_map/all_to_all | solution.py:17
  401.3 3.9 all-to-all-start.15
  406.3 1.6 convolution_convert_fusion.3
  407.9 9.0 %all-to-all-done.15 = bf16[32,24,128]{2,1,0:T(8,128)(2,1)S(1)} async-done(((bf16[32,24,128]{2,1,0:T(8,128)(2,1)}), bf16[32,24,128]{2,1,0:T(8,128)(2,1)S(1)}, u32[]{:S(2)}, u32[]{:S(2)}) %all-to-all-start.15) | async-done | bytes 196640 | tf_op jit(solution)/shard_map/all_to_all | solution.py:17
  418.7 3.9 all-to-all-start.16
  423.7 1.6 convolution_convert_fusion.2
  425.3 9.3 %all-to-all-done.16 = bf16[32,24,128]{2,1,0:T(8,128)(2,1)S(1)} async-done(((bf16[32,24,128]{2,1,0:T(8,128)(2,1)}), bf16[32,24,128]{2,1,0:T(8,128)(2,1)S(1)}, u32[]{:S(2)}, u32[]{:S(2)}) %all-to-all-start.16) | async-done | bytes 196640 | tf_op jit(solution)/shard_map/all_to_all | solution.py:17
  436.4 3.9 all-to-all-start.17
  440.8 11.2 %all-to-all-done.17 = bf16[32,24,128]{2,1,0:T(8,128)(2,1)S(1)} async-done(((bf16[32,24,128]{2,1,0:T(8,128)(2,1)}), bf16[32,24,128]{2,1,0:T(8,128)(2,1)S(1)}, u32[]{:S(2)}, u32[]{:S(2)}) %all-to-all-start.17) | async-done | bytes 196640 | tf_op jit(solution)/shard_map/all_to_all | solution.py:17
  453.0 4.0 all-to-all-start.18
  457.4 10.9 %all-to-all-done.18 = bf16[32,2,192]{2,1,0:T(2,128)(2,1)S(1)} async-done(((bf16[32,2,192]{2,1,0:T(2,128)(2,1)}), bf16[32,2,192]{2,1,0:T(2,128)(2,1)S(1)}, u32[]{:S(2)}, u32[]{:S(2)}) %all-to-all-start.18) | async-done | bytes 24608 | tf_op jit(solution)/shard_map/all_to_all | solution.py:17
  468.8 32.1 %all_to_all.102 = bf16[16,120,128]{2,1,0:T(8,128)(2,1)S(1)} all-to-all(bf16[16,120,128]{2,1,0:T(8,128)(2,1)S(1)} %constant_dynamic-update-slice_fusion), channel_id=1, replica_groups=mesh['tm'=16,'space'=32] {'tm'}, dimensions={0} | all-to-all | bytes 983040 | tf_op jit(solution)/shard_map/all_to_all | solution.py:63
  (109 shorter events, 40.0 us)
Async XLA Ops:
  7.2 111.5 %all-gather.5.cloned.1.call-start = ((), (), s32[]{:S(2)}) async-start(), calls=%async_computation.21 | async-start | bytes 17825792 | tf_op jit(solution)/shard_map/all_gather | solution.py:35
  7.9 2.4 copy-start.6
  10.2 28.1 %copy-start.2 = (bf16[1,128,4096]{2,1,0:T(8,128)(2,1)S(1)}, bf16[1,128,4096]{2,1,0:T(8,128)(2,1)}, u32[]{:S(2)}) copy-start(bf16[1,128,4096]{2,1,0:T(8,128)(2,1)} %param.11) | copy-start | bytes 3145732
  10.3 328.7 %all-gather.3.cloned.1.call-start = ((), (), s32[]{:S(2)}) async-start(), calls=%async_computation.20 | async-start | bytes 20054016 | tf_op jit(solution)/shard_map/all_gather | solution.py:42
  39.5 1.2 copy-start.3
  39.5 1.2 copy-start.12
  54.8 74.2 %copy-start.5 = (bf16[16,24,128]{2,1,0:T(8,128)(2,1)}, bf16[16,24,128]{2,1,0:T(8,128)(2,1)S(1)}, u32[]{:S(2)}) copy-start(bf16[16,24,128]{2,1,0:T(8,128)(2,1)S(1)} %all_to_all.101) | copy-start | bytes 294916
  55.5 73.5 %all-to-all-start.1 = ((bf16[32,24,128]{2,1,0:T(8,128)(2,1)}), bf16[32,24,128]{2,1,0:T(8,128)(2,1)S(1)}, u32[]{:S(2)}, u32[]{:S(2)}) async-start(bf16[32,24,128]{2,1,0:T(8,128)(2,1)} %broadcast_in_dim.45), calls=%async_computation.1 | async-start | bytes 393216 | tf_op jit(solution)/shard_map/all_to_all | solution.py:17
  131.4 25.8 %all-to-all-start.3 = ((bf16[32,24,128]{2,1,0:T(8,128)(2,1)}), bf16[32,24,128]{2,1,0:T(8,128)(2,1)S(1)}, u32[]{:S(2)}, u32[]{:S(2)}) async-start(bf16[32,24,128]{2,1,0:T(8,128)(2,1)} %broadcast_in_dim.46), calls=%async_computation.3 | async-start | bytes 393216 | tf_op jit(solution)/shard_map/all_to_all | solution.py:17
  159.6 18.3 %all-to-all-start.4 = ((bf16[32,24,128]{2,1,0:T(8,128)(2,1)}), bf16[32,24,128]{2,1,0:T(8,128)(2,1)}, u32[]{:S(2)}, u32[]{:S(2)}) async-start(bf16[32,24,128]{2,1,0:T(8,128)(2,1)} %broadcast_in_dim.47), calls=%async_computation.4 | async-start | bytes 393216 | tf_op jit(solution)/shard_map/all_to_all | solution.py:17
  180.3 17.9 %all-to-all-start.5 = ((bf16[32,24,128]{2,1,0:T(8,128)(2,1)}), bf16[32,24,128]{2,1,0:T(8,128)(2,1)}, u32[]{:S(2)}, u32[]{:S(2)}) async-start(bf16[32,24,128]{2,1,0:T(8,128)(2,1)} %broadcast_in_dim.48), calls=%async_computation.5 | async-start | bytes 393216 | tf_op jit(solution)/shard_map/all_to_all | solution.py:17
  200.6 18.2 %all-to-all-start.6 = ((bf16[32,24,128]{2,1,0:T(8,128)(2,1)}), bf16[32,24,128]{2,1,0:T(8,128)(2,1)}, u32[]{:S(2)}, u32[]{:S(2)}) async-start(bf16[32,24,128]{2,1,0:T(8,128)(2,1)} %broadcast_in_dim.49), calls=%async_computation.6 | async-start | bytes 393216 | tf_op jit(solution)/shard_map/all_to_all | solution.py:17
  221.2 17.5 %all-to-all-start.7 = ((bf16[32,24,128]{2,1,0:T(8,128)(2,1)}), bf16[32,24,128]{2,1,0:T(8,128)(2,1)}, u32[]{:S(2)}, u32[]{:S(2)}) async-start(bf16[32,24,128]{2,1,0:T(8,128)(2,1)} %broadcast_in_dim.50), calls=%async_computation.7 | async-start | bytes 393216 | tf_op jit(solution)/shard_map/all_to_all | solution.py:17
  241.0 16.2 %all-to-all-start.8 = ((bf16[32,24,128]{2,1,0:T(8,128)(2,1)}), bf16[32,24,128]{2,1,0:T(8,128)(2,1)}, u32[]{:S(2)}, u32[]{:S(2)}) async-start(bf16[32,24,128]{2,1,0:T(8,128)(2,1)} %broadcast_in_dim.51), calls=%async_computation.8 | async-start | bytes 393216 | tf_op jit(solution)/shard_map/all_to_all | solution.py:17
  259.6 16.3 %all-to-all-start.9 = ((bf16[32,24,128]{2,1,0:T(8,128)(2,1)}), bf16[32,24,128]{2,1,0:T(8,128)(2,1)}, u32[]{:S(2)}, u32[]{:S(2)}) async-start(bf16[32,24,128]{2,1,0:T(8,128)(2,1)} %broadcast_in_dim.52), calls=%async_computation.9 | async-start | bytes 393216 | tf_op jit(solution)/shard_map/all_to_all | solution.py:17
  278.3 16.3 %all-to-all-start.10 = ((bf16[32,24,128]{2,1,0:T(8,128)(2,1)}), bf16[32,24,128]{2,1,0:T(8,128)(2,1)}, u32[]{:S(2)}, u32[]{:S(2)}) async-start(bf16[32,24,128]{2,1,0:T(8,128)(2,1)} %broadcast_in_dim.53), calls=%async_computation.10 | async-start | bytes 393216 | tf_op jit(solution)/shard_map/all_to_all | solution.py:17
  296.9 16.3 %all-to-all-start.11 = ((bf16[32,24,128]{2,1,0:T(8,128)(2,1)}), bf16[32,24,128]{2,1,0:T(8,128)(2,1)}, u32[]{:S(2)}, u32[]{:S(2)}) async-start(bf16[32,24,128]{2,1,0:T(8,128)(2,1)} %broadcast_in_dim.54), calls=%async_computation.11 | async-start | bytes 393216 | tf_op jit(solution)/shard_map/all_to_all | solution.py:17
  315.6 16.3 %all-to-all-start.12 = ((bf16[32,24,128]{2,1,0:T(8,128)(2,1)}), bf16[32,24,128]{2,1,0:T(8,128)(2,1)}, u32[]{:S(2)}, u32[]{:S(2)}) async-start(bf16[32,24,128]{2,1,0:T(8,128)(2,1)} %broadcast_in_dim.55), calls=%async_computation.12 | async-start | bytes 393216 | tf_op jit(solution)/shard_map/all_to_all | solution.py:17
  334.2 39.8 %all-to-all-start.13 = ((bf16[32,24,128]{2,1,0:T(8,128)(2,1)}), bf16[32,24,128]{2,1,0:T(8,128)(2,1)}, u32[]{:S(2)}, u32[]{:S(2)}) async-start(bf16[32,24,128]{2,1,0:T(8,128)(2,1)} %broadcast_in_dim.56), calls=%async_computation.13 | async-start | bytes 393216 | tf_op jit(solution)/shard_map/all_to_all | solution.py:17
  376.4 23.2 %all-to-all-start.14 = ((bf16[32,24,128]{2,1,0:T(8,128)(2,1)}), bf16[32,24,128]{2,1,0:T(8,128)(2,1)S(1)}, u32[]{:S(2)}, u32[]{:S(2)}) async-start(bf16[32,24,128]{2,1,0:T(8,128)(2,1)} %broadcast_in_dim.57), calls=%async_computation.14 | async-start | bytes 393216 | tf_op jit(solution)/shard_map/all_to_all | solution.py:17
  401.3 15.6 %all-to-all-start.15 = ((bf16[32,24,128]{2,1,0:T(8,128)(2,1)}), bf16[32,24,128]{2,1,0:T(8,128)(2,1)S(1)}, u32[]{:S(2)}, u32[]{:S(2)}) async-start(bf16[32,24,128]{2,1,0:T(8,128)(2,1)} %broadcast_in_dim.58), calls=%async_computation.15 | async-start | bytes 393216 | tf_op jit(solution)/shard_map/all_to_all | solution.py:17
  418.7 15.8 %all-to-all-start.16 = ((bf16[32,24,128]{2,1,0:T(8,128)(2,1)}), bf16[32,24,128]{2,1,0:T(8,128)(2,1)S(1)}, u32[]{:S(2)}, u32[]{:S(2)}) async-start(bf16[32,24,128]{2,1,0:T(8,128)(2,1)} %broadcast_in_dim.59), calls=%async_computation.16 | async-start | bytes 393216 | tf_op jit(solution)/shard_map/all_to_all | solution.py:17
  425.3 15.0 %copy-start.1 = (bf16[144,4096]{1,0:T(8,128)(2,1)S(1)}, bf16[144,4096]{1,0:T(8,128)(2,1)}, u32[]{:S(2)}) copy-start(bf16[144,4096]{1,0:T(8,128)(2,1)} %get-tuple-element.3) | copy-start | bytes 3538948
  435.6 16.4 %copy-start = (bf16[144,4096]{1,0:T(8,128)(2,1)S(1)}, bf16[144,4096]{1,0:T(8,128)(2,1)}, u32[]{:S(2)}) copy-start(bf16[144,4096]{1,0:T(8,128)(2,1)} %get-tuple-element.2) | copy-start | bytes 3538948
  435.6 16.3 %copy-start.7 = (f32[24,16]{0,1:T(8,128)S(1)}, f32[24,16]{0,1:T(8,128)}, u32[]{:S(2)}) copy-start(f32[24,16]{0,1:T(8,128)} %copy.78) | copy-start | bytes 4612
  436.4 15.6 %all-to-all-start.17 = ((bf16[32,24,128]{2,1,0:T(8,128)(2,1)}), bf16[32,24,128]{2,1,0:T(8,128)(2,1)S(1)}, u32[]{:S(2)}, u32[]{:S(2)}) async-start(bf16[32,24,128]{2,1,0:T(8,128)(2,1)} %broadcast_in_dim.60), calls=%async_computation.17 | async-start | bytes 393216 | tf_op jit(solution)/shard_map/all_to_all | solution.py:17
  440.8 27.7 %copy-start.10 = (bf16[24,128]{1,0:T(8,128)(2,1)S(1)}, bf16[24,128]{1,0:T(8,128)(2,1)}, u32[]{:S(2)}) copy-start(bf16[24,128]{1,0:T(8,128)(2,1)} %convolution_convert_fusion.15) | copy-start | bytes 18436
  452.2 16.4 %copy-start.11 = (bf16[24,128]{1,0:T(8,128)(2,1)S(1)}, bf16[24,128]{1,0:T(8,128)(2,1)}, u32[]{:S(2)}) copy-start(bf16[24,128]{1,0:T(8,128)(2,1)} %convolution_convert_fusion.14) | copy-start | bytes 18436
  452.2 16.5 %copy-start.9 = (bf16[24,128]{1,0:T(8,128)(2,1)S(1)}, bf16[24,128]{1,0:T(8,128)(2,1)}, u32[]{:S(2)}) copy-start(bf16[24,128]{1,0:T(8,128)(2,1)} %convolution_convert_fusion.8) | copy-start | bytes 18436
  453.0 15.7 %copy-start.8 = (bf16[24,128]{1,0:T(8,128)(2,1)S(1)}, bf16[24,128]{1,0:T(8,128)(2,1)}, u32[]{:S(2)}) copy-start(bf16[24,128]{1,0:T(8,128)(2,1)} %convolution_convert_fusion.7) | copy-start | bytes 18436
  453.0 15.2 %all-to-all-start.18 = ((bf16[32,2,192]{2,1,0:T(2,128)(2,1)}), bf16[32,2,192]{2,1,0:T(2,128)(2,1)S(1)}, u32[]{:S(2)}, u32[]{:S(2)}) async-start(bf16[32,2,192]{2,1,0:T(2,128)(2,1)} %reshape.178), calls=%async_computation.18 | async-start | bytes 65536 | tf_op jit(solution)/shard_map/all_to_all | solution.py:17
  468.8 32.1 %copy-start.4 = (bf16[512,512]{1,0:T(8,128)(2,1)S(1)}, bf16[512,512]{1,0:T(8,128)(2,1)}, u32[]{:S(2)}) copy-start(bf16[512,512]{1,0:T(8,128)(2,1)} %param.13) | copy-start | bytes 1572868
Sparse Core Ops, SparseCore 0:
  10.4 108.2 all-gather.4
  120.8 127.8 all-gather.2

commit v5 on v2

v5 whole, which is shorter than its diff:
```python
import jax
import jax.numpy as jnp
import numpy as np
from jax import lax
from jax.sharding import Mesh
from jax.sharding import PartitionSpec as P

TILE = 128
CONTRACT = (((1,), (1,)), ((), ()))
AXES = ("yl", "x", "c", "yh", "z")
SIZES = (2, 4, 2, 4, 8)
DEAL = ("yl", "x")
COPY = ("c", "z")
CHAIN = ("yl", "x", "yh")
CHUNKS = (2, 3, 3)
OUT_AFTER = 5


def spread(value, axis):
    count = lax.axis_size(axis)
    copies = jnp.broadcast_to(value[None], (count, *value.shape))
    return lax.all_to_all(copies, axis, 0, 0)


def chain_order(deal, lower, piece):
    old = jnp.arange(lower * deal * piece).reshape(lower, deal, piece)
    new = old.transpose(1, 0, 2).reshape(deal, lower * piece)
    return (old.reshape(lower, deal * piece, 1, 1) == new).astype(jnp.bfloat16)


def product(left, right):
    return lax.dot_general(left, right, CONTRACT, preferred_element_type=jnp.float32)


def per_device(rhs_nodes, rhs_arrow, coupling, pattern, pivot_inverse, arrow_factor, tip_inverse):
    _, local_rows, node_count = coupling.shape
    rhs_count = rhs_nodes.shape[1]
    arrow_count = arrow_factor.shape[1]
    deal, copies, group = (lax.axis_size(axes) for axes in (DEAL, COPY, CHAIN))
    cores, lower = lax.axis_size("c"), lax.axis_size("z")
    steps = deal * cores
    piece = local_rows // deal
    width = rhs_count // copies
    arrow_rows = arrow_count // group
    mine = lax.axis_index(COPY)

    weights = pattern.astype(jnp.bfloat16)[0, :, None, :, None]
    masked = (coupling.reshape(local_rows // TILE, TILE, node_count // TILE, TILE) * weights).reshape(
        local_rows, node_count
    )
    upper = lax.axis_size("yh")
    order = chain_order(deal, lower, piece)

    def reorder(rows):
        moved = jnp.einsum(
            "ryzl,zlum->ruym",
            rows.reshape(local_rows, upper, lower, TILE),
            order,
            preferred_element_type=jnp.float32,
        )
        return moved.astype(jnp.bfloat16).reshape(local_rows, node_count)

    rows = jnp.concatenate([reorder(masked), rhs_nodes[0].T], 1)
    rows = lax.all_to_all(rows.reshape(deal, piece, -1), DEAL, 0, 0)
    first, second, third = jnp.split(rows, np.cumsum(CHUNKS)[:-1])
    links = [lax.all_gather(first, COPY, axis=0)]
    out_rows = lax.all_to_all(reorder(pivot_inverse[0]).reshape(deal, piece, -1), DEAL, 0, 0)
    second, out_rows = lax.optimization_barrier((second, out_rows))
    links.append(lax.all_gather(second, COPY, axis=0))
    arrows = lax.all_to_all(arrow_factor.reshape(group, arrow_rows, TILE), CHAIN, 0, 0)
    third, arrows = lax.optimization_barrier((third, arrows))
    links.append(lax.all_gather(third, COPY, axis=0))

    def of_step(held, pair, core):
        return held.reshape(cores, lower, *held.shape[1:])[core, :, pair].reshape(local_rows, -1)

    def link_rows(step):
        pair, core = step // cores, step % cores
        for chunk, pairs in enumerate(CHUNKS):
            if pair < pairs:
                return of_step(links[chunk], pair, core)
            pair -= pairs

    select = (jnp.arange(rhs_count)[None] == mine * width + jnp.arange(width)[:, None]).astype(jnp.bfloat16)
    previous = jnp.zeros((width, node_count), jnp.bfloat16)
    history = []
    for step in range(steps):
        held = link_rows(step)
        source = product(select, held[:, node_count:])
        linked = product(previous, held[:, :node_count])
        fresh = (source - linked).astype(jnp.bfloat16)
        if step == OUT_AFTER:
            fresh, out_rows, arrows = lax.optimization_barrier((fresh, out_rows, arrows))
            out_rows = lax.all_gather(out_rows, COPY, axis=0)
            arrows = lax.all_gather(arrows.reshape(deal, upper, arrow_rows, TILE), COPY, axis=0)
        previous = spread(fresh, CHAIN).transpose(1, 0, 2).reshape(width, node_count)
        history.append(previous)
    arrows = arrows.reshape(cores, lower, deal, upper, arrow_rows, TILE)
    arrows = jnp.einsum("czpyal,zlum->pcauym", arrows, order, preferred_element_type=jnp.float32)
    arrows = arrows.astype(jnp.bfloat16).reshape(steps, arrow_rows, node_count)
    solved = [
        product(history[step], of_step(out_rows, step // cores, step % cores)).astype(jnp.bfloat16)
        for step in range(steps)
    ]
    terms = [product(arrows[step], history[step]) for step in range(steps)]

    place = lax.axis_index(CHAIN)
    own = lax.dynamic_slice(rhs_arrow, (mine * width, place * arrow_rows), (width, arrow_rows)).T
    rest = spread((own - sum(terms)).astype(jnp.bfloat16), CHAIN).reshape(arrow_count, width).T
    parts = arrow_count // TILE
    rest = rest.reshape(width, parts, TILE).transpose(1, 0, 2).reshape(1, parts * width, TILE)

    solved = jnp.stack(solved).reshape(deal, cores, width, lower, piece)
    solved = solved.transpose(1, 3, 2, 0, 4).reshape(copies, width, deal * piece)
    sent = jnp.concatenate([solved, jnp.broadcast_to(rest, (copies, parts * width, TILE))], 1)
    arrived = lax.all_to_all(sent, COPY, 0, 0)
    rest = arrived[:, width:].reshape(copies, parts, width, TILE)
    arrow_solved = sum(
        product(rest[:, part].reshape(rhs_count, TILE), tip_inverse[:, part * TILE : (part + 1) * TILE])
        for part in range(parts)
    )
    solved = arrived[:, :width].reshape(rhs_count, deal, piece).transpose(1, 0, 2)
    solved = lax.all_to_all(solved, DEAL, 0, 0)
    solved = solved.transpose(1, 0, 2).reshape(1, rhs_count, local_rows)
    return (solved, arrow_solved)


def solution(mesh):
    fine = Mesh(mesh.devices.reshape(SIZES), AXES)
    steps, nodes = ("yl", "x", "c"), ("yh", "z")
    placed = (
        P(steps, None, nodes),
        P(),
        P(steps, nodes, None),
        P(steps, nodes, None),
        P(steps, nodes, None),
        P(steps, None, nodes),
        P(),
    )
    return jax.shard_map(
        per_device,
        mesh=fine,
        in_specs=placed,
        out_specs=(P(steps, None, nodes), P()),
        check_vma=False,
    )
```

time: 584 us -> 438 us (0.75)
  waiting for transfers between devices: 185 us -> 40.7 us
  starting transfers between devices: 82.2 us -> 24.7 us
  blocking collectives: 219 us -> 268 us
  matrix products: 29.7 us -> 45 us
  local copies, waits for them, and re-layouts: 50.8 us -> 41.8 us
    all_to_all x6 -> x4, waiting for transfers between devices: 172 us -> 18 us  [spread(): return lax.all_to_all(copies, axis, 0, 0)]
    all_to_all x1 -> x2, blocking collectives: 14.9 us -> 63.7 us  [the longest x1 39.1 us: per_device(): arrived = lax.all_to_all(sent, COPY, 0, 0)]
    all_to_all x2 -> x1, starting transfers between devices: 34.5 us -> 3.56 us  [per_device(): lax.all_to_all(reorder(pivot_inverse[0]).reshape(deal, piece, -1), DEAL,...]
    all_to_all x6 -> x4, starting transfers between devices: 44.2 us -> 17.6 us  [spread(): return lax.all_to_all(copies, axis, 0, 0)]
    dot_general x67 -> x71, matrix products: 29.7 us -> 45 us  [the longest x68 37.5 us: product(): lax.dot_general(left, right, CONTRACT, preferred_element_type=jnp.float32)]
    all_gather x1 -> x4, waiting for transfers between devices: 0.02 us -> 10.6 us  [the longest x1 10.6 us: per_device(): links = [lax.all_gather(first, COPY, axis=0)]]
    unnamed x118 -> x89, local copies, waits for them, and re-layouts: 12.3 us -> 4.84 us
    slice x3 -> x4, local copies, waits for them, and re-layouts: 21.1 us -> 19.2 us  [of_step(): held.reshape(cores, lower, *held.shape[1:])[core, :, pair]]
  transfers between devices with their start and end apart: 11 -> 11, of which waited for: 7 -> 6; matrix products, arithmetic and copies ran while one was open for 12% -> 14% of each run, Pallas kernels for 0% -> 0%
where the time goes in v5:
time: 438 us; the launch traced here: 435 us
  blocking collectives  268 us (61%)
  matrix products  45 us (10%)
  local copies, waits for them, and re-layouts  41.8 us (10%)
  waiting for transfers between devices  40.7 us (9%)
  starting transfers between devices  24.7 us (6%)
  between operations  14.8 us (3%)
    all_to_all x13, blocking collectives, spread(): return lax.all_to_all(copies, axis, 0, 0)  186 us
    all_to_all x1, blocking collectives, per_device(): arrived = lax.all_to_all(sent, COPY, 0, 0)  39.1 us
    dot_general x68, matrix products, product(): lax.dot_general(left, right, CONTRACT, preferred_element_type=jnp.float32)  37.5 us
    all_to_all x1, blocking collectives, per_device(): lax.all_to_all(arrow_factor.reshape(group, arrow_rows, TILE), CHAIN, 0, 0)  24.6 us
    slice x4, local copies, waits for them, and re-layouts, of_step(): held.reshape(cores, lower, *held.shape[1:])[core, :, pair]  19.2 us
    all_to_all x1, blocking collectives, per_device(): rows = lax.all_to_all(rows.reshape(deal, piece, -1), DEAL, 0, 0)  18.6 us
    all_to_all x4, waiting for transfers between devices, spread(): return lax.all_to_all(copies, axis, 0, 0)  18 us
    all_to_all x4, starting transfers between devices, spread(): return lax.all_to_all(copies, axis, 0, 0)  17.6 us
  transfers between devices with their start and end apart: 11, of which 6 were waited for; matrix products, arithmetic and copies ran while one was open for 14% of the time, Pallas kernels for 0%

profile of v5, /device:TPU:1, one launch (start us, length us, event | category | flops | bytes accessed | tf_op | source)
XLA Modules:
  0.0 434.9 jit_solution(17527400809319768398)
XLA Ops:
  7.2 1.0 copy.117
  8.4 1.5 copy.173
  10.0 1.6 fusion.21
  11.6 1.0 copy.116
  12.6 0.8 concatenate.11
  13.5 18.6 %all_to_all.110 = bf16[8,16,4480]{2,1,0:T(8,128)(2,1)S(1)} all-to-all(bf16[8,16,4480]{2,1,0:T(8,128)(2,1)S(1)} %pad_maximum_fusion), channel_id=1, replica_groups=mesh['yl'=2,'x'=4,'c'=2,'yh'=4,'z'=8] {'yl','x'}, dimensions={0} | all-to-all | bytes 2293760 | tf_op jit(solution)/shard_map/all_to_all | solution.py:64
  33.1 1.6 fusion.24
  34.7 1.0 copy.121
  35.7 1.6 reshape_reshape.22
  37.3 3.6 all-to-all-start.2
  40.9 1.0 fusion.251
  41.9 8.3 %all-to-all-done.2 = bf16[8,16,4096]{2,1,0:T(8,128)(2,1)S(1)} async-done(((bf16[8,16,4096]{2,1,0:T(8,128)(2,1)}), bf16[8,16,4096]{2,1,0:T(8,128)(2,1)S(1)}, u32[]{:S(2)}, u32[]{:S(2)}) %all-to-all-start.2) | async-done | bytes 1048608 | tf_op jit(solution)/shard_map/all_to_all | solution.py:67
  50.3 24.6 %all_to_all.111 = bf16[32,16,128]{2,1,0:T(8,128)(2,1)} all-to-all(bf16[32,16,128]{2,1,0:T(8,128)(2,1)S(1)} %bitcast.609), channel_id=1, replica_groups=mesh['yl'=2,'x'=4,'c'=2,'yh'=4,'z'=8] {'yl','x','yh'}, dimensions={0} | all-to-all | bytes 262144 | tf_op jit(solution)/shard_map/all_to_all | solution.py:70
  75.0 10.6 %all-gather.12.cloned.1.call-done = bf16[32,16,4480]{2,1,0:T(8,128)(2,1)} async-done(((bf16[2,16,4480]{2,1,0:T(8,128)(2,1)}), bf16[32,16,4480]{2,1,0:T(8,128)(2,1)}) %all-gather.12.cloned.1.call-update) | async-done | bytes 4587536 | tf_op jit(solution)/shard_map/all_gather | solution.py:66
  85.5 2.6 fusion.250
  88.8 18.9 %all_to_all.112 = bf16[32,24,128]{2,1,0:T(8,128)(2,1)S(1)} all-to-all(bf16[32,24,128]{2,1,0:T(8,128)(2,1)S(1)} %broadcast_in_dim.41), channel_id=1, replica_groups=mesh['yl'=2,'x'=4,'c'=2,'yh'=4,'z'=8] {'yl','x','yh'}, dimensions={0} | all-to-all | bytes 393216 | tf_op jit(solution)/shard_map/all_to_all | solution.py:22
  108.3 14.3 %all_to_all.113 = bf16[32,24,128]{2,1,0:T(8,128)(2,1)S(1)} all-to-all(bf16[32,24,128]{2,1,0:T(8,128)(2,1)S(1)} %broadcast_in_dim.42), channel_id=1, replica_groups=mesh['yl'=2,'x'=4,'c'=2,'yh'=4,'z'=8] {'yl','x','yh'}, dimensions={0} | all-to-all | bytes 393216 | tf_op jit(solution)/shard_map/all_to_all | solution.py:22
  123.2 13.2 %all_to_all.114 = bf16[32,24,128]{2,1,0:T(8,128)(2,1)S(1)} all-to-all(bf16[32,24,128]{2,1,0:T(8,128)(2,1)S(1)} %broadcast_in_dim.43), channel_id=1, replica_groups=mesh['yl'=2,'x'=4,'c'=2,'yh'=4,'z'=8] {'yl','x','yh'}, dimensions={0} | all-to-all | bytes 393216 | tf_op jit(solution)/shard_map/all_to_all | solution.py:22
  137.9 4.6 %all-to-all-start.5 = ((bf16[32,24,128]{2,1,0:T(8,128)(2,1)}), bf16[32,24,128]{2,1,0:T(8,128)(2,1)}, u32[]{:S(2)}, u32[]{:S(2)}) async-start(bf16[32,24,128]{2,1,0:T(8,128)(2,1)} %broadcast_in_dim.44), calls=%async_computation.5 | async-start | bytes 393216 | tf_op jit(solution)/shard_map/all_to_all | solution.py:22
  142.5 5.0 %fusion.249 = (bf16[1,8,1,16,4480]{4,3,2,1,0:T(8,128)(2,1)S(1)}, bf16[1,8,1,16,4480]{4,3,2,1,0:T(8,128)(2,1)S(1)}, bf16[1,8,1,16,4480]{4,3,2,1,0:T(8,128)(2,1)S(...) fusion(bf16[2,8,3,16,4480]{4,3,2,1,0:T(8,128)(2,1)} %bitcast.545), kind=kLoop, calls=%fused_computation.317 | loop fusion | bytes 13762560 | tf_op jit(solution)/shard_map/slice | solution.py:75
  147.5 4.5 %all-to-all-done.5 = bf16[32,24,128]{2,1,0:T(8,128)(2,1)} async-done(((bf16[32,24,128]{2,1,0:T(8,128)(2,1)}), bf16[32,24,128]{2,1,0:T(8,128)(2,1)}, u32[]{:S(2)}, u32[]{:S(2)}) %all-to-all-start.5) | async-done | bytes 196640 | tf_op jit(solution)/shard_map/all_to_all | solution.py:22
  152.1 1.9 fusion.99
  154.0 1.1 fusion.29
  155.1 13.9 %all_to_all.115 = bf16[32,24,128]{2,1,0:T(8,128)(2,1)S(1)} all-to-all(bf16[32,24,128]{2,1,0:T(8,128)(2,1)S(1)} %broadcast_in_dim.45), channel_id=1, replica_groups=mesh['yl'=2,'x'=4,'c'=2,'yh'=4,'z'=8] {'yl','x','yh'}, dimensions={0} | all-to-all | bytes 393216 | tf_op jit(solution)/shard_map/all_to_all | solution.py:22
  170.3 12.9 %all_to_all.116 = bf16[32,24,128]{2,1,0:T(8,128)(2,1)S(1)} all-to-all(bf16[32,24,128]{2,1,0:T(8,128)(2,1)S(1)} %broadcast_in_dim.46), channel_id=1, replica_groups=mesh['yl'=2,'x'=4,'c'=2,'yh'=4,'z'=8] {'yl','x','yh'}, dimensions={0} | all-to-all | bytes 393216 | tf_op jit(solution)/shard_map/all_to_all | solution.py:22
  183.2 1.7 fusion.95
  184.9 1.1 fusion.33
  186.0 13.0 %all_to_all.117 = bf16[32,24,128]{2,1,0:T(8,128)(2,1)S(1)} all-to-all(bf16[32,24,128]{2,1,0:T(8,128)(2,1)S(1)} %broadcast_in_dim.47), channel_id=1, replica_groups=mesh['yl'=2,'x'=4,'c'=2,'yh'=4,'z'=8] {'yl','x','yh'}, dimensions={0} | all-to-all | bytes 393216 | tf_op jit(solution)/shard_map/all_to_all | solution.py:22
  199.7 12.9 %all_to_all.118 = bf16[32,24,128]{2,1,0:T(8,128)(2,1)S(1)} all-to-all(bf16[32,24,128]{2,1,0:T(8,128)(2,1)S(1)} %broadcast_in_dim.48), channel_id=1, replica_groups=mesh['yl'=2,'x'=4,'c'=2,'yh'=4,'z'=8] {'yl','x','yh'}, dimensions={0} | all-to-all | bytes 393216 | tf_op jit(solution)/shard_map/all_to_all | solution.py:22
  213.2 12.9 %all_to_all.119 = bf16[32,24,128]{2,1,0:T(8,128)(2,1)S(1)} all-to-all(bf16[32,24,128]{2,1,0:T(8,128)(2,1)S(1)} %broadcast_in_dim.49), channel_id=1, replica_groups=mesh['yl'=2,'x'=4,'c'=2,'yh'=4,'z'=8] {'yl','x','yh'}, dimensions={0} | all-to-all | bytes 393216 | tf_op jit(solution)/shard_map/all_to_all | solution.py:22
  227.5 4.6 %all-to-all-start.12 = ((bf16[32,24,128]{2,1,0:T(8,128)(2,1)}), bf16[32,24,128]{2,1,0:T(8,128)(2,1)}, u32[]{:S(2)}, u32[]{:S(2)}) async-start(bf16[32,24,128]{2,1,0:T(8,128)(2,1)} %broadcast_in_dim.50), calls=%async_computation.12 | async-start | bytes 393216 | tf_op jit(solution)/shard_map/all_to_all | solution.py:22
  232.1 5.0 %fusion.248 = (bf16[1,8,1,16,4480]{4,3,2,1,0:T(8,128)(2,1)S(1)}, bf16[1,8,1,16,4480]{4,3,2,1,0:T(8,128)(2,1)S(1)}, bf16[1,8,1,16,4480]{4,3,2,1,0:T(8,128)(2,1)S(...) fusion(bf16[2,8,3,16,4480]{4,3,2,1,0:T(8,128)(2,1)} %bitcast.544), kind=kLoop, calls=%fused_computation.316 | loop fusion | bytes 13762560 | tf_op jit(solution)/shard_map/slice | solution.py:75
  237.1 4.6 %all-to-all-done.12 = bf16[32,24,128]{2,1,0:T(8,128)(2,1)} async-done(((bf16[32,24,128]{2,1,0:T(8,128)(2,1)}), bf16[32,24,128]{2,1,0:T(8,128)(2,1)}, u32[]{:S(2)}, u32[]{:S(2)}) %all-to-all-start.12) | async-done | bytes 196640 | tf_op jit(solution)/shard_map/all_to_all | solution.py:22
  241.7 1.8 fusion.87
  243.5 1.1 fusion.37
  244.7 14.0 %all_to_all.120 = bf16[32,24,128]{2,1,0:T(8,128)(2,1)S(1)} all-to-all(bf16[32,24,128]{2,1,0:T(8,128)(2,1)S(1)} %broadcast_in_dim.51), channel_id=1, replica_groups=mesh['yl'=2,'x'=4,'c'=2,'yh'=4,'z'=8] {'yl','x','yh'}, dimensions={0} | all-to-all | bytes 393216 | tf_op jit(solution)/shard_map/all_to_all | solution.py:22
  259.3 14.1 %all_to_all.121 = bf16[32,24,128]{2,1,0:T(8,128)(2,1)S(1)} all-to-all(bf16[32,24,128]{2,1,0:T(8,128)(2,1)S(1)} %broadcast_in_dim.52), channel_id=1, replica_groups=mesh['yl'=2,'x'=4,'c'=2,'yh'=4,'z'=8] {'yl','x','yh'}, dimensions={0} | all-to-all | bytes 393216 | tf_op jit(solution)/shard_map/all_to_all | solution.py:22
  274.0 13.9 %all_to_all.122 = bf16[32,24,128]{2,1,0:T(8,128)(2,1)S(1)} all-to-all(bf16[32,24,128]{2,1,0:T(8,128)(2,1)S(1)} %broadcast_in_dim.53), channel_id=1, replica_groups=mesh['yl'=2,'x'=4,'c'=2,'yh'=4,'z'=8] {'yl','x','yh'}, dimensions={0} | all-to-all | bytes 393216 | tf_op jit(solution)/shard_map/all_to_all | solution.py:22
  288.5 13.7 %all_to_all.123 = bf16[32,24,128]{2,1,0:T(8,128)(2,1)S(1)} all-to-all(bf16[32,24,128]{2,1,0:T(8,128)(2,1)S(1)} %broadcast_in_dim.54), channel_id=1, replica_groups=mesh['yl'=2,'x'=4,'c'=2,'yh'=4,'z'=8] {'yl','x','yh'}, dimensions={0} | all-to-all | bytes 393216 | tf_op jit(solution)/shard_map/all_to_all | solution.py:22
  303.7 3.9 all-to-all-start.17
  307.5 0.8 dynamic_slice.3
  308.4 8.8 %all-to-all-done.17 = bf16[32,24,128]{2,1,0:T(8,128)(2,1)S(1)} async-done(((bf16[32,24,128]{2,1,0:T(8,128)(2,1)}), bf16[32,24,128]{2,1,0:T(8,128)(2,1)S(1)}, u32[]{:S(2)}, u32[]{:S(2)}) %all-to-all-start.17) | async-done | bytes 196640 | tf_op jit(solution)/shard_map/all_to_all | solution.py:22
  318.5 4.6 %all-to-all-start.18 = ((bf16[32,24,128]{2,1,0:T(8,128)(2,1)}), bf16[32,24,128]{2,1,0:T(8,128)(2,1)}, u32[]{:S(2)}, u32[]{:S(2)}) async-start(bf16[32,24,128]{2,1,0:T(8,128)(2,1)} %broadcast_in_dim.56), calls=%async_computation.18 | async-start | bytes 393216 | tf_op jit(solution)/shard_map/all_to_all | solution.py:22
  323.1 4.4 %fusion.6 = bf16[8,2,16,8,4,128]{5,2,4,0,1,3:T(8,128)(2,1)S(1)} fusion(bf16[2,8,8,4,16,128]{5,4,3,2,1,0:T(8,128)(2,1)} %bitcast.613, s32[8,128]{1,0:T(8,128)S(1)} %get-tuple-element.62, s32[8,128]{1,0:T(8,128)S(1)} %get-tuple-element.63), kind=kOutput, calls=%fused_computation.7 | convolution fusion | flops 2149580800 | bytes 4202496 | tf_op jit(solution)/shard_map/czpyal,zlum->pcauym/dot_general | solution.py:99
  327.5 1.0 copy.140
  328.5 2.8 reshape.269
  331.4 1.2 fusion.157
  332.6 1.1 convolution_add_fusion.17
  333.7 1.1 convolution_add_fusion.16
  334.9 1.2 convolution_add_fusion.15
  336.1 1.1 convolution_add_fusion.14
  337.2 1.1 convolution_add_fusion.13
  338.9 1.1 convolution_add_fusion.9
  341.0 1.1 fusion.44
  342.3 17.8 %all_to_all.124 = bf16[32,2,192]{2,1,0:T(2,128)(2,1)S(1)} all-to-all(bf16[32,2,192]{2,1,0:T(2,128)(2,1)S(1)} %reshape.305), channel_id=1, replica_groups=mesh['yl'=2,'x'=4,'c'=2,'yh'=4,'z'=8] {'yl','x','yh'}, dimensions={0} | all-to-all | bytes 49152 | tf_op jit(solution)/shard_map/all_to_all | solution.py:22
  360.4 6.6 %fusion.247 = (bf16[1,8,1,16,4096]{4,3,2,1,0:T(8,128)(2,1)S(1)}, bf16[1,8,1,16,4096]{4,3,2,1,0:T(8,128)(2,1)S(1)}, bf16[1,8,1,16,4096]{4,3,2,1,0:T(8,128)(2,1)S(...) fusion(bf16[2,8,8,16,4096]{4,3,2,1,0:T(8,128)(2,1)} %bitcast.543), kind=kLoop, calls=%fused_computation.315 | loop fusion | bytes 33554432 | tf_op jit(solution)/shard_map/slice | solution.py:75
  368.3 1.3 fusion.52
  371.8 1.4 fusion.64
  375.4 1.3 fusion.76
  378.4 39.1 %all_to_all.125 = bf16[16,120,128]{2,1,0:T(8,128)(2,1)S(1)} all-to-all(bf16[16,120,128]{2,1,0:T(8,128)(2,1)S(1)} %pad_maximum_fusion.1), channel_id=1, replica_groups=mesh['yl'=2,'x'=4,'c'=2,'yh'=4,'z'=8] {'c','z'}, dimensions={0} | all-to-all | bytes 983040 | tf_op jit(solution)/shard_map/all_to_all | solution.py:116
  417.9 1.1 reshape.272
  419.1 3.4 all-to-all-start.21
  423.4 1.1 convolution_add_fusion
  424.5 3.2 all-to-all-done.21
  (191 shorter events, 24.7 us)
Async XLA Ops:
  7.2 78.4 %all-gather.12.cloned.1.call-start = ((), (), s32[]{:S(2)}) async-start(), calls=%async_computation.23 | async-start | bytes 4874240 | tf_op jit(solution)/shard_map/all_gather | solution.py:66
  7.2 2.7 copy-start.40
  13.5 19.4 %copy-start.5 = (bf16[1,128,4096]{2,1,0:T(8,128)(2,1)S(1)}, bf16[1,128,4096]{2,1,0:T(8,128)(2,1)}, u32[]{:S(2)}) copy-start(bf16[1,128,4096]{2,1,0:T(8,128)(2,1)} %param.11) | copy-start | bytes 3145732
  37.3 12.9 %all-to-all-start.2 = ((bf16[8,16,4096]{2,1,0:T(8,128)(2,1)}), bf16[8,16,4096]{2,1,0:T(8,128)(2,1)S(1)}, u32[]{:S(2)}, u32[]{:S(2)}) async-start(bf16[8,16,4096]{2,1,0:T(8,128)(2,1)} %reshape_reshape.22), calls=%async_computation.2 | async-start | bytes 2097152 | tf_op jit(solution)/shard_map/all_to_all | solution.py:67
  40.9 9.4 %copy-start.39 = (bf16[1,512,128]{2,1,0:T(8,128)(2,1)S(1)}, bf16[1,512,128]{2,1,0:T(8,128)(2,1)}, u32[]{:S(2)}) copy-start(bf16[1,512,128]{2,1,0:T(8,128)(2,1)} %param.12) | copy-start | bytes 393220
  40.9 101.6 %all-gather.14.cloned.1.call-start = ((), (), s32[]{:S(2)}) async-start(), calls=%async_computation.24 | async-start | bytes 7311360 | tf_op jit(solution)/shard_map/all_gather | solution.py:69
  50.2 37.9 %copy-start = (bf16[8,16,4096]{2,1,0:T(8,128)(2,1)}, bf16[8,16,4096]{2,1,0:T(8,128)(2,1)S(1)}, u32[]{:S(2)}) copy-start(bf16[8,16,4096]{2,1,0:T(8,128)(2,1)S(1)} %all-to-all-done.2) | copy-start | bytes 3145732
  50.2 181.9 %all-gather.18.cloned.1.call-start = ((), (), s32[]{:S(2)}) async-start(), calls=%async_computation.26 | async-start | bytes 7311360 | tf_op jit(solution)/shard_map/all_gather | solution.py:72
  107.7 15.3 %copy-start.6 = (bf16[32,24,128]{2,1,0:T(8,128)(2,1)}, bf16[32,24,128]{2,1,0:T(8,128)(2,1)S(1)}, u32[]{:S(2)}) copy-start(bf16[32,24,128]{2,1,0:T(8,128)(2,1)S(1)} %all_to_all.112) | copy-start | bytes 589828
  122.6 14.2 %copy-start.8 = (bf16[32,24,128]{2,1,0:T(8,128)(2,1)}, bf16[32,24,128]{2,1,0:T(8,128)(2,1)S(1)}, u32[]{:S(2)}) copy-start(bf16[32,24,128]{2,1,0:T(8,128)(2,1)S(1)} %all_to_all.113) | copy-start | bytes 589828
  136.4 0.7 copy-start.10
  137.9 14.2 %all-to-all-start.5 = ((bf16[32,24,128]{2,1,0:T(8,128)(2,1)}), bf16[32,24,128]{2,1,0:T(8,128)(2,1)}, u32[]{:S(2)}, u32[]{:S(2)}) async-start(bf16[32,24,128]{2,1,0:T(8,128)(2,1)} %broadcast_in_dim.44), calls=%async_computation.5 | async-start | bytes 393216 | tf_op jit(solution)/shard_map/all_to_all | solution.py:22
  142.4 180.6 %all-gather.10.cloned.1.call-start = ((), (), s32[]{:S(2)}) async-start(), calls=%async_computation.22 | async-start | bytes 2228224 | tf_op jit(solution)/shard_map/all_gather | solution.py:95
  152.1 16.9 %copy-start.3 = (bf16[1,8,1,16,4480]{4,3,2,1,0:T(8,128)(2,1)S(1)}, bf16[1,8,1,16,4480]{4,3,2,1,0:T(8,128)(2,1)}, u32[]{:S(2)}) copy-start(bf16[1,8,1,16,4480]{4,3,2,1,0:T(8,128)(2,1)} %get-tuple-element.51) | copy-start | bytes 3440644
  169.0 0.7 copy-start.12
  169.7 190.7 %all-gather.16.cloned.1.call-start = ((), (), s32[]{:S(2)}) async-start(), calls=%async_computation.25 | async-start | bytes 17825792 | tf_op jit(solution)/shard_map/all_gather | solution.py:94
  183.2 16.2 %copy-start.14 = (bf16[32,24,128]{2,1,0:T(8,128)(2,1)}, bf16[32,24,128]{2,1,0:T(8,128)(2,1)S(1)}, u32[]{:S(2)}) copy-start(bf16[32,24,128]{2,1,0:T(8,128)(2,1)S(1)} %all_to_all.116) | copy-start | bytes 589828
  199.0 13.9 %copy-start.16 = (bf16[32,24,128]{2,1,0:T(8,128)(2,1)}, bf16[32,24,128]{2,1,0:T(8,128)(2,1)S(1)}, u32[]{:S(2)}) copy-start(bf16[32,24,128]{2,1,0:T(8,128)(2,1)S(1)} %all_to_all.117) | copy-start | bytes 589828
  212.6 13.9 %copy-start.18 = (bf16[32,24,128]{2,1,0:T(8,128)(2,1)}, bf16[32,24,128]{2,1,0:T(8,128)(2,1)S(1)}, u32[]{:S(2)}) copy-start(bf16[32,24,128]{2,1,0:T(8,128)(2,1)S(1)} %all_to_all.118) | copy-start | bytes 589828
  226.1 0.7 copy-start.20
  227.5 14.2 %all-to-all-start.12 = ((bf16[32,24,128]{2,1,0:T(8,128)(2,1)}), bf16[32,24,128]{2,1,0:T(8,128)(2,1)}, u32[]{:S(2)}, u32[]{:S(2)}) async-start(bf16[32,24,128]{2,1,0:T(8,128)(2,1)} %broadcast_in_dim.50), calls=%async_computation.12 | async-start | bytes 393216 | tf_op jit(solution)/shard_map/all_to_all | solution.py:22
  241.7 16.9 %copy-start.4 = (bf16[1,8,1,16,4480]{4,3,2,1,0:T(8,128)(2,1)S(1)}, bf16[1,8,1,16,4480]{4,3,2,1,0:T(8,128)(2,1)}, u32[]{:S(2)}) copy-start(bf16[1,8,1,16,4480]{4,3,2,1,0:T(8,128)(2,1)} %get-tuple-element.44) | copy-start | bytes 3440644
  244.7 28.7 %copy-start.2 = (bf16[1,8,1,16,4480]{4,3,2,1,0:T(8,128)(2,1)S(1)}, bf16[1,8,1,16,4480]{4,3,2,1,0:T(8,128)(2,1)}, u32[]{:S(2)}) copy-start(bf16[1,8,1,16,4480]{4,3,2,1,0:T(8,128)(2,1)} %get-tuple-element.43) | copy-start | bytes 3440644
  258.7 15.1 %copy-start.23 = (bf16[32,24,128]{2,1,0:T(8,128)(2,1)}, bf16[32,24,128]{2,1,0:T(8,128)(2,1)S(1)}, u32[]{:S(2)}) copy-start(bf16[32,24,128]{2,1,0:T(8,128)(2,1)S(1)} %all_to_all.120) | copy-start | bytes 589828
  273.4 14.9 %copy-start.26 = (bf16[32,24,128]{2,1,0:T(8,128)(2,1)}, bf16[32,24,128]{2,1,0:T(8,128)(2,1)S(1)}, u32[]{:S(2)}) copy-start(bf16[32,24,128]{2,1,0:T(8,128)(2,1)S(1)} %all_to_all.121) | copy-start | bytes 589828
  287.9 14.7 %copy-start.29 = (bf16[32,24,128]{2,1,0:T(8,128)(2,1)}, bf16[32,24,128]{2,1,0:T(8,128)(2,1)S(1)}, u32[]{:S(2)}) copy-start(bf16[32,24,128]{2,1,0:T(8,128)(2,1)S(1)} %all_to_all.122) | copy-start | bytes 589828
  302.3 0.7 copy-start.32
  303.7 13.5 %all-to-all-start.17 = ((bf16[32,24,128]{2,1,0:T(8,128)(2,1)}), bf16[32,24,128]{2,1,0:T(8,128)(2,1)S(1)}, u32[]{:S(2)}, u32[]{:S(2)}) async-start(bf16[32,24,128]{2,1,0:T(8,128)(2,1)} %broadcast_in_dim.55), calls=%async_computation.17 | async-start | bytes 393216 | tf_op jit(solution)/shard_map/all_to_all | solution.py:22
  317.2 5.9 %copy-start.35 = (bf16[32,24,128]{2,1,0:T(8,128)(2,1)}, bf16[32,24,128]{2,1,0:T(8,128)(2,1)S(1)}, u32[]{:S(2)}) copy-start(bf16[32,24,128]{2,1,0:T(8,128)(2,1)S(1)} %all-to-all-done.17) | copy-start | bytes 589828
  318.5 22.5 %all-to-all-start.18 = ((bf16[32,24,128]{2,1,0:T(8,128)(2,1)}), bf16[32,24,128]{2,1,0:T(8,128)(2,1)}, u32[]{:S(2)}, u32[]{:S(2)}) async-start(bf16[32,24,128]{2,1,0:T(8,128)(2,1)} %broadcast_in_dim.56), calls=%async_computation.18 | async-start | bytes 393216 | tf_op jit(solution)/shard_map/all_to_all | solution.py:22
  328.5 2.9 copy-start.7
  328.5 4.1 copy-start.9
  328.5 5.2 %copy-start.11 = (bf16[32,24,128]{2,1,0:T(8,128)(2,1)S(1)}, bf16[32,24,128]{2,1,0:T(8,128)(2,1)}, u32[]{:S(2)}) copy-start(bf16[32,24,128]{2,1,0:T(8,128)(2,1)} %copy-done.10) | copy-start | bytes 589828
  328.5 7.5 %copy-start.13 = (bf16[32,24,128]{2,1,0:T(8,128)(2,1)S(1)}, bf16[32,24,128]{2,1,0:T(8,128)(2,1)}, u32[]{:S(2)}) copy-start(bf16[32,24,128]{2,1,0:T(8,128)(2,1)} %copy-done.12) | copy-start | bytes 589828
  328.5 8.6 %copy-start.15 = (bf16[32,24,128]{2,1,0:T(8,128)(2,1)S(1)}, bf16[32,24,128]{2,1,0:T(8,128)(2,1)}, u32[]{:S(2)}) copy-start(bf16[32,24,128]{2,1,0:T(8,128)(2,1)} %copy-done.14) | copy-start | bytes 589828
  331.4 6.9 %copy-start.1 = (bf16[16,16,4096]{2,1,0:T(8,128)(2,1)S(1)}, bf16[16,16,4096]{2,1,0:T(8,128)(2,1)}, u32[]{:S(2)}) copy-start(bf16[16,16,4096]{2,1,0:T(8,128)(2,1)} %reshape.269) | copy-start | bytes 6291460
  331.4 7.0 %copy-start.17 = (bf16[32,24,128]{2,1,0:T(8,128)(2,1)S(1)}, bf16[32,24,128]{2,1,0:T(8,128)(2,1)}, u32[]{:S(2)}) copy-start(bf16[32,24,128]{2,1,0:T(8,128)(2,1)} %copy-done.16) | copy-start | bytes 589828
  332.6 5.9 %copy-start.19 = (bf16[32,24,128]{2,1,0:T(8,128)(2,1)S(1)}, bf16[32,24,128]{2,1,0:T(8,128)(2,1)}, u32[]{:S(2)}) copy-start(bf16[32,24,128]{2,1,0:T(8,128)(2,1)} %copy-done.18) | copy-start | bytes 589828
  333.7 5.0 %copy-start.21 = (bf16[32,24,128]{2,1,0:T(8,128)(2,1)S(1)}, bf16[32,24,128]{2,1,0:T(8,128)(2,1)}, u32[]{:S(2)}) copy-start(bf16[32,24,128]{2,1,0:T(8,128)(2,1)} %copy-done.20) | copy-start | bytes 589828
  336.0 4.0 copy-start.24
  337.2 3.0 copy-start.27
  338.3 2.1 copy-start.30
  338.5 2.1 copy-start.33
  338.7 2.1 copy-start.36
  370.4 0.9 copy-start.22
  371.4 1.8 copy-start.25
  371.8 1.8 copy-start.28
  373.1 0.9 copy-start.31
  373.6 1.0 copy-start.34
  374.1 0.9 copy-start.37
  417.9 4.6 %copy-start.38 = (bf16[512,512]{1,0:T(8,128)(2,1)S(1)}, bf16[512,512]{1,0:T(8,128)(2,1)}, u32[]{:S(2)}) copy-start(bf16[512,512]{1,0:T(8,128)(2,1)} %param.13) | copy-start | bytes 1572868
  419.1 8.6 %all-to-all-start.21 = ((bf16[8,384,16]{1,2,0:T(8,128)(2,1)}), bf16[8,384,16]{1,2,0:T(8,128)(2,1)S(1)}, u32[]{:S(2)}, u32[]{:S(2)}) async-start(bf16[8,384,16]{1,2,0:T(8,128)(2,1)} %bitcast.112), calls=%async_computation.21 | async-start | bytes 196608 | tf_op jit(solution)/shard_map/all_to_all | solution.py:123
Sparse Core Ops, SparseCore 0:
  33.0 52.4 all-gather.11
  87.6 50.4 all-gather.13
  140.8 50.3 all-gather.17
  193.2 41.3 all-gather.9
  236.5 96.6 all-gather.15

commit v6 on v5

v6 whole, which is shorter than its diff:
```python
import jax
import jax.numpy as jnp
import numpy as np
from jax import lax
from jax.sharding import Mesh
from jax.sharding import PartitionSpec as P

TILE = 128
CONTRACT = (((1,), (1,)), ((), ()))
AXES = ("yl", "x", "c", "yh", "z")
SIZES = (2, 4, 2, 4, 8)
DEAL = ("yl", "x")
COPY = ("c", "z")
CHAIN = ("yl", "x", "yh")
CHUNKS = (2, 2, 4)
OUT_AFTER = 2


def spread(value, axis):
    count = lax.axis_size(axis)
    copies = jnp.broadcast_to(value[None], (count, *value.shape))
    return lax.all_to_all(copies, axis, 0, 0)


def chain_order(deal, lower, piece):
    old = jnp.arange(lower * deal * piece).reshape(lower, deal, piece)
    new = old.transpose(1, 0, 2).reshape(deal, lower * piece)
    return (old.reshape(lower, deal * piece, 1, 1) == new).astype(jnp.bfloat16)


def product(left, right):
    return lax.dot_general(left, right, CONTRACT, preferred_element_type=jnp.float32)


def per_device(rhs_nodes, rhs_arrow, coupling, pattern, pivot_inverse, arrow_factor, tip_inverse):
    _, local_rows, node_count = coupling.shape
    rhs_count = rhs_nodes.shape[1]
    arrow_count = arrow_factor.shape[1]
    deal, copies, group = (lax.axis_size(axes) for axes in (DEAL, COPY, CHAIN))
    cores, lower = lax.axis_size("c"), lax.axis_size("z")
    steps = deal * cores
    piece = local_rows // deal
    width = rhs_count // copies
    mine = lax.axis_index(COPY)

    weights = pattern.astype(jnp.bfloat16)[0, :, None, :, None]
    masked = (coupling.reshape(local_rows // TILE, TILE, node_count // TILE, TILE) * weights).reshape(
        local_rows, node_count
    )
    upper = lax.axis_size("yh")
    order = chain_order(deal, lower, piece)

    def reorder(rows):
        moved = jnp.einsum(
            "ryzl,zlum->ruym",
            rows.reshape(local_rows, upper, lower, TILE),
            order,
            preferred_element_type=jnp.float32,
        )
        return moved.astype(jnp.bfloat16).reshape(local_rows, node_count)

    initial = jnp.zeros((8, node_count), jnp.bfloat16)
    entering = jnp.where(lax.axis_index(DEAL + ("c",)) == 0, product(masked, initial)[:, :1], 0.0)
    forcing = (rhs_nodes[0].T.astype(jnp.float32) - entering).astype(jnp.bfloat16)
    rows = jnp.concatenate([reorder(masked), forcing], 1)
    rows = lax.all_to_all(rows.reshape(deal, piece, -1), DEAL, 0, 0)
    forcing = rows[:, :, node_count:].reshape(deal * piece, copies, width).transpose(1, 0, 2)
    first, second, third = jnp.split(rows[:, :, :node_count], np.cumsum(CHUNKS)[:-1])
    links = [lax.all_gather(first, COPY, axis=0)]
    forcing = lax.all_to_all(forcing, COPY, 0, 0).reshape(cores, lower, deal, piece, width)
    forcing = forcing.transpose(2, 0, 4, 1, 3).reshape(steps, width, local_rows)
    previous = spread(forcing[0], CHAIN)
    second, previous = lax.optimization_barrier((second, previous))
    links.append(lax.all_gather(second, COPY, axis=0))
    out_rows = jnp.concatenate([reorder(pivot_inverse[0]), arrow_factor[0].T], 1)
    out_rows = lax.all_to_all(out_rows.reshape(deal, piece, -1), DEAL, 0, 0)
    third, out_rows = lax.optimization_barrier((third, out_rows))
    links.append(lax.all_gather(third, COPY, axis=0))

    def of_step(held, pair, core):
        return held.reshape(cores, lower, *held.shape[1:])[core, :, pair].reshape(local_rows, -1)

    def link_rows(step):
        pair, core = step // cores, step % cores
        for chunk, pairs in enumerate(CHUNKS):
            if pair < pairs:
                return of_step(links[chunk], pair, core)
            pair -= pairs

    def whole(gathered):
        return gathered.transpose(1, 0, 2).reshape(width, node_count)

    parts = [forcing[0]]
    history = [whole(previous)]
    for step in range(1, steps):
        linked = product(history[-1], link_rows(step))
        fresh = (forcing[step].astype(jnp.float32) - linked).astype(jnp.bfloat16)
        if step == OUT_AFTER:
            fresh, out_rows = lax.optimization_barrier((fresh, out_rows))
            out_rows = lax.all_gather(out_rows, COPY, axis=0)
        parts.append(fresh)
        if step < steps - 1:
            history.append(whole(spread(fresh, CHAIN)))

    held = [of_step(out_rows, step // cores, step % cores) for step in range(steps)]
    terms = jnp.zeros((width, arrow_count), jnp.float32)
    for step in range(steps):
        terms = terms + jnp.dot(parts[step], held[step][:, node_count:], preferred_element_type=jnp.float32)
    tiles = arrow_count // TILE
    share = width // (group // tiles)
    terms = terms.reshape(group // tiles, share, tiles, TILE).transpose(0, 2, 1, 3).reshape(group, share, TILE)
    last = jnp.broadcast_to(parts[-1].astype(jnp.float32), (group, width, local_rows))
    arrived = lax.all_to_all(jnp.concatenate([last, terms], 1), CHAIN, 0, 0)
    history.append(whole(arrived[:, :width].astype(jnp.bfloat16)))
    place = lax.axis_index(CHAIN)
    corner = (mine * width + place // tiles * share, place % tiles * TILE)
    own = lax.dynamic_slice(rhs_arrow, corner, (share, TILE))
    rest = spread((own - jnp.sum(arrived[:, width:], 0)).astype(jnp.bfloat16), CHAIN)
    rest = rest.reshape(group // tiles, tiles, share, TILE).transpose(1, 0, 2, 3).reshape(1, tiles * width, TILE)
    solved = [product(history[step], held[step][:, :node_count]).astype(jnp.bfloat16) for step in range(steps)]

    solved = jnp.stack(solved).reshape(deal, cores, width, lower, piece)
    solved = solved.transpose(1, 3, 2, 0, 4).reshape(copies, width, deal * piece)
    sent = jnp.concatenate([solved, jnp.broadcast_to(rest, (copies, tiles * width, TILE))], 1)
    arrived = lax.all_to_all(sent, COPY, 0, 0)
    rest = arrived[:, width:].reshape(copies, tiles, width, TILE)
    arrow_solved = sum(
        product(rest[:, part].reshape(rhs_count, TILE), tip_inverse[:, part * TILE : (part + 1) * TILE])
        for part in range(tiles)
    )
    solved = arrived[:, :width].reshape(rhs_count, deal, piece).transpose(1, 0, 2)
    solved = lax.all_to_all(solved, DEAL, 0, 0)
    solved = solved.transpose(1, 0, 2).reshape(1, rhs_count, local_rows)
    return (solved, arrow_solved)


def solution(mesh):
    fine = Mesh(mesh.devices.reshape(SIZES), AXES)
    steps, nodes = ("yl", "x", "c"), ("yh", "z")
    placed = (
        P(steps, None, nodes),
        P(),
        P(steps, nodes, None),
        P(steps, nodes, None),
        P(steps, nodes, None),
        P(steps, None, nodes),
        P(),
    )
    return jax.shard_map(
        per_device,
        mesh=fine,
        in_specs=placed,
        out_specs=(P(steps, None, nodes), P()),
        check_vma=False,
    )
```

time: 438 us -> 435 us (level)
  blocking collectives: 268 us -> 251 us
  starting transfers between devices: 24.7 us -> 31.9 us
    all_to_all x13 -> x12, blocking collectives: 186 us -> 171 us  [spread(): return lax.all_to_all(copies, axis, 0, 0)]
    all_gather x1, waiting for transfers between devices: 10.6 us -> 0.02 us  [per_device(): links = [lax.all_gather(first, COPY, axis=0)]]
    all_to_all x4, waiting for transfers between devices: 18 us -> 24.7 us  [spread(): return lax.all_to_all(copies, axis, 0, 0)]
    all_to_all x1 -> x2, waiting for transfers between devices: 8.32 us -> 11.5 us  [the longest x1 11.5 us: per_device(): out_rows = lax.all_to_all(out_rows.reshape(deal, piece, -1), DEAL, 0, 0)]
    dot_general x68 -> x36, matrix products: 37.5 us -> 38.3 us  [product(): lax.dot_general(left, right, CONTRACT, preferred_element_type=jnp.float32)]
where the time goes in v6:
time: 435 us; the launch traced here: 432 us
  blocking collectives  251 us (58%)
  local copies, waits for them, and re-layouts  45.6 us (10%)
  matrix products  45 us (10%)
  waiting for transfers between devices  39.6 us (9%)
  starting transfers between devices  31.9 us (7%)
  between operations  14.9 us (3%)
  other arithmetic  4.37 us (1%)
    all_to_all x12, blocking collectives, spread(): return lax.all_to_all(copies, axis, 0, 0)  171 us
    all_to_all x1, blocking collectives, per_device(): arrived = lax.all_to_all(sent, COPY, 0, 0)  39 us
    dot_general x36, matrix products, product(): lax.dot_general(left, right, CONTRACT, preferred_element_type=jnp.float32)  38.3 us
    all_to_all x4, waiting for transfers between devices, spread(): return lax.all_to_all(copies, axis, 0, 0)  24.7 us
    all_to_all x1, blocking collectives, per_device(): lax.all_to_all(forcing, COPY, 0, 0)  22.6 us
    all_to_all x4, starting transfers between devices, spread(): return lax.all_to_all(copies, axis, 0, 0)  20.7 us
    slice x4, local copies, waits for them, and re-layouts, of_step(): held.reshape(cores, lower, *held.shape[1:])[core, :, pair]  20 us
    all_to_all x1, blocking collectives, per_device(): rows = lax.all_to_all(rows.reshape(deal, piece, -1), DEAL, 0, 0)  18.4 us
  transfers between devices with their start and end apart: 11, of which 6 were waited for; matrix products, arithmetic and copies ran while one was open for 14% of the time, Pallas kernels for 0%

profile of v6, /device:TPU:1, one launch (start us, length us, event | category | flops | bytes accessed | tf_op | source)
XLA Modules:
  0.0 432.0 jit_solution(9184897734977333716)
XLA Ops:
  8.6 1.0 copy.133
  9.8 1.5 copy.181
  11.4 1.4 fusion.14
  15.5 18.4 %all_to_all.110 = bf16[8,16,4480]{2,1,0:T(8,128)(2,1)S(1)} all-to-all(bf16[8,16,4480]{2,1,0:T(8,128)(2,1)S(1)} %pad_maximum_fusion.1), channel_id=1, replica_groups=mesh['yl'=2,'x'=4,'c'=2,'yh'=4,'z'=8] {'yl','x'}, dimensions={0} | all-to-all | bytes 2293760 | tf_op jit(solution)/shard_map/all_to_all | solution.py:66
  36.0 22.6 %all_to_all.111 = bf16[16,128,24]{1,2,0:T(8,128)(2,1)S(1)} all-to-all(bf16[16,128,24]{1,2,0:T(8,128)(2,1)S(1)} %copy.134), channel_id=1, replica_groups=mesh['yl'=2,'x'=4,'c'=2,'yh'=4,'z'=8] {'c','z'}, dimensions={0} | all-to-all | bytes 196608 | tf_op jit(solution)/shard_map/all_to_all | solution.py:70
  60.2 16.3 %all_to_all.112 = bf16[32,24,128]{2,1,0:T(8,128)(2,1)S(1)} all-to-all(bf16[32,24,128]{2,1,0:T(8,128)(2,1)S(1)} %broadcast_in_dim.49), channel_id=1, replica_groups=mesh['yl'=2,'x'=4,'c'=2,'yh'=4,'z'=8] {'yl','x','yh'}, dimensions={0} | all-to-all | bytes 393216 | tf_op jit(solution)/shard_map/all_to_all | solution.py:22
  76.6 1.5 copy.182
  78.1 1.3 fusion.17
  81.2 1.0 copy.140
  82.2 1.1 pad_maximum_fusion
  83.4 3.6 all-to-all-start.4
  87.8 11.5 %all-to-all-done.4 = bf16[8,16,4608]{2,1,0:T(8,128)(2,1)S(1)} async-done(((bf16[8,16,4608]{2,1,0:T(8,128)(2,1)}), bf16[8,16,4608]{2,1,0:T(8,128)(2,1)S(1)}, u32[]{:S(2)}, u32[]{:S(2)}) %all-to-all-start.4) | async-done | bytes 1179680 | tf_op jit(solution)/shard_map/all_to_all | solution.py:76
  99.4 2.5 fusion.180
  102.4 18.4 %all_to_all.113 = bf16[32,24,128]{2,1,0:T(8,128)(2,1)S(1)} all-to-all(bf16[32,24,128]{2,1,0:T(8,128)(2,1)S(1)} %broadcast_in_dim.50), channel_id=1, replica_groups=mesh['yl'=2,'x'=4,'c'=2,'yh'=4,'z'=8] {'yl','x','yh'}, dimensions={0} | all-to-all | bytes 393216 | tf_op jit(solution)/shard_map/all_to_all | solution.py:22
  122.0 14.1 %all_to_all.114 = bf16[32,24,128]{2,1,0:T(8,128)(2,1)S(1)} all-to-all(bf16[32,24,128]{2,1,0:T(8,128)(2,1)S(1)} %broadcast_in_dim.51), channel_id=1, replica_groups=mesh['yl'=2,'x'=4,'c'=2,'yh'=4,'z'=8] {'yl','x','yh'}, dimensions={0} | all-to-all | bytes 393216 | tf_op jit(solution)/shard_map/all_to_all | solution.py:22
  137.5 4.0 all-to-all-start.6
  141.6 3.5 fusion.179
  145.1 6.0 %all-to-all-done.6 = bf16[32,24,128]{2,1,0:T(8,128)(2,1)S(1)} async-done(((bf16[32,24,128]{2,1,0:T(8,128)(2,1)}), bf16[32,24,128]{2,1,0:T(8,128)(2,1)S(1)}, u32[]{:S(2)}, u32[]{:S(2)}) %all-to-all-start.6) | async-done | bytes 196640 | tf_op jit(solution)/shard_map/all_to_all | solution.py:22
  151.1 1.7 fusion.23
  152.8 13.2 %all_to_all.115 = bf16[32,24,128]{2,1,0:T(8,128)(2,1)S(1)} all-to-all(bf16[32,24,128]{2,1,0:T(8,128)(2,1)S(1)} %broadcast_in_dim.53), channel_id=1, replica_groups=mesh['yl'=2,'x'=4,'c'=2,'yh'=4,'z'=8] {'yl','x','yh'}, dimensions={0} | all-to-all | bytes 393216 | tf_op jit(solution)/shard_map/all_to_all | solution.py:22
  166.4 12.9 %all_to_all.116 = bf16[32,24,128]{2,1,0:T(8,128)(2,1)S(1)} all-to-all(bf16[32,24,128]{2,1,0:T(8,128)(2,1)S(1)} %broadcast_in_dim.54), channel_id=1, replica_groups=mesh['yl'=2,'x'=4,'c'=2,'yh'=4,'z'=8] {'yl','x','yh'}, dimensions={0} | all-to-all | bytes 393216 | tf_op jit(solution)/shard_map/all_to_all | solution.py:22
  179.8 13.0 %all_to_all.117 = bf16[32,24,128]{2,1,0:T(8,128)(2,1)S(1)} all-to-all(bf16[32,24,128]{2,1,0:T(8,128)(2,1)S(1)} %broadcast_in_dim.55), channel_id=1, replica_groups=mesh['yl'=2,'x'=4,'c'=2,'yh'=4,'z'=8] {'yl','x','yh'}, dimensions={0} | all-to-all | bytes 393216 | tf_op jit(solution)/shard_map/all_to_all | solution.py:22
  194.2 3.9 all-to-all-start.10
  198.1 5.7 %fusion.178 = (bf16[1,8,1,16,4096]{4,3,2,1,0:T(8,128)(2,1)S(1)}, bf16[1,8,1,16,4096]{4,3,2,1,0:T(8,128)(2,1)S(1)}, bf16[1,8,1,16,4096]{4,3,2,1,0:T(8,128)(2,1)S(...) fusion(bf16[2,8,4,16,4096]{4,3,2,1,0:T(8,128)(2,1)} %bitcast.504), kind=kLoop, calls=%fused_computation.254 | loop fusion | bytes 16777216 | tf_op jit(solution)/shard_map/slice | solution.py:81
  203.8 3.9 all-to-all-done.10
  207.7 1.8 fusion.27
  209.6 14.7 %all_to_all.118 = bf16[32,24,128]{2,1,0:T(8,128)(2,1)S(1)} all-to-all(bf16[32,24,128]{2,1,0:T(8,128)(2,1)S(1)} %broadcast_in_dim.57), channel_id=1, replica_groups=mesh['yl'=2,'x'=4,'c'=2,'yh'=4,'z'=8] {'yl','x','yh'}, dimensions={0} | all-to-all | bytes 393216 | tf_op jit(solution)/shard_map/all_to_all | solution.py:22
  224.3 1.1 fusion.28
  225.4 13.1 %all_to_all.119 = bf16[32,24,128]{2,1,0:T(8,128)(2,1)S(1)} all-to-all(bf16[32,24,128]{2,1,0:T(8,128)(2,1)S(1)} %broadcast_in_dim.58), channel_id=1, replica_groups=mesh['yl'=2,'x'=4,'c'=2,'yh'=4,'z'=8] {'yl','x','yh'}, dimensions={0} | all-to-all | bytes 393216 | tf_op jit(solution)/shard_map/all_to_all | solution.py:22
  238.5 1.1 fusion.29
  239.7 13.4 %all_to_all.120 = bf16[32,24,128]{2,1,0:T(8,128)(2,1)S(1)} all-to-all(bf16[32,24,128]{2,1,0:T(8,128)(2,1)S(1)} %broadcast_in_dim.59), channel_id=1, replica_groups=mesh['yl'=2,'x'=4,'c'=2,'yh'=4,'z'=8] {'yl','x','yh'}, dimensions={0} | all-to-all | bytes 393216 | tf_op jit(solution)/shard_map/all_to_all | solution.py:22
  253.1 1.1 fusion.30
  254.3 13.7 %all_to_all.121 = bf16[32,24,128]{2,1,0:T(8,128)(2,1)S(1)} all-to-all(bf16[32,24,128]{2,1,0:T(8,128)(2,1)S(1)} %broadcast_in_dim.60), channel_id=1, replica_groups=mesh['yl'=2,'x'=4,'c'=2,'yh'=4,'z'=8] {'yl','x','yh'}, dimensions={0} | all-to-all | bytes 393216 | tf_op jit(solution)/shard_map/all_to_all | solution.py:22
  268.0 1.1 fusion.31
  269.1 13.9 %all_to_all.122 = bf16[32,24,128]{2,1,0:T(8,128)(2,1)S(1)} all-to-all(bf16[32,24,128]{2,1,0:T(8,128)(2,1)S(1)} %broadcast_in_dim.61), channel_id=1, replica_groups=mesh['yl'=2,'x'=4,'c'=2,'yh'=4,'z'=8] {'yl','x','yh'}, dimensions={0} | all-to-all | bytes 393216 | tf_op jit(solution)/shard_map/all_to_all | solution.py:22
  283.0 1.1 fusion.32
  284.2 13.8 %all_to_all.123 = bf16[32,24,128]{2,1,0:T(8,128)(2,1)S(1)} all-to-all(bf16[32,24,128]{2,1,0:T(8,128)(2,1)S(1)} %broadcast_in_dim.62), channel_id=1, replica_groups=mesh['yl'=2,'x'=4,'c'=2,'yh'=4,'z'=8] {'yl','x','yh'}, dimensions={0} | all-to-all | bytes 393216 | tf_op jit(solution)/shard_map/all_to_all | solution.py:22
  298.0 1.1 fusion.33
  299.8 3.9 all-to-all-start.17
  303.7 9.6 %all-to-all-done.17 = bf16[32,24,128]{2,1,0:T(8,128)(2,1)S(1)} async-done(((bf16[32,24,128]{2,1,0:T(8,128)(2,1)}), bf16[32,24,128]{2,1,0:T(8,128)(2,1)S(1)}, u32[]{:S(2)}, u32[]{:S(2)}) %all-to-all-start.17) | async-done | bytes 196640 | tf_op jit(solution)/shard_map/all_to_all | solution.py:22
  313.3 1.7 fusion.34
  315.0 8.3 %fusion.177 = (bf16[1,8,1,16,4608]{4,3,2,1,0:T(8,128)(2,1)S(1)}, bf16[1,8,1,16,4608]{4,3,2,1,0:T(8,128)(2,1)S(1)}, bf16[1,8,1,16,4608]{4,3,2,1,0:T(8,128)(2,1)S(...) fusion(bf16[2,8,8,16,4608]{4,3,2,1,0:T(8,128)(2,1)} %bitcast.503), kind=kLoop, calls=%fused_computation.253 | loop fusion | bytes 37748736 | tf_op jit(solution)/shard_map/slice | solution.py:81
  323.4 4.3 %fusion.36 = bf16[16,24,128]{2,1,0:T(8,128)(2,1)} fusion(bf16[128,4608]{1,0:T(8,128)(2,1)} %bitcast.556, bf16[32,24,128]{2,1,0:T(8,128)(2,1)} %copy-done.31), kind=kOutput, calls=%fused_computation.81 | convolution fusion | flops 25168896 | bytes 1251328 | tf_op jit(solution)/shard_map/dot_general | solution.py:32
  327.8 1.4 fusion.168
  332.0 1.4 reshape.295
  335.2 4.1 all-to-all-start.18
  339.3 2.4 fusion.38
  341.8 2.4 fusion.40
  344.2 1.0 fusion.42
  346.2 1.0 fusion.46
  348.2 1.0 fusion.50
  349.2 1.0 fusion.52
  351.2 1.0 fusion.56
  352.2 1.0 fusion.58
  355.2 1.0 fusion.64
  357.6 8.9 %all-to-all-start.19 = ((bf16[32,3,128]{2,1,0:T(4,128)(2,1)}), bf16[32,3,128]{2,1,0:T(4,128)(2,1)S(1)}, u32[]{:S(2)}, u32[]{:S(2)}) async-start(bf16[32,3,128]{2,1,0:T(4,128)(2,1)} %broadcast_in_dim.65), calls=%async_computation.19 | async-start | bytes 65536 | tf_op jit(solution)/shard_map/all_to_all | solution.py:22
  366.6 1.0 fusion.66
  367.6 1.4 reshape.298
  370.0 5.2 %all-to-all-done.19 = bf16[32,3,128]{2,1,0:T(4,128)(2,1)S(1)} async-done(((bf16[32,3,128]{2,1,0:T(4,128)(2,1)}), bf16[32,3,128]{2,1,0:T(4,128)(2,1)S(1)}, u32[]{:S(2)}, u32[]{:S(2)}) %all-to-all-start.19) | async-done | bytes 24608 | tf_op jit(solution)/shard_map/all_to_all | solution.py:22
  375.4 39.0 %all_to_all.124 = bf16[16,120,128]{2,1,0:T(8,128)(2,1)S(1)} all-to-all(bf16[16,120,128]{2,1,0:T(8,128)(2,1)S(1)} %pad_maximum_fusion.3), channel_id=1, replica_groups=mesh['yl'=2,'x'=4,'c'=2,'yh'=4,'z'=8] {'c','z'}, dimensions={0} | all-to-all | bytes 983040 | tf_op jit(solution)/shard_map/all_to_all | solution.py:125
  415.0 1.1 reshape.301
  416.1 3.4 all-to-all-start.21
  420.3 1.1 convolution_add_fusion
  421.5 3.3 all-to-all-done.21
  (269 shorter events, 31.2 us)
Async XLA Ops:
  7.2 92.2 %all-gather.9.cloned.1.call-start = ((), (), s32[]{:S(2)}) async-start(), calls=%async_computation.22 | async-start | bytes 4456448 | tf_op jit(solution)/shard_map/all_gather | solution.py:69
  34.8 106.7 %all-gather.13.cloned.1.call-start = ((), (), s32[]{:S(2)}) async-start(), calls=%async_computation.24 | async-start | bytes 4456448 | tf_op jit(solution)/shard_map/all_gather | solution.py:74
  60.1 132.6 %copy-start.58 = (bf16[16,24,128]{2,1,0:T(8,128)(2,1)}, bf16[16,24,128]{2,1,0:T(8,128)(2,1)S(1)}, u32[]{:S(2)}) copy-start(bf16[16,24,128]{2,1,0:T(8,128)(2,1)S(1)} %reshape.275) | copy-start | bytes 294916
  76.5 25.4 %copy-start.31 = (bf16[32,24,128]{2,1,0:T(8,128)(2,1)}, bf16[32,24,128]{2,1,0:T(8,128)(2,1)S(1)}, u32[]{:S(2)}) copy-start(bf16[32,24,128]{2,1,0:T(8,128)(2,1)S(1)} %all_to_all.112) | copy-start | bytes 589828
  83.4 15.9 %all-to-all-start.4 = ((bf16[8,16,4608]{2,1,0:T(8,128)(2,1)}), bf16[8,16,4608]{2,1,0:T(8,128)(2,1)S(1)}, u32[]{:S(2)}, u32[]{:S(2)}) async-start(bf16[8,16,4608]{2,1,0:T(8,128)(2,1)} %pad_maximum_fusion), calls=%async_computation.4 | async-start | bytes 2359296 | tf_op jit(solution)/shard_map/all_to_all | solution.py:76
  87.0 111.1 %all-gather.15.cloned.1.call-start = ((), (), s32[]{:S(2)}) async-start(), calls=%async_computation.25 | async-start | bytes 8912896 | tf_op jit(solution)/shard_map/all_gather | solution.py:78
  99.3 2.6 copy-start
  99.3 215.6 %all-gather.11.cloned.1.call-start = ((), (), s32[]{:S(2)}) async-start(), calls=%async_computation.23 | async-start | bytes 20054016 | tf_op jit(solution)/shard_map/all_gather | solution.py:100
  136.8 4.8 %copy-start.59 = (bf16[24,128]{1,0:T(8,128)(2,1)}, bf16[24,128]{1,0:T(8,128)(2,1)S(1)}, u32[]{:S(2)}) copy-start(bf16[24,128]{1,0:T(8,128)(2,1)S(1)} %fusion.22) | copy-start | bytes 18436
  137.5 13.6 %all-to-all-start.6 = ((bf16[32,24,128]{2,1,0:T(8,128)(2,1)}), bf16[32,24,128]{2,1,0:T(8,128)(2,1)S(1)}, u32[]{:S(2)}, u32[]{:S(2)}) async-start(bf16[32,24,128]{2,1,0:T(8,128)(2,1)} %broadcast_in_dim.52), calls=%async_computation.6 | async-start | bytes 393216 | tf_op jit(solution)/shard_map/all_to_all | solution.py:22
  151.1 15.3 %copy-start.33 = (bf16[32,24,128]{2,1,0:T(8,128)(2,1)}, bf16[32,24,128]{2,1,0:T(8,128)(2,1)S(1)}, u32[]{:S(2)}) copy-start(bf16[32,24,128]{2,1,0:T(8,128)(2,1)S(1)} %all-to-all-done.6) | copy-start | bytes 589828
  152.7 26.6 %copy-start.61 = (bf16[24,128]{1,0:T(8,128)(2,1)}, bf16[24,128]{1,0:T(8,128)(2,1)S(1)}, u32[]{:S(2)}) copy-start(bf16[24,128]{1,0:T(8,128)(2,1)S(1)} %fusion.23) | copy-start | bytes 18436
  166.0 13.8 %copy-start.35 = (bf16[32,24,128]{2,1,0:T(8,128)(2,1)}, bf16[32,24,128]{2,1,0:T(8,128)(2,1)S(1)}, u32[]{:S(2)}) copy-start(bf16[32,24,128]{2,1,0:T(8,128)(2,1)S(1)} %all_to_all.115) | copy-start | bytes 589828
  166.4 26.4 %copy-start.63 = (bf16[24,128]{1,0:T(8,128)(2,1)}, bf16[24,128]{1,0:T(8,128)(2,1)S(1)}, u32[]{:S(2)}) copy-start(bf16[24,128]{1,0:T(8,128)(2,1)S(1)} %fusion.24) | copy-start | bytes 18436
  179.4 13.8 %copy-start.37 = (bf16[32,24,128]{2,1,0:T(8,128)(2,1)}, bf16[32,24,128]{2,1,0:T(8,128)(2,1)S(1)}, u32[]{:S(2)}) copy-start(bf16[32,24,128]{2,1,0:T(8,128)(2,1)S(1)} %all_to_all.116) | copy-start | bytes 589828
  179.8 14.4 %copy-start.65 = (bf16[24,128]{1,0:T(8,128)(2,1)}, bf16[24,128]{1,0:T(8,128)(2,1)S(1)}, u32[]{:S(2)}) copy-start(bf16[24,128]{1,0:T(8,128)(2,1)S(1)} %fusion.25) | copy-start | bytes 18436
  193.5 10.3 %copy-start.67 = (bf16[24,128]{1,0:T(8,128)(2,1)}, bf16[24,128]{1,0:T(8,128)(2,1)S(1)}, u32[]{:S(2)}) copy-start(bf16[24,128]{1,0:T(8,128)(2,1)S(1)} %fusion.26) | copy-start | bytes 18436
  194.2 13.5 %all-to-all-start.10 = ((bf16[32,24,128]{2,1,0:T(8,128)(2,1)}), bf16[32,24,128]{2,1,0:T(8,128)(2,1)S(1)}, u32[]{:S(2)}, u32[]{:S(2)}) async-start(bf16[32,24,128]{2,1,0:T(8,128)(2,1)} %broadcast_in_dim.56), calls=%async_computation.10 | async-start | bytes 393216 | tf_op jit(solution)/shard_map/all_to_all | solution.py:22
  207.7 17.7 %copy-start.41 = (bf16[32,24,128]{2,1,0:T(8,128)(2,1)}, bf16[32,24,128]{2,1,0:T(8,128)(2,1)S(1)}, u32[]{:S(2)}) copy-start(bf16[32,24,128]{2,1,0:T(8,128)(2,1)S(1)} %all-to-all-done.10) | copy-start | bytes 589828
  207.7 16.6 %copy-start.4 = (bf16[1,8,1,16,4096]{4,3,2,1,0:T(8,128)(2,1)S(1)}, bf16[1,8,1,16,4096]{4,3,2,1,0:T(8,128)(2,1)}, u32[]{:S(2)}) copy-start(bf16[1,8,1,16,4096]{4,3,2,1,0:T(8,128)(2,1)} %get-tuple-element.44) | copy-start | bytes 3145732
  209.5 29.0 %copy-start.69 = (bf16[24,128]{1,0:T(8,128)(2,1)}, bf16[24,128]{1,0:T(8,128)(2,1)S(1)}, u32[]{:S(2)}) copy-start(bf16[24,128]{1,0:T(8,128)(2,1)S(1)} %fusion.27) | copy-start | bytes 18436
  209.5 29.0 %copy-start.3 = (bf16[1,8,1,16,4096]{4,3,2,1,0:T(8,128)(2,1)S(1)}, bf16[1,8,1,16,4096]{4,3,2,1,0:T(8,128)(2,1)}, u32[]{:S(2)}) copy-start(bf16[1,8,1,16,4096]{4,3,2,1,0:T(8,128)(2,1)} %get-tuple-element.43) | copy-start | bytes 3145732
  224.3 15.4 %copy-start.43 = (bf16[32,24,128]{2,1,0:T(8,128)(2,1)}, bf16[32,24,128]{2,1,0:T(8,128)(2,1)S(1)}, u32[]{:S(2)}) copy-start(bf16[32,24,128]{2,1,0:T(8,128)(2,1)S(1)} %all_to_all.118) | copy-start | bytes 589828
  225.4 27.8 %copy-start.71 = (bf16[24,128]{1,0:T(8,128)(2,1)}, bf16[24,128]{1,0:T(8,128)(2,1)S(1)}, u32[]{:S(2)}) copy-start(bf16[24,128]{1,0:T(8,128)(2,1)S(1)} %fusion.28) | copy-start | bytes 18436
  225.4 27.8 %copy-start.2 = (bf16[1,8,1,16,4096]{4,3,2,1,0:T(8,128)(2,1)S(1)}, bf16[1,8,1,16,4096]{4,3,2,1,0:T(8,128)(2,1)}, u32[]{:S(2)}) copy-start(bf16[1,8,1,16,4096]{4,3,2,1,0:T(8,128)(2,1)} %get-tuple-element.42) | copy-start | bytes 3145732
  238.5 15.7 %copy-start.45 = (bf16[32,24,128]{2,1,0:T(8,128)(2,1)}, bf16[32,24,128]{2,1,0:T(8,128)(2,1)S(1)}, u32[]{:S(2)}) copy-start(bf16[32,24,128]{2,1,0:T(8,128)(2,1)S(1)} %all_to_all.119) | copy-start | bytes 589828
  239.7 28.3 %copy-start.73 = (bf16[24,128]{1,0:T(8,128)(2,1)}, bf16[24,128]{1,0:T(8,128)(2,1)S(1)}, u32[]{:S(2)}) copy-start(bf16[24,128]{1,0:T(8,128)(2,1)S(1)} %fusion.29) | copy-start | bytes 18436
  239.7 28.3 %copy-start.1 = (bf16[1,8,1,16,4096]{4,3,2,1,0:T(8,128)(2,1)S(1)}, bf16[1,8,1,16,4096]{4,3,2,1,0:T(8,128)(2,1)}, u32[]{:S(2)}) copy-start(bf16[1,8,1,16,4096]{4,3,2,1,0:T(8,128)(2,1)} %get-tuple-element.41) | copy-start | bytes 3145732
  253.1 15.9 %copy-start.47 = (bf16[32,24,128]{2,1,0:T(8,128)(2,1)}, bf16[32,24,128]{2,1,0:T(8,128)(2,1)S(1)}, u32[]{:S(2)}) copy-start(bf16[32,24,128]{2,1,0:T(8,128)(2,1)S(1)} %all_to_all.120) | copy-start | bytes 589828
  254.3 28.8 %copy-start.75 = (bf16[24,128]{1,0:T(8,128)(2,1)}, bf16[24,128]{1,0:T(8,128)(2,1)S(1)}, u32[]{:S(2)}) copy-start(bf16[24,128]{1,0:T(8,128)(2,1)S(1)} %fusion.30) | copy-start | bytes 18436
  268.0 16.2 %copy-start.49 = (bf16[32,24,128]{2,1,0:T(8,128)(2,1)}, bf16[32,24,128]{2,1,0:T(8,128)(2,1)S(1)}, u32[]{:S(2)}) copy-start(bf16[32,24,128]{2,1,0:T(8,128)(2,1)S(1)} %all_to_all.121) | copy-start | bytes 589828
  269.1 28.9 %copy-start.77 = (bf16[24,128]{1,0:T(8,128)(2,1)}, bf16[24,128]{1,0:T(8,128)(2,1)S(1)}, u32[]{:S(2)}) copy-start(bf16[24,128]{1,0:T(8,128)(2,1)S(1)} %fusion.31) | copy-start | bytes 18436
  283.0 16.0 %copy-start.51 = (bf16[32,24,128]{2,1,0:T(8,128)(2,1)}, bf16[32,24,128]{2,1,0:T(8,128)(2,1)S(1)}, u32[]{:S(2)}) copy-start(bf16[32,24,128]{2,1,0:T(8,128)(2,1)S(1)} %all_to_all.122) | copy-start | bytes 589828
  284.1 15.6 %copy-start.79 = (bf16[24,128]{1,0:T(8,128)(2,1)}, bf16[24,128]{1,0:T(8,128)(2,1)S(1)}, u32[]{:S(2)}) copy-start(bf16[24,128]{1,0:T(8,128)(2,1)S(1)} %fusion.32) | copy-start | bytes 18436
  299.1 15.9 %copy-start.81 = (bf16[24,128]{1,0:T(8,128)(2,1)}, bf16[24,128]{1,0:T(8,128)(2,1)S(1)}, u32[]{:S(2)}) copy-start(bf16[24,128]{1,0:T(8,128)(2,1)S(1)} %fusion.33) | copy-start | bytes 18436
  299.8 13.5 %all-to-all-start.17 = ((bf16[32,24,128]{2,1,0:T(8,128)(2,1)}), bf16[32,24,128]{2,1,0:T(8,128)(2,1)S(1)}, u32[]{:S(2)}, u32[]{:S(2)}) async-start(bf16[32,24,128]{2,1,0:T(8,128)(2,1)} %broadcast_in_dim.63), calls=%async_computation.17 | async-start | bytes 393216 | tf_op jit(solution)/shard_map/all_to_all | solution.py:22
  323.2 7.4 %copy-start.9 = (bf16[1,8,1,16,4608]{4,3,2,1,0:T(8,128)(2,1)}, bf16[1,8,1,16,4608]{4,3,2,1,0:T(8,128)(2,1)S(1)}, u32[]{:S(2)}) copy-start(bf16[1,8,1,16,4608]{4,3,2,1,0:T(8,128)(2,1)S(1)} %get-tuple-element.26) | copy-start | bytes 3538948
  323.2 7.5 %copy-start.7 = (bf16[1,8,1,16,4608]{4,3,2,1,0:T(8,128)(2,1)}, bf16[1,8,1,16,4608]{4,3,2,1,0:T(8,128)(2,1)S(1)}, u32[]{:S(2)}) copy-start(bf16[1,8,1,16,4608]{4,3,2,1,0:T(8,128)(2,1)S(1)} %get-tuple-element.25) | copy-start | bytes 3538948
  323.2 7.6 %copy-start.5 = (bf16[1,8,1,16,4608]{4,3,2,1,0:T(8,128)(2,1)}, bf16[1,8,1,16,4608]{4,3,2,1,0:T(8,128)(2,1)S(1)}, u32[]{:S(2)}) copy-start(bf16[1,8,1,16,4608]{4,3,2,1,0:T(8,128)(2,1)S(1)} %get-tuple-element.24) | copy-start | bytes 3538948
  323.3 7.8 %copy-start.11 = (bf16[1,8,1,16,4608]{4,3,2,1,0:T(8,128)(2,1)}, bf16[1,8,1,16,4608]{4,3,2,1,0:T(8,128)(2,1)S(1)}, u32[]{:S(2)}) copy-start(bf16[1,8,1,16,4608]{4,3,2,1,0:T(8,128)(2,1)S(1)} %get-tuple-element.27) | copy-start | bytes 3538948
  323.3 7.8 %copy-start.13 = (bf16[1,8,1,16,4608]{4,3,2,1,0:T(8,128)(2,1)}, bf16[1,8,1,16,4608]{4,3,2,1,0:T(8,128)(2,1)S(1)}, u32[]{:S(2)}) copy-start(bf16[1,8,1,16,4608]{4,3,2,1,0:T(8,128)(2,1)S(1)} %get-tuple-element.28) | copy-start | bytes 3538948
  323.3 7.8 %copy-start.15 = (bf16[1,8,1,16,4608]{4,3,2,1,0:T(8,128)(2,1)}, bf16[1,8,1,16,4608]{4,3,2,1,0:T(8,128)(2,1)S(1)}, u32[]{:S(2)}) copy-start(bf16[1,8,1,16,4608]{4,3,2,1,0:T(8,128)(2,1)S(1)} %get-tuple-element.29) | copy-start | bytes 3538948
  323.3 7.9 %copy-start.17 = (bf16[1,8,1,16,4608]{4,3,2,1,0:T(8,128)(2,1)}, bf16[1,8,1,16,4608]{4,3,2,1,0:T(8,128)(2,1)S(1)}, u32[]{:S(2)}) copy-start(bf16[1,8,1,16,4608]{4,3,2,1,0:T(8,128)(2,1)S(1)} %get-tuple-element.30) | copy-start | bytes 3538948
  323.3 7.9 %copy-start.19 = (bf16[1,8,1,16,4608]{4,3,2,1,0:T(8,128)(2,1)}, bf16[1,8,1,16,4608]{4,3,2,1,0:T(8,128)(2,1)S(1)}, u32[]{:S(2)}) copy-start(bf16[1,8,1,16,4608]{4,3,2,1,0:T(8,128)(2,1)S(1)} %get-tuple-element.31) | copy-start | bytes 3538948
  323.3 7.9 %copy-start.21 = (bf16[1,8,1,16,4608]{4,3,2,1,0:T(8,128)(2,1)}, bf16[1,8,1,16,4608]{4,3,2,1,0:T(8,128)(2,1)S(1)}, u32[]{:S(2)}) copy-start(bf16[1,8,1,16,4608]{4,3,2,1,0:T(8,128)(2,1)S(1)} %get-tuple-element.32) | copy-start | bytes 3538948
  323.3 7.9 %copy-start.23 = (bf16[1,8,1,16,4608]{4,3,2,1,0:T(8,128)(2,1)}, bf16[1,8,1,16,4608]{4,3,2,1,0:T(8,128)(2,1)S(1)}, u32[]{:S(2)}) copy-start(bf16[1,8,1,16,4608]{4,3,2,1,0:T(8,128)(2,1)S(1)} %get-tuple-element.33) | copy-start | bytes 3538948
  323.3 7.9 %copy-start.25 = (bf16[1,8,1,16,4608]{4,3,2,1,0:T(8,128)(2,1)}, bf16[1,8,1,16,4608]{4,3,2,1,0:T(8,128)(2,1)S(1)}, u32[]{:S(2)}) copy-start(bf16[1,8,1,16,4608]{4,3,2,1,0:T(8,128)(2,1)S(1)} %get-tuple-element.34) | copy-start | bytes 3538948
  323.3 7.9 %copy-start.27 = (bf16[1,8,1,16,4608]{4,3,2,1,0:T(8,128)(2,1)}, bf16[1,8,1,16,4608]{4,3,2,1,0:T(8,128)(2,1)S(1)}, u32[]{:S(2)}) copy-start(bf16[1,8,1,16,4608]{4,3,2,1,0:T(8,128)(2,1)S(1)} %get-tuple-element.35) | copy-start | bytes 3538948
  323.4 11.9 %copy-start.28 = (bf16[1,8,1,16,4608]{4,3,2,1,0:T(8,128)(2,1)}, bf16[1,8,1,16,4608]{4,3,2,1,0:T(8,128)(2,1)S(1)}, u32[]{:S(2)}) copy-start(bf16[1,8,1,16,4608]{4,3,2,1,0:T(8,128)(2,1)S(1)} %get-tuple-element.36) | copy-start | bytes 3538948
  323.4 6.1 %copy-start.60 = (bf16[24,128]{1,0:T(8,128)(2,1)S(1)}, bf16[24,128]{1,0:T(8,128)(2,1)}, u32[]{:S(2)}) copy-start(bf16[24,128]{1,0:T(8,128)(2,1)} %copy-done.59) | copy-start | bytes 18436
  323.4 6.2 %copy-start.62 = (bf16[24,128]{1,0:T(8,128)(2,1)S(1)}, bf16[24,128]{1,0:T(8,128)(2,1)}, u32[]{:S(2)}) copy-start(bf16[24,128]{1,0:T(8,128)(2,1)} %copy-done.61) | copy-start | bytes 18436
  323.4 6.4 %copy-start.64 = (bf16[24,128]{1,0:T(8,128)(2,1)S(1)}, bf16[24,128]{1,0:T(8,128)(2,1)}, u32[]{:S(2)}) copy-start(bf16[24,128]{1,0:T(8,128)(2,1)} %copy-done.63) | copy-start | bytes 18436
  323.4 6.5 %copy-start.66 = (bf16[24,128]{1,0:T(8,128)(2,1)S(1)}, bf16[24,128]{1,0:T(8,128)(2,1)}, u32[]{:S(2)}) copy-start(bf16[24,128]{1,0:T(8,128)(2,1)} %copy-done.65) | copy-start | bytes 18436
  323.4 6.6 %copy-start.68 = (bf16[24,128]{1,0:T(8,128)(2,1)S(1)}, bf16[24,128]{1,0:T(8,128)(2,1)}, u32[]{:S(2)}) copy-start(bf16[24,128]{1,0:T(8,128)(2,1)} %copy-done.67) | copy-start | bytes 18436
  327.8 2.5 copy-start.72
  327.8 2.7 copy-start.74
  335.2 21.0 %all-to-all-start.18 = ((f32[32,27,128]{2,1,0:T(8,128)}), f32[32,27,128]{2,1,0:T(8,128)S(1)}, u32[]{:S(2)}, u32[]{:S(2)}) async-start(f32[32,27,128]{2,1,0:T(8,128)} %pad_maximum_fusion.2), calls=%async_computation.18 | async-start | bytes 1048576 | tf_op jit(solution)/shard_map/all_to_all | solution.py:113
  339.3 4.8 %copy-start.26 = (bf16[1,8,1,16,4608]{4,3,2,1,0:T(8,128)(2,1)S(1)}, bf16[1,8,1,16,4608]{4,3,2,1,0:T(8,128)(2,1)}, u32[]{:S(2)}) copy-start(bf16[1,8,1,16,4608]{4,3,2,1,0:T(8,128)(2,1)} %copy-done.25) | copy-start | bytes 3538948
  339.3 4.8 %copy-start.34 = (bf16[32,24,128]{2,1,0:T(8,128)(2,1)S(1)}, bf16[32,24,128]{2,1,0:T(8,128)(2,1)}, u32[]{:S(2)}) copy-start(bf16[32,24,128]{2,1,0:T(8,128)(2,1)} %copy-done.33) | copy-start | bytes 589828
  341.8 3.4 copy-start.24
  341.8 3.4 copy-start.36
  357.6 17.6 %all-to-all-start.19 = ((bf16[32,3,128]{2,1,0:T(4,128)(2,1)}), bf16[32,3,128]{2,1,0:T(4,128)(2,1)S(1)}, u32[]{:S(2)}, u32[]{:S(2)}) async-start(bf16[32,3,128]{2,1,0:T(4,128)(2,1)} %broadcast_in_dim.65), calls=%async_computation.19 | async-start | bytes 65536 | tf_op jit(solution)/shard_map/all_to_all | solution.py:22
  414.5 5.0 %copy-start.57 = (bf16[512,512]{1,0:T(8,128)(2,1)S(1)}, bf16[512,512]{1,0:T(8,128)(2,1)}, u32[]{:S(2)}) copy-start(bf16[512,512]{1,0:T(8,128)(2,1)} %param.13) | copy-start | bytes 1572868
  416.1 8.6 %all-to-all-start.21 = ((bf16[8,384,16]{1,2,0:T(8,128)(2,1)}), bf16[8,384,16]{1,2,0:T(8,128)(2,1)S(1)}, u32[]{:S(2)}, u32[]{:S(2)}) async-start(bf16[8,384,16]{1,2,0:T(8,128)(2,1)} %bitcast.111), calls=%async_computation.21 | async-start | bytes 196608 | tf_op jit(solution)/shard_map/all_to_all | solution.py:132
  (31 other events, 53.9 us)
Sparse Core Ops, SparseCore 0:
  35.0 52.4 all-gather.8
  89.5 43.7 all-gather.12
  136.0 57.4 all-gather.14
  195.5 106.7 all-gather.10

commit v7 on v6

--- a/solution.py
+++ b/solution.py
@@ -2,6 +2,7 @@
 import jax.numpy as jnp
 import numpy as np
 from jax import lax
+from jax.experimental.layout import Layout, with_layout_constraint
 from jax.sharding import Mesh
 from jax.sharding import PartitionSpec as P
 
@@ -62,9 +63,10 @@
     initial = jnp.zeros((8, node_count), jnp.bfloat16)
     entering = jnp.where(lax.axis_index(DEAL + ("c",)) == 0, product(masked, initial)[:, :1], 0.0)
     forcing = (rhs_nodes[0].T.astype(jnp.float32) - entering).astype(jnp.bfloat16)
-    rows = jnp.concatenate([reorder(masked), forcing], 1)
+    rows = jnp.concatenate([reorder(masked), forcing, arrow_factor[0].T], 1)
     rows = lax.all_to_all(rows.reshape(deal, piece, -1), DEAL, 0, 0)
-    forcing = rows[:, :, node_count:].reshape(deal * piece, copies, width).transpose(1, 0, 2)
+    forcing = rows[:, :, node_count : node_count + rhs_count].reshape(deal * piece, copies, width).transpose(1, 0, 2)
+    arrows = rows[:, :, node_count + rhs_count :].transpose(1, 0, 2).reshape(1, piece, deal * arrow_count)
     first, second, third = jnp.split(rows[:, :, :node_count], np.cumsum(CHUNKS)[:-1])
     links = [lax.all_gather(first, COPY, axis=0)]
     forcing = lax.all_to_all(forcing, COPY, 0, 0).reshape(cores, lower, deal, piece, width)
@@ -72,10 +74,8 @@
     previous = spread(forcing[0], CHAIN)
     second, previous = lax.optimization_barrier((second, previous))
     links.append(lax.all_gather(second, COPY, axis=0))
-    out_rows = jnp.concatenate([reorder(pivot_inverse[0]), arrow_factor[0].T], 1)
-    out_rows = lax.all_to_all(out_rows.reshape(deal, piece, -1), DEAL, 0, 0)
-    third, out_rows = lax.optimization_barrier((third, out_rows))
-    links.append(lax.all_gather(third, COPY, axis=0))
+    third = jnp.concatenate([third, arrows], 0)
+    out_rows = with_layout_constraint(reorder(pivot_inverse[0]), Layout((0, 1)))
 
     def of_step(held, pair, core):
         return held.reshape(cores, lower, *held.shape[1:])[core, :, pair].reshape(local_rows, -1)
@@ -91,36 +91,55 @@
         return gathered.transpose(1, 0, 2).reshape(width, node_count)
 
     parts = [forcing[0]]
-    history = [whole(previous)]
+    history = [previous]
     for step in range(1, steps):
-        linked = product(history[-1], link_rows(step))
+        linked = product(whole(history[-1]), link_rows(step))
         fresh = (forcing[step].astype(jnp.float32) - linked).astype(jnp.bfloat16)
+        if step == 1:
+            fresh, third, out_rows = lax.optimization_barrier((fresh, third, out_rows))
+            links.append(lax.all_gather(third, COPY, axis=0))
         if step == OUT_AFTER:
             fresh, out_rows = lax.optimization_barrier((fresh, out_rows))
             out_rows = lax.all_gather(out_rows, COPY, axis=0)
+        if step == steps - 3:
+            fresh, *parts = lax.optimization_barrier((fresh, *parts))
+        if step == steps - 2:
+            fresh, *history = lax.optimization_barrier((fresh, *history))
+        if step == steps - 1:
+            fresh, out_rows = lax.optimization_barrier((fresh, out_rows))
         parts.append(fresh)
         if step < steps - 1:
-            history.append(whole(spread(fresh, CHAIN)))
+            history.append(spread(fresh, CHAIN))
 
-    held = [of_step(out_rows, step // cores, step % cores) for step in range(steps)]
     terms = jnp.zeros((width, arrow_count), jnp.float32)
     for step in range(steps):
-        terms = terms + jnp.dot(parts[step], held[step][:, node_count:], preferred_element_type=jnp.float32)
+        pair, core = step // cores, step % cores
+        columns = slice(pair * arrow_count, (pair + 1) * arrow_count)
+        held = of_step(links[-1], CHUNKS[-1], core)[:, columns]
+        terms = terms + jnp.dot(parts[step], held, preferred_element_type=jnp.float32)
     tiles = arrow_count // TILE
     share = width // (group // tiles)
     terms = terms.reshape(group // tiles, share, tiles, TILE).transpose(0, 2, 1, 3).reshape(group, share, TILE)
     last = jnp.broadcast_to(parts[-1].astype(jnp.float32), (group, width, local_rows))
     arrived = lax.all_to_all(jnp.concatenate([last, terms], 1), CHAIN, 0, 0)
-    history.append(whole(arrived[:, :width].astype(jnp.bfloat16)))
+    history.append(arrived[:, :width].astype(jnp.bfloat16))
     place = lax.axis_index(CHAIN)
     corner = (mine * width + place // tiles * share, place % tiles * TILE)
     own = lax.dynamic_slice(rhs_arrow, corner, (share, TILE))
-    rest = spread((own - jnp.sum(arrived[:, width:], 0)).astype(jnp.bfloat16), CHAIN)
+    rest = (own - jnp.sum(arrived[:, width:], 0)).astype(jnp.bfloat16)
+    rest, history[-1] = lax.optimization_barrier((rest, history[-1]))
+    rest = spread(rest, CHAIN)
     rest = rest.reshape(group // tiles, tiles, share, TILE).transpose(1, 0, 2, 3).reshape(1, tiles * width, TILE)
-    solved = [product(history[step], held[step][:, :node_count]).astype(jnp.bfloat16) for step in range(steps)]
-
-    solved = jnp.stack(solved).reshape(deal, cores, width, lower, piece)
-    solved = solved.transpose(1, 3, 2, 0, 4).reshape(copies, width, deal * piece)
+    pair = lax.axis_index(DEAL)
+    solved = []
+    for core in range(cores):
+        chosen = history[core]
+        for other in range(1, deal):
+            chosen = jnp.where(pair == other, history[other * cores + core], chosen)
+        held = out_rows[core * lower : (core + 1) * lower].reshape(lower * local_rows, node_count)
+        result = product(whole(chosen), held).astype(jnp.bfloat16)
+        solved.append(result.reshape(width, lower, local_rows).transpose(1, 0, 2))
+    solved = jnp.concatenate(solved, 0)
     sent = jnp.concatenate([solved, jnp.broadcast_to(rest, (copies, tiles * width, TILE))], 1)
     arrived = lax.all_to_all(sent, COPY, 0, 0)
     rest = arrived[:, width:].reshape(copies, tiles, width, TILE)
@@ -128,9 +147,7 @@
         product(rest[:, part].reshape(rhs_count, TILE), tip_inverse[:, part * TILE : (part + 1) * TILE])
         for part in range(tiles)
     )
-    solved = arrived[:, :width].reshape(rhs_count, deal, piece).transpose(1, 0, 2)
-    solved = lax.all_to_all(solved, DEAL, 0, 0)
-    solved = solved.transpose(1, 0, 2).reshape(1, rhs_count, local_rows)
+    solved = arrived[:, :width].reshape(1, rhs_count, local_rows)
     return (solved, arrow_solved)
 
 

time: 435 us -> 419 us (0.963)
  blocking collectives: 251 us -> 223 us
  starting transfers between devices: 31.9 us -> 41.2 us
  waiting for transfers between devices: 39.6 us -> 45.3 us
    all_to_all x12 -> x10, blocking collectives: 171 us -> 153 us  [spread(): return lax.all_to_all(copies, axis, 0, 0)]
    all_to_all x4 -> x6, starting transfers between devices: 20.7 us -> 36.9 us  [spread(): return lax.all_to_all(copies, axis, 0, 0)]
    all_to_all x2 -> x0, waiting for transfers between devices: 14.7 us -> none  [the longest x1 11.5 us: per_device(): out_rows = lax.all_to_all(out_rows.reshape(deal, piece, -1), DEAL, 0, 0)]
    all_to_all x1, blocking collectives: 39 us -> 27.9 us  [per_device(): arrived = lax.all_to_all(sent, COPY, 0, 0)]
    dot_general x36 -> x22, matrix products: 38.3 us -> 28.2 us  [product(): lax.dot_general(left, right, CONTRACT, preferred_element_type=jnp.float32)]
    slice x3 -> x4, local copies, waits for them, and re-layouts: 0.45 us -> 10.2 us  [the longest x1 9.47 us: per_device(): out_rows[core * lower:(core + 1) * lower]]
    all_gather x1, waiting for transfers between devices: 0.02 us -> 8.74 us  [per_device(): links.append(lax.all_gather(third, COPY, axis=0))]
    dot_general x16, matrix products: 4.05 us -> 12.7 us  [per_device(): jnp.dot(parts[step], held, preferred_element_type=jnp.float32)]
  transfers between devices with their start and end apart: 11 -> 11, of which waited for: 6 -> 7; matrix products, arithmetic and copies ran while one was open for 14% -> 16% of each run, Pallas kernels for 0% -> 0%
where the time goes in v7:
time: 419 us; the launch traced here: 417 us
  blocking collectives  223 us (53%)
  waiting for transfers between devices  45.3 us (11%)
  local copies, waits for them, and re-layouts  44.7 us (11%)
  matrix products  44 us (11%)
  starting transfers between devices  41.2 us (10%)
  between operations  14.7 us (4%)
    all_to_all x10, blocking collectives, spread(): return lax.all_to_all(copies, axis, 0, 0)  153 us
    all_to_all x6, starting transfers between devices, spread(): return lax.all_to_all(copies, axis, 0, 0)  36.9 us
    all_to_all x6, waiting for transfers between devices, spread(): return lax.all_to_all(copies, axis, 0, 0)  28.4 us
    dot_general x22, matrix products, product(): lax.dot_general(left, right, CONTRACT, preferred_element_type=jnp.float32)  28.2 us
    all_to_all x1, blocking collectives, per_device(): arrived = lax.all_to_all(sent, COPY, 0, 0)  27.9 us
    all_to_all x1, blocking collectives, per_device(): lax.all_to_all(forcing, COPY, 0, 0)  22.7 us
    all_to_all x1, blocking collectives, per_device(): rows = lax.all_to_all(rows.reshape(deal, piece, -1), DEAL, 0, 0)  19.8 us
    slice x3, local copies, waits for them, and re-layouts, of_step(): held.reshape(cores, lower, *held.shape[1:])[core, :, pair]  12.8 us
  transfers between devices with their start and end apart: 11, of which 7 were waited for; matrix products, arithmetic and copies ran while one was open for 16% of the time, Pallas kernels for 0%

profile of v7, /device:TPU:1, one launch (start us, length us, event | category | flops | bytes accessed | tf_op | source)
XLA Modules:
  0.0 417.0 jit_solution(6303285219339500212)
XLA Ops:
  8.9 1.0 copy.69
  9.9 1.0 copy.70
  10.9 1.5 copy.121
  12.4 1.6 fusion.10
  14.1 1.0 copy.68
  16.5 19.8 %all_to_all.100 = bf16[8,16,4992]{2,1,0:T(8,128)(2,1)S(1)} all-to-all(bf16[8,16,4992]{2,1,0:T(8,128)(2,1)S(1)} %pad_maximum_fusion), channel_id=1, replica_groups=mesh['yl'=2,'x'=4,'c'=2,'yh'=4,'z'=8] {'yl','x'}, dimensions={0} | all-to-all | bytes 2555904 | tf_op jit(solution)/shard_map/all_to_all | solution.py:67
  36.2 0.8 fusion.100
  38.3 22.7 %all_to_all.101 = bf16[16,128,24]{1,2,0:T(8,128)(2,1)S(1)} all-to-all(bf16[16,128,24]{1,2,0:T(8,128)(2,1)S(1)} %copy.71), channel_id=1, replica_groups=mesh['yl'=2,'x'=4,'c'=2,'yh'=4,'z'=8] {'c','z'}, dimensions={0} | all-to-all | bytes 196608 | tf_op jit(solution)/shard_map/all_to_all | solution.py:72
  62.6 16.0 %all_to_all.102 = bf16[32,24,128]{2,1,0:T(8,128)(2,1)S(1)} all-to-all(bf16[32,24,128]{2,1,0:T(8,128)(2,1)S(1)} %broadcast_in_dim.49), channel_id=1, replica_groups=mesh['yl'=2,'x'=4,'c'=2,'yh'=4,'z'=8] {'yl','x','yh'}, dimensions={0} | all-to-all | bytes 393216 | tf_op jit(solution)/shard_map/all_to_all | solution.py:23
  78.7 1.5 copy.122
  80.2 1.5 fusion.11
  82.5 1.6 reshape.285
  84.3 0.9 pad_maximum_fusion.1
  85.2 4.3 %all-gather.9.cloned.1.call-done = bf16[32,16,4096]{2,1,0:T(8,128)(2,1)} async-done(((bf16[2,16,4096]{2,1,0:T(8,128)(2,1)}), bf16[32,16,4096]{2,1,0:T(8,128)(2,1)}) %all-gather.9.cloned.1.call-update) | async-done | bytes 4194320 | tf_op jit(solution)/shard_map/all_gather | solution.py:71
  89.5 2.1 fusion.98
  92.1 18.9 %all_to_all.103 = bf16[32,24,128]{2,1,0:T(8,128)(2,1)S(1)} all-to-all(bf16[32,24,128]{2,1,0:T(8,128)(2,1)S(1)} %broadcast_in_dim.50), channel_id=1, replica_groups=mesh['yl'=2,'x'=4,'c'=2,'yh'=4,'z'=8] {'yl','x','yh'}, dimensions={0} | all-to-all | bytes 393216 | tf_op jit(solution)/shard_map/all_to_all | solution.py:23
  111.4 14.3 %all_to_all.104 = bf16[32,24,128]{2,1,0:T(8,128)(2,1)S(1)} all-to-all(bf16[32,24,128]{2,1,0:T(8,128)(2,1)S(1)} %broadcast_in_dim.51), channel_id=1, replica_groups=mesh['yl'=2,'x'=4,'c'=2,'yh'=4,'z'=8] {'yl','x','yh'}, dimensions={0} | all-to-all | bytes 393216 | tf_op jit(solution)/shard_map/all_to_all | solution.py:23
  126.8 4.8 %all-to-all-start.5 = ((bf16[32,24,128]{2,1,0:T(8,128)(2,1)}), bf16[32,24,128]{2,1,0:T(8,128)(2,1)}, u32[]{:S(2)}, u32[]{:S(2)}) async-start(bf16[32,24,128]{2,1,0:T(8,128)(2,1)} %broadcast_in_dim.52), calls=%async_computation.5 | async-start | bytes 393216 | tf_op jit(solution)/shard_map/all_to_all | solution.py:23
  131.6 3.8 all-gather.11.cloned.1.call-done
  135.4 3.5 fusion.99
  138.9 2.3 all-to-all-done.5
  141.2 1.6 fusion.19
  143.5 16.5 %all_to_all.105 = bf16[32,24,128]{2,1,0:T(8,128)(2,1)S(1)} all-to-all(bf16[32,24,128]{2,1,0:T(8,128)(2,1)S(1)} %broadcast_in_dim.53), channel_id=1, replica_groups=mesh['yl'=2,'x'=4,'c'=2,'yh'=4,'z'=8] {'yl','x','yh'}, dimensions={0} | all-to-all | bytes 393216 | tf_op jit(solution)/shard_map/all_to_all | solution.py:23
  159.9 1.1 fusion.20
  161.1 14.2 %all_to_all.106 = bf16[32,24,128]{2,1,0:T(8,128)(2,1)S(1)} all-to-all(bf16[32,24,128]{2,1,0:T(8,128)(2,1)S(1)} %broadcast_in_dim.54), channel_id=1, replica_groups=mesh['yl'=2,'x'=4,'c'=2,'yh'=4,'z'=8] {'yl','x','yh'}, dimensions={0} | all-to-all | bytes 393216 | tf_op jit(solution)/shard_map/all_to_all | solution.py:23
  175.2 1.1 fusion.21
  177.0 13.3 %all_to_all.107 = bf16[32,24,128]{2,1,0:T(8,128)(2,1)S(1)} all-to-all(bf16[32,24,128]{2,1,0:T(8,128)(2,1)S(1)} %broadcast_in_dim.55), channel_id=1, replica_groups=mesh['yl'=2,'x'=4,'c'=2,'yh'=4,'z'=8] {'yl','x','yh'}, dimensions={0} | all-to-all | bytes 393216 | tf_op jit(solution)/shard_map/all_to_all | solution.py:23
  190.3 1.1 fusion.22
  192.1 4.6 %all-to-all-start.9 = ((bf16[32,24,128]{2,1,0:T(8,128)(2,1)}), bf16[32,24,128]{2,1,0:T(8,128)(2,1)}, u32[]{:S(2)}, u32[]{:S(2)}) async-start(bf16[32,24,128]{2,1,0:T(8,128)(2,1)} %broadcast_in_dim.56), calls=%async_computation.9 | async-start | bytes 393216 | tf_op jit(solution)/shard_map/all_to_all | solution.py:23
  196.6 8.7 %all-gather.13.cloned.1.call-done = bf16[80,16,4096]{2,1,0:T(8,128)(2,1)} async-done(((bf16[5,16,4096]{2,1,0:T(8,128)(2,1)}), bf16[80,16,4096]{2,1,0:T(8,128)(2,1)}) %all-gather.13.cloned.1.call-update) | async-done | bytes 10485776 | tf_op jit(solution)/shard_map/all_gather | solution.py:100
  205.4 7.2 %fusion.97 = (bf16[1,8,1,16,4096]{4,3,2,1,0:T(8,128)(2,1)S(1)}, bf16[1,8,1,16,4096]{4,3,2,1,0:T(8,128)(2,1)S(1)}, bf16[1,8,1,16,4096]{4,3,2,1,0:T(8,128)(2,1)S(1...) fusion(bf16[2,8,5,16,4096]{4,3,2,1,0:T(8,128)(2,1)} %bitcast.372), kind=kLoop, calls=%fused_computation.168 | loop fusion | bytes 20971520 | tf_op jit(solution)/shard_map/slice | solution.py:81
  212.6 1.8 fusion.23
  215.1 18.9 %all_to_all.108 = bf16[32,24,128]{2,1,0:T(8,128)(2,1)S(1)} all-to-all(bf16[32,24,128]{2,1,0:T(8,128)(2,1)S(1)} %broadcast_in_dim.57), channel_id=1, replica_groups=mesh['yl'=2,'x'=4,'c'=2,'yh'=4,'z'=8] {'yl','x','yh'}, dimensions={0} | all-to-all | bytes 393216 | tf_op jit(solution)/shard_map/all_to_all | solution.py:23
  233.9 1.7 fusion.24
  235.7 14.3 %all_to_all.109 = bf16[32,24,128]{2,1,0:T(8,128)(2,1)S(1)} all-to-all(bf16[32,24,128]{2,1,0:T(8,128)(2,1)S(1)} %broadcast_in_dim.58), channel_id=1, replica_groups=mesh['yl'=2,'x'=4,'c'=2,'yh'=4,'z'=8] {'yl','x','yh'}, dimensions={0} | all-to-all | bytes 393216 | tf_op jit(solution)/shard_map/all_to_all | solution.py:23
  250.0 1.7 fusion.25
  252.3 13.2 %all_to_all.110 = bf16[32,24,128]{2,1,0:T(8,128)(2,1)S(1)} all-to-all(bf16[32,24,128]{2,1,0:T(8,128)(2,1)S(1)} %broadcast_in_dim.59), channel_id=1, replica_groups=mesh['yl'=2,'x'=4,'c'=2,'yh'=4,'z'=8] {'yl','x','yh'}, dimensions={0} | all-to-all | bytes 393216 | tf_op jit(solution)/shard_map/all_to_all | solution.py:23
  265.5 1.1 fusion.26
  266.6 13.2 %all_to_all.111 = bf16[32,24,128]{2,1,0:T(8,128)(2,1)S(1)} all-to-all(bf16[32,24,128]{2,1,0:T(8,128)(2,1)S(1)} %broadcast_in_dim.60), channel_id=1, replica_groups=mesh['yl'=2,'x'=4,'c'=2,'yh'=4,'z'=8] {'yl','x','yh'}, dimensions={0} | all-to-all | bytes 393216 | tf_op jit(solution)/shard_map/all_to_all | solution.py:23
  279.8 1.1 fusion.27
  282.2 4.6 %all-to-all-start.14 = ((bf16[32,24,128]{2,1,0:T(8,128)(2,1)}), bf16[32,24,128]{2,1,0:T(8,128)(2,1)}, u32[]{:S(2)}, u32[]{:S(2)}) async-start(bf16[32,24,128]{2,1,0:T(8,128)(2,1)} %broadcast_in_dim.61), calls=%async_computation.14 | async-start | bytes 393216 | tf_op jit(solution)/shard_map/all_to_all | solution.py:23
  286.9 9.6 %all-to-all-done.14 = bf16[32,24,128]{2,1,0:T(8,128)(2,1)} async-done(((bf16[32,24,128]{2,1,0:T(8,128)(2,1)}), bf16[32,24,128]{2,1,0:T(8,128)(2,1)}, u32[]{:S(2)}, u32[]{:S(2)}) %all-to-all-start.14) | async-done | bytes 196640 | tf_op jit(solution)/shard_map/all_to_all | solution.py:23
  296.5 1.7 fusion.28
  299.5 4.6 %all-to-all-start.15 = ((bf16[32,24,128]{2,1,0:T(8,128)(2,1)}), bf16[32,24,128]{2,1,0:T(8,128)(2,1)}, u32[]{:S(2)}, u32[]{:S(2)}) async-start(bf16[32,24,128]{2,1,0:T(8,128)(2,1)} %broadcast_in_dim.62), calls=%async_computation.15 | async-start | bytes 393216 | tf_op jit(solution)/shard_map/all_to_all | solution.py:23
  305.1 0.8 convolution_add_fusion.15
  306.0 0.8 convolution_add_fusion.14
  306.8 0.8 convolution_add_fusion.13
  307.6 0.8 convolution_add_fusion.12
  312.6 1.5 convolution_add_fusion.6
  314.1 1.6 fusion.29
  316.4 9.2 %all-to-all-start.16 = ((bf16[32,24,128]{2,1,0:T(8,128)(2,1)}), bf16[32,24,128]{2,1,0:T(8,128)(2,1)}, u32[]{:S(2)}, u32[]{:S(2)}) async-start(bf16[32,24,128]{2,1,0:T(8,128)(2,1)} %broadcast_in_dim.63), calls=%async_computation.16 | async-start | bytes 393216 | tf_op jit(solution)/shard_map/all_to_all | solution.py:23
  325.7 0.9 convolution_add_fusion.5
  327.4 7.9 %all-to-all-done.16 = bf16[32,24,128]{2,1,0:T(8,128)(2,1)} async-done(((bf16[32,24,128]{2,1,0:T(8,128)(2,1)}), bf16[32,24,128]{2,1,0:T(8,128)(2,1)}, u32[]{:S(2)}, u32[]{:S(2)}) %all-to-all-start.16) | async-done | bytes 196640 | tf_op jit(solution)/shard_map/all_to_all | solution.py:23
  335.3 1.3 fusion.30
  336.6 0.9 convolution_add_fusion.3
  337.7 0.8 pad_maximum_fusion.2
  338.5 4.1 all-to-all-start.17
  342.7 9.5 %fusion.96 = (bf16[8,128,4096]{2,1,0:T(8,128)(2,1)S(1)}, bf16[8,128,4096]{2,1,0:T(8,128)(2,1)}) fusion(bf16[16,128,4096]{2,1,0:T(8,128)(2,1)} %bitcast.371), kind=kLoop, calls=%fused_computation.167 | loop fusion | bytes 33554432 | tf_op jit(solution)/shard_map/slice | solution.py:139
  352.2 2.3 fusion.14
  355.5 5.7 %fusion.15 = bf16[3,8,8,128]{3,1,2,0:T(8,128)(2,1)S(1)} fusion(bf16[1024,4096]{1,0:T(8,128)(2,1)} %bitcast.369, bf16[32,24,128]{2,1,0:T(8,128)(2,1)S(1)} %slice.434, bf16[32,24,128]{2,1,0:T(8,128)(2,1)} %all-to-all-done.15, bf16[32,24,128]{2,1,0:T(8,128)(2,1)S(1)} %copy-done.13, bf16[32,24,128]{2,1,0:T(8,128)(2,1)S(1)} %copy-done.11, ...), kind=kOutput, calls=%fused_computation.20 | convolution fusion | flops 202039296 | bytes 10010631 | tf_op jit(solution)/shard_map/dot_general | solution.py:33
  361.8 9.2 %all-to-all-start.18 = ((bf16[32,3,128]{2,1,0:T(4,128)(2,1)}), bf16[32,3,128]{2,1,0:T(4,128)(2,1)S(1)}, u32[]{:S(2)}, u32[]{:S(2)}) async-start(bf16[32,3,128]{2,1,0:T(4,128)(2,1)} %broadcast_in_dim.65), calls=%async_computation.18 | async-start | bytes 65536 | tf_op jit(solution)/shard_map/all_to_all | solution.py:23
  371.2 8.6 %all-to-all-done.18 = bf16[32,3,128]{2,1,0:T(4,128)(2,1)S(1)} async-done(((bf16[32,3,128]{2,1,0:T(4,128)(2,1)}), bf16[32,3,128]{2,1,0:T(4,128)(2,1)S(1)}, u32[]{:S(2)}, u32[]{:S(2)}) %all-to-all-start.18) | async-done | bytes 24608 | tf_op jit(solution)/shard_map/all_to_all | solution.py:23
  379.9 27.9 %all_to_all.112 = bf16[16,120,128]{2,1,0:T(8,128)(2,1)S(1)} all-to-all(bf16[16,120,128]{2,1,0:T(8,128)(2,1)S(1)} %pad_maximum_fusion.3), channel_id=1, replica_groups=mesh['yl'=2,'x'=4,'c'=2,'yh'=4,'z'=8] {'c','z'}, dimensions={0} | all-to-all | bytes 983040 | tf_op jit(solution)/shard_map/all_to_all | solution.py:144
  408.7 1.1 convolution_add_fusion
  (155 shorter events, 25.1 us)
Async XLA Ops:
  7.2 82.3 %all-gather.9.cloned.1.call-start = ((), (), s32[]{:S(2)}) async-start(), calls=%async_computation.20 | async-start | bytes 4456448 | tf_op jit(solution)/shard_map/all_gather | solution.py:71
  12.4 3.5 copy-start.18
  37.1 98.3 %all-gather.11.cloned.1.call-start = ((), (), s32[]{:S(2)}) async-start(), calls=%async_computation.21 | async-start | bytes 4456448 | tf_op jit(solution)/shard_map/all_gather | solution.py:76
  62.5 63.2 %copy-start.20 = (bf16[16,24,128]{2,1,0:T(8,128)(2,1)}, bf16[16,24,128]{2,1,0:T(8,128)(2,1)S(1)}, u32[]{:S(2)}) copy-start(bf16[16,24,128]{2,1,0:T(8,128)(2,1)S(1)} %reshape.281) | copy-start | bytes 294916
  62.5 16.2 %copy-start.33 = (bf16[24,128]{1,0:T(8,128)(2,1)}, bf16[24,128]{1,0:T(8,128)(2,1)S(1)}, u32[]{:S(2)}) copy-start(bf16[24,128]{1,0:T(8,128)(2,1)S(1)} %slice_bitcast_fusion.2) | copy-start | bytes 18436
  78.6 126.8 %all-gather.13.cloned.1.call-start = ((), (), s32[]{:S(2)}) async-start(), calls=%async_computation.22 | async-start | bytes 11141120 | tf_op jit(solution)/shard_map/all_gather | solution.py:100
  92.0 244.6 %all-gather.15.cloned.1.call-start = ((), (), s32[]{:S(2)}) async-start(), calls=%async_computation.23 | async-start | bytes 17825792 | tf_op jit(solution)/shard_map/all_gather | solution.py:103
  125.7 9.7 %copy-start.2 = (bf16[32,24,128]{2,1,0:T(8,128)(2,1)}, bf16[32,24,128]{2,1,0:T(8,128)(2,1)S(1)}, u32[]{:S(2)}) copy-start(bf16[32,24,128]{2,1,0:T(8,128)(2,1)S(1)} %all_to_all.104) | copy-start | bytes 589828
  126.1 9.3 %copy-start.21 = (bf16[24,128]{1,0:T(8,128)(2,1)}, bf16[24,128]{1,0:T(8,128)(2,1)S(1)}, u32[]{:S(2)}) copy-start(bf16[24,128]{1,0:T(8,128)(2,1)S(1)} %fusion.18) | copy-start | bytes 18436
  126.8 14.4 %all-to-all-start.5 = ((bf16[32,24,128]{2,1,0:T(8,128)(2,1)}), bf16[32,24,128]{2,1,0:T(8,128)(2,1)}, u32[]{:S(2)}, u32[]{:S(2)}) async-start(bf16[32,24,128]{2,1,0:T(8,128)(2,1)} %broadcast_in_dim.52), calls=%async_computation.5 | async-start | bytes 393216 | tf_op jit(solution)/shard_map/all_to_all | solution.py:23
  142.8 0.6 copy-start.22
  159.9 31.4 %copy-start.6 = (bf16[32,24,128]{2,1,0:T(8,128)(2,1)}, bf16[32,24,128]{2,1,0:T(8,128)(2,1)S(1)}, u32[]{:S(2)}) copy-start(bf16[32,24,128]{2,1,0:T(8,128)(2,1)S(1)} %all_to_all.105) | copy-start | bytes 589828
  161.0 30.3 %copy-start.23 = (bf16[24,128]{1,0:T(8,128)(2,1)}, bf16[24,128]{1,0:T(8,128)(2,1)S(1)}, u32[]{:S(2)}) copy-start(bf16[24,128]{1,0:T(8,128)(2,1)S(1)} %fusion.20) | copy-start | bytes 18436
  175.2 30.1 %copy-start.4 = (bf16[32,24,128]{2,1,0:T(8,128)(2,1)}, bf16[32,24,128]{2,1,0:T(8,128)(2,1)S(1)}, u32[]{:S(2)}) copy-start(bf16[32,24,128]{2,1,0:T(8,128)(2,1)S(1)} %all_to_all.106) | copy-start | bytes 589828
  176.3 0.6 copy-start.24
  190.3 15.1 %copy-start.8 = (bf16[32,24,128]{2,1,0:T(8,128)(2,1)}, bf16[32,24,128]{2,1,0:T(8,128)(2,1)S(1)}, u32[]{:S(2)}) copy-start(bf16[32,24,128]{2,1,0:T(8,128)(2,1)S(1)} %all_to_all.107) | copy-start | bytes 589828
  191.4 14.0 %copy-start.25 = (bf16[24,128]{1,0:T(8,128)(2,1)}, bf16[24,128]{1,0:T(8,128)(2,1)S(1)}, u32[]{:S(2)}) copy-start(bf16[24,128]{1,0:T(8,128)(2,1)S(1)} %fusion.22) | copy-start | bytes 18436
  192.1 20.6 %all-to-all-start.9 = ((bf16[32,24,128]{2,1,0:T(8,128)(2,1)}), bf16[32,24,128]{2,1,0:T(8,128)(2,1)}, u32[]{:S(2)}, u32[]{:S(2)}) async-start(bf16[32,24,128]{2,1,0:T(8,128)(2,1)} %broadcast_in_dim.56), calls=%async_computation.9 | async-start | bytes 393216 | tf_op jit(solution)/shard_map/all_to_all | solution.py:23
  212.6 52.9 %copy-start.1 = (bf16[1,8,1,16,4096]{4,3,2,1,0:T(8,128)(2,1)S(1)}, bf16[1,8,1,16,4096]{4,3,2,1,0:T(8,128)(2,1)}, u32[]{:S(2)}) copy-start(bf16[1,8,1,16,4096]{4,3,2,1,0:T(8,128)(2,1)} %get-tuple-element.90) | copy-start | bytes 3145732
  212.6 67.2 %copy-start = (bf16[1,8,1,16,4096]{4,3,2,1,0:T(8,128)(2,1)S(1)}, bf16[1,8,1,16,4096]{4,3,2,1,0:T(8,128)(2,1)}, u32[]{:S(2)}) copy-start(bf16[1,8,1,16,4096]{4,3,2,1,0:T(8,128)(2,1)} %get-tuple-element.89) | copy-start | bytes 3145732
  214.4 0.6 copy-start.26
  233.9 1.7 copy-start.14
  235.6 16.0 %copy-start.27 = (bf16[24,128]{1,0:T(8,128)(2,1)}, bf16[24,128]{1,0:T(8,128)(2,1)S(1)}, u32[]{:S(2)}) copy-start(bf16[24,128]{1,0:T(8,128)(2,1)S(1)} %fusion.24) | copy-start | bytes 18436
  250.0 31.0 %copy-start.10 = (bf16[32,24,128]{2,1,0:T(8,128)(2,1)}, bf16[32,24,128]{2,1,0:T(8,128)(2,1)S(1)}, u32[]{:S(2)}) copy-start(bf16[32,24,128]{2,1,0:T(8,128)(2,1)S(1)} %all_to_all.109) | copy-start | bytes 589828
  251.7 0.6 copy-start.28
  265.5 15.4 %copy-start.16 = (bf16[32,24,128]{2,1,0:T(8,128)(2,1)}, bf16[32,24,128]{2,1,0:T(8,128)(2,1)S(1)}, u32[]{:S(2)}) copy-start(bf16[32,24,128]{2,1,0:T(8,128)(2,1)S(1)} %all_to_all.110) | copy-start | bytes 589828
  266.6 14.4 %copy-start.29 = (bf16[24,128]{1,0:T(8,128)(2,1)}, bf16[24,128]{1,0:T(8,128)(2,1)S(1)}, u32[]{:S(2)}) copy-start(bf16[24,128]{1,0:T(8,128)(2,1)S(1)} %fusion.26) | copy-start | bytes 18436
  279.8 1.1 copy-start.12
  281.0 0.6 copy-start.30
  282.2 14.2 %all-to-all-start.14 = ((bf16[32,24,128]{2,1,0:T(8,128)(2,1)}), bf16[32,24,128]{2,1,0:T(8,128)(2,1)}, u32[]{:S(2)}, u32[]{:S(2)}) async-start(bf16[32,24,128]{2,1,0:T(8,128)(2,1)} %broadcast_in_dim.61), calls=%async_computation.14 | async-start | bytes 393216 | tf_op jit(solution)/shard_map/all_to_all | solution.py:23
  298.1 0.6 copy-start.31
  299.5 14.6 %all-to-all-start.15 = ((bf16[32,24,128]{2,1,0:T(8,128)(2,1)}), bf16[32,24,128]{2,1,0:T(8,128)(2,1)}, u32[]{:S(2)}, u32[]{:S(2)}) async-start(bf16[32,24,128]{2,1,0:T(8,128)(2,1)} %broadcast_in_dim.62), calls=%async_computation.15 | async-start | bytes 393216 | tf_op jit(solution)/shard_map/all_to_all | solution.py:23
  305.0 20.7 %copy-start.32 = (bf16[24,128]{1,0:T(8,128)(2,1)S(1)}, bf16[24,128]{1,0:T(8,128)(2,1)}, u32[]{:S(2)}) copy-start(bf16[24,128]{1,0:T(8,128)(2,1)} %copy-done.31) | copy-start | bytes 18436
  316.4 18.8 %all-to-all-start.16 = ((bf16[32,24,128]{2,1,0:T(8,128)(2,1)}), bf16[32,24,128]{2,1,0:T(8,128)(2,1)}, u32[]{:S(2)}, u32[]{:S(2)}) async-start(bf16[32,24,128]{2,1,0:T(8,128)(2,1)} %broadcast_in_dim.63), calls=%async_computation.16 | async-start | bytes 393216 | tf_op jit(solution)/shard_map/all_to_all | solution.py:23
  338.5 16.1 %all-to-all-start.17 = ((f32[32,27,128]{2,1,0:T(8,128)}), f32[32,27,128]{2,1,0:T(8,128)S(1)}, u32[]{:S(2)}, u32[]{:S(2)}) async-start(f32[32,27,128]{2,1,0:T(8,128)} %pad_maximum_fusion.2), calls=%async_computation.17 | async-start | bytes 1048576 | tf_op jit(solution)/shard_map/all_to_all | solution.py:124
  342.6 9.5 %copy-start.3 = (bf16[32,24,128]{2,1,0:T(8,128)(2,1)S(1)}, bf16[32,24,128]{2,1,0:T(8,128)(2,1)}, u32[]{:S(2)}) copy-start(bf16[32,24,128]{2,1,0:T(8,128)(2,1)} %copy-done.2) | copy-start | bytes 589828
  342.6 9.5 %copy-start.7 = (bf16[32,24,128]{2,1,0:T(8,128)(2,1)S(1)}, bf16[32,24,128]{2,1,0:T(8,128)(2,1)}, u32[]{:S(2)}) copy-start(bf16[32,24,128]{2,1,0:T(8,128)(2,1)} %copy-done.6) | copy-start | bytes 589828
  342.7 9.5 %copy-start.9 = (bf16[32,24,128]{2,1,0:T(8,128)(2,1)S(1)}, bf16[32,24,128]{2,1,0:T(8,128)(2,1)}, u32[]{:S(2)}) copy-start(bf16[32,24,128]{2,1,0:T(8,128)(2,1)} %copy-done.8) | copy-start | bytes 589828
  342.7 9.5 %copy-start.15 = (bf16[32,24,128]{2,1,0:T(8,128)(2,1)S(1)}, bf16[32,24,128]{2,1,0:T(8,128)(2,1)}, u32[]{:S(2)}) copy-start(bf16[32,24,128]{2,1,0:T(8,128)(2,1)} %copy-done.14) | copy-start | bytes 589828
  342.7 9.5 %copy-start.17 = (bf16[32,24,128]{2,1,0:T(8,128)(2,1)S(1)}, bf16[32,24,128]{2,1,0:T(8,128)(2,1)}, u32[]{:S(2)}) copy-start(bf16[32,24,128]{2,1,0:T(8,128)(2,1)} %copy-done.16) | copy-start | bytes 589828
  352.2 3.3 copy-start.5
  352.2 3.3 copy-start.11
  352.2 3.3 copy-start.13
  361.2 46.7 %copy-start.19 = (bf16[512,512]{1,0:T(8,128)(2,1)S(1)}, bf16[512,512]{1,0:T(8,128)(2,1)}, u32[]{:S(2)}) copy-start(bf16[512,512]{1,0:T(8,128)(2,1)} %param.13) | copy-start | bytes 1572868
  361.8 17.9 %all-to-all-start.18 = ((bf16[32,3,128]{2,1,0:T(4,128)(2,1)}), bf16[32,3,128]{2,1,0:T(4,128)(2,1)S(1)}, u32[]{:S(2)}, u32[]{:S(2)}) async-start(bf16[32,3,128]{2,1,0:T(4,128)(2,1)} %broadcast_in_dim.65), calls=%async_computation.18 | async-start | bytes 65536 | tf_op jit(solution)/shard_map/all_to_all | solution.py:23
Sparse Core Ops, SparseCore 0:
  37.2 52.1 all-gather.8
  91.6 43.7 all-gather.10
  138.1 67.2 all-gather.12
  207.4 96.8 all-gather.14

commit v8 on v7

--- a/solution.py
+++ b/solution.py
@@ -13,7 +13,7 @@
 DEAL = ("yl", "x")
 COPY = ("c", "z")
 CHAIN = ("yl", "x", "yh")
-CHUNKS = (2, 2, 4)
+CHUNKS = (2, 3, 3)
 OUT_AFTER = 2
 
 
@@ -44,21 +44,19 @@
     width = rhs_count // copies
     mine = lax.axis_index(COPY)
 
-    weights = pattern.astype(jnp.bfloat16)[0, :, None, :, None]
-    masked = (coupling.reshape(local_rows // TILE, TILE, node_count // TILE, TILE) * weights).reshape(
-        local_rows, node_count
-    )
+    weights = jnp.repeat(pattern.astype(jnp.bfloat16)[0], TILE, axis=1)
+    masked = coupling[0] * weights
     upper = lax.axis_size("yh")
     order = chain_order(deal, lower, piece)
 
     def reorder(rows):
-        moved = jnp.einsum(
-            "ryzl,zlum->ruym",
-            rows.reshape(local_rows, upper, lower, TILE),
-            order,
-            preferred_element_type=jnp.float32,
-        )
-        return moved.astype(jnp.bfloat16).reshape(local_rows, node_count)
+        span = node_count // upper
+        table = order.reshape(span, span)
+        moved = [
+            jnp.dot(rows[:, at : at + span], table, preferred_element_type=jnp.float32).astype(jnp.bfloat16)
+            for at in range(0, node_count, span)
+        ]
+        return jnp.concatenate([block[:, at : at + TILE] for at in range(0, span, TILE) for block in moved], 1)
 
     initial = jnp.zeros((8, node_count), jnp.bfloat16)
     entering = jnp.where(lax.axis_index(DEAL + ("c",)) == 0, product(masked, initial)[:, :1], 0.0)

time: 419 us -> 408 us (0.974)
  blocking collectives: 223 us -> 209 us
  local copies, waits for them, and re-layouts: 44.7 us -> 37.7 us
  waiting for transfers between devices: 45.3 us -> 51.4 us
    all_to_all x10 -> x9, blocking collectives: 153 us -> 134 us  [spread(): return lax.all_to_all(copies, axis, 0, 0)]
    all_to_all x6 -> x7, waiting for transfers between devices: 28.4 us -> 42.5 us  [spread(): return lax.all_to_all(copies, axis, 0, 0)]
    all_gather x1, waiting for transfers between devices: 8.74 us -> 0.02 us  [per_device(): links.append(lax.all_gather(third, COPY, axis=0))]
    dot_general x2 -> x8, matrix products: 3.11 us -> 9.04 us  [reorder(): jnp.dot(rows[:, at:at + span], table, preferred_element_type=jnp.float32)]
    dot_general x16, matrix products: 12.7 us -> 7.07 us  [per_device(): jnp.dot(parts[step], held, preferred_element_type=jnp.float32)]
    all_to_all x1, blocking collectives: 27.9 us -> 32.7 us  [per_device(): arrived = lax.all_to_all(sent, COPY, 0, 0)]
    unnamed x74 -> x161, local copies, waits for them, and re-layouts: 8.75 us -> 4.75 us
    all_to_all x6 -> x7, starting transfers between devices: 36.9 us -> 39.5 us  [spread(): return lax.all_to_all(copies, axis, 0, 0)]
  transfers between devices with their start and end apart: 11 -> 12, of which waited for: 7 -> 8; matrix products, arithmetic and copies ran while one was open for 16% -> 16% of each run, Pallas kernels for 0% -> 0%
where the time goes in v8:
time: 408 us; the launch traced here: 406 us
  blocking collectives  209 us (51%)
  waiting for transfers between devices  51.4 us (13%)
  matrix products  44.6 us (11%)
  starting transfers between devices  43.7 us (11%)
  local copies, waits for them, and re-layouts  37.7 us (9%)
  between operations  15.2 us (4%)
  other arithmetic  4.75 us (1%)
    all_to_all x9, blocking collectives, spread(): return lax.all_to_all(copies, axis, 0, 0)  134 us
    all_to_all x7, waiting for transfers between devices, spread(): return lax.all_to_all(copies, axis, 0, 0)  42.5 us
    all_to_all x7, starting transfers between devices, spread(): return lax.all_to_all(copies, axis, 0, 0)  39.5 us
    all_to_all x1, blocking collectives, per_device(): arrived = lax.all_to_all(sent, COPY, 0, 0)  32.7 us
    dot_general x22, matrix products, product(): lax.dot_general(left, right, CONTRACT, preferred_element_type=jnp.float32)  28.5 us
    all_to_all x1, blocking collectives, per_device(): lax.all_to_all(forcing, COPY, 0, 0)  22.7 us
    all_to_all x1, blocking collectives, per_device(): rows = lax.all_to_all(rows.reshape(deal, piece, -1), DEAL, 0, 0)  19.8 us
    slice x3, local copies, waits for them, and re-layouts, of_step(): held.reshape(cores, lower, *held.shape[1:])[core, :, pair]  12.8 us
  transfers between devices with their start and end apart: 12, of which 8 were waited for; matrix products, arithmetic and copies ran while one was open for 16% of the time, Pallas kernels for 0%

profile of v8, /device:TPU:1, one launch (start us, length us, event | category | flops | bytes accessed | tf_op | source)
XLA Modules:
  0.0 406.2 jit_solution(7877680288061989770)
XLA Ops:
  8.1 1.3 bitcast_multiply_fusion
  9.4 0.9 fusion.41
  10.3 0.9 fusion.38
  11.3 0.9 fusion.35
  12.2 0.9 fusion.32
  14.6 19.8 %all_to_all.100 = bf16[8,16,4992]{2,1,0:T(8,128)(2,1)S(1)} all-to-all(bf16[8,16,4992]{2,1,0:T(8,128)(2,1)S(1)} %bitcast.377), channel_id=1, replica_groups=mesh['yl'=2,'x'=4,'c'=2,'yh'=4,'z'=8] {'yl','x'}, dimensions={0} | all-to-all | bytes 2555904 | tf_op jit(solution)/shard_map/all_to_all | solution.py:65
  36.3 22.7 %all_to_all.101 = bf16[16,128,24]{1,2,0:T(8,128)(2,1)S(1)} all-to-all(bf16[16,128,24]{1,2,0:T(8,128)(2,1)S(1)} %copy.102), channel_id=1, replica_groups=mesh['yl'=2,'x'=4,'c'=2,'yh'=4,'z'=8] {'c','z'}, dimensions={0} | all-to-all | bytes 196608 | tf_op jit(solution)/shard_map/all_to_all | solution.py:70
  61.3 6.6 %all-to-all-start.2 = ((bf16[32,24,128]{2,1,0:T(8,128)(2,1)}), bf16[32,24,128]{2,1,0:T(8,128)(2,1)S(1)}, u32[]{:S(2)}, u32[]{:S(2)}) async-start(bf16[32,24,128]{2,1,0:T(8,128)(2,1)} %broadcast_in_dim.55), calls=%async_computation.2 | async-start | bytes 393216 | tf_op jit(solution)/shard_map/all_to_all | solution.py:23
  68.8 8.7 %all-to-all-done.2 = bf16[32,24,128]{2,1,0:T(8,128)(2,1)S(1)} async-done(((bf16[32,24,128]{2,1,0:T(8,128)(2,1)}), bf16[32,24,128]{2,1,0:T(8,128)(2,1)S(1)}, u32[]{:S(2)}, u32[]{:S(2)}) %all-to-all-start.2) | async-done | bytes 196640 | tf_op jit(solution)/shard_map/all_to_all | solution.py:23
  77.8 1.8 fusion.65
  79.6 1.9 fusion.62
  81.6 0.9 fusion.59
  82.5 0.9 fusion.56
  84.2 1.0 pad_maximum_fusion
  85.2 2.4 all-gather.9.cloned.1.call-done
  87.5 2.1 fusion.162
  90.2 18.9 %all_to_all.102 = bf16[32,24,128]{2,1,0:T(8,128)(2,1)S(1)} all-to-all(bf16[32,24,128]{2,1,0:T(8,128)(2,1)S(1)} %broadcast_in_dim.56), channel_id=1, replica_groups=mesh['yl'=2,'x'=4,'c'=2,'yh'=4,'z'=8] {'yl','x','yh'}, dimensions={0} | all-to-all | bytes 393216 | tf_op jit(solution)/shard_map/all_to_all | solution.py:23
  109.0 1.1 fusion.71
  110.2 14.3 %all_to_all.103 = bf16[32,24,128]{2,1,0:T(8,128)(2,1)S(1)} all-to-all(bf16[32,24,128]{2,1,0:T(8,128)(2,1)S(1)} %broadcast_in_dim.57), channel_id=1, replica_groups=mesh['yl'=2,'x'=4,'c'=2,'yh'=4,'z'=8] {'yl','x','yh'}, dimensions={0} | all-to-all | bytes 393216 | tf_op jit(solution)/shard_map/all_to_all | solution.py:23
  124.5 1.1 fusion.72
  126.3 4.6 %all-to-all-start.5 = ((bf16[32,24,128]{2,1,0:T(8,128)(2,1)}), bf16[32,24,128]{2,1,0:T(8,128)(2,1)}, u32[]{:S(2)}, u32[]{:S(2)}) async-start(bf16[32,24,128]{2,1,0:T(8,128)(2,1)} %broadcast_in_dim.58), calls=%async_computation.5 | async-start | bytes 393216 | tf_op jit(solution)/shard_map/all_to_all | solution.py:23
  130.8 6.4 %all-gather.11.cloned.1.call-done = bf16[48,16,4096]{2,1,0:T(8,128)(2,1)} async-done(((bf16[3,16,4096]{2,1,0:T(8,128)(2,1)}), bf16[48,16,4096]{2,1,0:T(8,128)(2,1)}) %all-gather.11.cloned.1.call-update) | async-done | bytes 6291472 | tf_op jit(solution)/shard_map/all_gather | solution.py:74
  137.2 4.7 %fusion.161 = (bf16[1,8,1,16,4096]{4,3,2,1,0:T(8,128)(2,1)}, bf16[1,8,1,16,4096]{4,3,2,1,0:T(8,128)(2,1)S(1)}, bf16[1,8,1,16,4096]{4,3,2,1,0:T(8,128)(2,1)S(1)},...) fusion(bf16[2,8,3,16,4096]{4,3,2,1,0:T(8,128)(2,1)} %bitcast.341), kind=kLoop, calls=%fused_computation.272 | loop fusion | bytes 12582912 | tf_op jit(solution)/shard_map/slice | solution.py:79
  141.9 1.7 fusion.73
  144.3 19.0 %all_to_all.104 = bf16[32,24,128]{2,1,0:T(8,128)(2,1)S(1)} all-to-all(bf16[32,24,128]{2,1,0:T(8,128)(2,1)S(1)} %broadcast_in_dim.59), channel_id=1, replica_groups=mesh['yl'=2,'x'=4,'c'=2,'yh'=4,'z'=8] {'yl','x','yh'}, dimensions={0} | all-to-all | bytes 393216 | tf_op jit(solution)/shard_map/all_to_all | solution.py:23
  163.3 1.1 fusion.74
  164.4 14.3 %all_to_all.105 = bf16[32,24,128]{2,1,0:T(8,128)(2,1)S(1)} all-to-all(bf16[32,24,128]{2,1,0:T(8,128)(2,1)S(1)} %broadcast_in_dim.60), channel_id=1, replica_groups=mesh['yl'=2,'x'=4,'c'=2,'yh'=4,'z'=8] {'yl','x','yh'}, dimensions={0} | all-to-all | bytes 393216 | tf_op jit(solution)/shard_map/all_to_all | solution.py:23
  178.7 1.1 fusion.75
  179.8 13.2 %all_to_all.106 = bf16[32,24,128]{2,1,0:T(8,128)(2,1)S(1)} all-to-all(bf16[32,24,128]{2,1,0:T(8,128)(2,1)S(1)} %broadcast_in_dim.61), channel_id=1, replica_groups=mesh['yl'=2,'x'=4,'c'=2,'yh'=4,'z'=8] {'yl','x','yh'}, dimensions={0} | all-to-all | bytes 393216 | tf_op jit(solution)/shard_map/all_to_all | solution.py:23
  193.0 1.1 fusion.76
  194.2 13.2 %all_to_all.107 = bf16[32,24,128]{2,1,0:T(8,128)(2,1)S(1)} all-to-all(bf16[32,24,128]{2,1,0:T(8,128)(2,1)S(1)} %broadcast_in_dim.62), channel_id=1, replica_groups=mesh['yl'=2,'x'=4,'c'=2,'yh'=4,'z'=8] {'yl','x','yh'}, dimensions={0} | all-to-all | bytes 393216 | tf_op jit(solution)/shard_map/all_to_all | solution.py:23
  207.4 1.1 fusion.77
  208.6 12.9 %all_to_all.108 = bf16[32,24,128]{2,1,0:T(8,128)(2,1)S(1)} all-to-all(bf16[32,24,128]{2,1,0:T(8,128)(2,1)S(1)} %broadcast_in_dim.63), channel_id=1, replica_groups=mesh['yl'=2,'x'=4,'c'=2,'yh'=4,'z'=8] {'yl','x','yh'}, dimensions={0} | all-to-all | bytes 393216 | tf_op jit(solution)/shard_map/all_to_all | solution.py:23
  221.5 1.1 fusion.78
  223.9 4.8 %all-to-all-start.11 = ((bf16[32,24,128]{2,1,0:T(8,128)(2,1)}), bf16[32,24,128]{2,1,0:T(8,128)(2,1)}, u32[]{:S(2)}, u32[]{:S(2)}) async-start(bf16[32,24,128]{2,1,0:T(8,128)(2,1)} %broadcast_in_dim.64), calls=%async_computation.11 | async-start | bytes 393216 | tf_op jit(solution)/shard_map/all_to_all | solution.py:23
  228.8 6.0 %fusion.160 = (bf16[1,8,1,16,4096]{4,3,2,1,0:T(8,128)(2,1)S(1)}, bf16[1,8,1,16,4096]{4,3,2,1,0:T(8,128)(2,1)S(1)}, bf16[1,8,1,16,4096]{4,3,2,1,0:T(8,128)(2,1)S(...) fusion(bf16[2,8,4,16,4096]{4,3,2,1,0:T(8,128)(2,1)} %bitcast.340), kind=kLoop, calls=%fused_computation.271 | loop fusion | bytes 16777216 | tf_op jit(solution)/shard_map/slice | solution.py:79
  234.7 3.4 all-to-all-done.11
  238.1 1.8 fusion.79
  240.6 15.0 %all_to_all.109 = bf16[32,24,128]{2,1,0:T(8,128)(2,1)S(1)} all-to-all(bf16[32,24,128]{2,1,0:T(8,128)(2,1)S(1)} %broadcast_in_dim.65), channel_id=1, replica_groups=mesh['yl'=2,'x'=4,'c'=2,'yh'=4,'z'=8] {'yl','x','yh'}, dimensions={0} | all-to-all | bytes 393216 | tf_op jit(solution)/shard_map/all_to_all | solution.py:23
  255.6 1.1 fusion.80
  256.8 13.0 %all_to_all.110 = bf16[32,24,128]{2,1,0:T(8,128)(2,1)S(1)} all-to-all(bf16[32,24,128]{2,1,0:T(8,128)(2,1)S(1)} %broadcast_in_dim.66), channel_id=1, replica_groups=mesh['yl'=2,'x'=4,'c'=2,'yh'=4,'z'=8] {'yl','x','yh'}, dimensions={0} | all-to-all | bytes 393216 | tf_op jit(solution)/shard_map/all_to_all | solution.py:23
  269.7 1.1 fusion.81
  272.2 4.6 %all-to-all-start.14 = ((bf16[32,24,128]{2,1,0:T(8,128)(2,1)}), bf16[32,24,128]{2,1,0:T(8,128)(2,1)}, u32[]{:S(2)}, u32[]{:S(2)}) async-start(bf16[32,24,128]{2,1,0:T(8,128)(2,1)} %broadcast_in_dim.67), calls=%async_computation.14 | async-start | bytes 393216 | tf_op jit(solution)/shard_map/all_to_all | solution.py:23
  276.8 9.6 %all-to-all-done.14 = bf16[32,24,128]{2,1,0:T(8,128)(2,1)} async-done(((bf16[32,24,128]{2,1,0:T(8,128)(2,1)}), bf16[32,24,128]{2,1,0:T(8,128)(2,1)}, u32[]{:S(2)}, u32[]{:S(2)}) %all-to-all-start.14) | async-done | bytes 196640 | tf_op jit(solution)/shard_map/all_to_all | solution.py:23
  286.4 1.6 fusion.82
  289.3 4.6 %all-to-all-start.15 = ((bf16[32,24,128]{2,1,0:T(8,128)(2,1)}), bf16[32,24,128]{2,1,0:T(8,128)(2,1)}, u32[]{:S(2)}, u32[]{:S(2)}) async-start(bf16[32,24,128]{2,1,0:T(8,128)(2,1)} %broadcast_in_dim.68), calls=%async_computation.15 | async-start | bytes 393216 | tf_op jit(solution)/shard_map/all_to_all | solution.py:23
  293.9 0.9 fusion.144
  295.1 0.8 convolution_add_fusion.15
  295.9 0.8 convolution_add_fusion.14
  299.3 4.3 %all-to-all-done.15 = bf16[32,24,128]{2,1,0:T(8,128)(2,1)} async-done(((bf16[32,24,128]{2,1,0:T(8,128)(2,1)}), bf16[32,24,128]{2,1,0:T(8,128)(2,1)}, u32[]{:S(2)}, u32[]{:S(2)}) %all-to-all-start.15) | async-done | bytes 196640 | tf_op jit(solution)/shard_map/all_to_all | solution.py:23
  303.5 1.6 fusion.83
  305.9 4.9 %all-to-all-start.16 = ((bf16[32,24,128]{2,1,0:T(8,128)(2,1)}), bf16[32,24,128]{2,1,0:T(8,128)(2,1)}, u32[]{:S(2)}, u32[]{:S(2)}) async-start(bf16[32,24,128]{2,1,0:T(8,128)(2,1)} %broadcast_in_dim.69), calls=%async_computation.16 | async-start | bytes 393216 | tf_op jit(solution)/shard_map/all_to_all | solution.py:23
  310.8 0.9 convolution_add_fusion.5
  312.5 7.9 %all-to-all-done.16 = bf16[32,24,128]{2,1,0:T(8,128)(2,1)} async-done(((bf16[32,24,128]{2,1,0:T(8,128)(2,1)}), bf16[32,24,128]{2,1,0:T(8,128)(2,1)}, u32[]{:S(2)}, u32[]{:S(2)}) %all-to-all-start.16) | async-done | bytes 196640 | tf_op jit(solution)/shard_map/all_to_all | solution.py:23
  320.4 1.3 fusion.84
  322.0 0.8 pad_maximum_fusion.1
  322.9 3.9 all-to-all-start.17
  326.8 9.5 %fusion.159 = (bf16[8,128,4096]{2,1,0:T(8,128)(2,1)S(1)}, bf16[8,128,4096]{2,1,0:T(8,128)(2,1)}) fusion(bf16[16,128,4096]{2,1,0:T(8,128)(2,1)} %bitcast.339), kind=kLoop, calls=%fused_computation.270 | loop fusion | bytes 33554432 | tf_op jit(solution)/shard_map/slice | solution.py:137
  336.4 2.3 fusion.68
  339.6 5.7 %fusion.69 = bf16[3,8,8,128]{3,1,2,0:T(8,128)(2,1)S(1)} fusion(bf16[1024,4096]{1,0:T(8,128)(2,1)} %bitcast.337, bf16[32,24,128]{2,1,0:T(8,128)(2,1)S(1)} %slice.874, bf16[32,24,128]{2,1,0:T(8,128)(2,1)} %all-to-all-done.15, bf16[32,24,128]{2,1,0:T(8,128)(2,1)S(1)} %copy-done.17, bf16[32,24,128]{2,1,0:T(8,128)(2,1)} %all-to-all-done.11, ...), kind=kOutput, calls=%fused_computation.50 | convolution fusion | flops 202039296 | bytes 10010631 | tf_op jit(solution)/shard_map/dot_general | solution.py:33
  346.0 9.5 %all-to-all-start.18 = ((bf16[32,3,128]{2,1,0:T(4,128)(2,1)}), bf16[32,3,128]{2,1,0:T(4,128)(2,1)S(1)}, u32[]{:S(2)}, u32[]{:S(2)}) async-start(bf16[32,3,128]{2,1,0:T(4,128)(2,1)} %broadcast_in_dim.140), calls=%async_computation.18 | async-start | bytes 65536 | tf_op jit(solution)/shard_map/all_to_all | solution.py:23
  355.5 8.6 %all-to-all-done.18 = bf16[32,3,128]{2,1,0:T(4,128)(2,1)S(1)} async-done(((bf16[32,3,128]{2,1,0:T(4,128)(2,1)}), bf16[32,3,128]{2,1,0:T(4,128)(2,1)S(1)}, u32[]{:S(2)}, u32[]{:S(2)}) %all-to-all-start.18) | async-done | bytes 24608 | tf_op jit(solution)/shard_map/all_to_all | solution.py:23
  364.3 32.7 %all_to_all.111 = bf16[16,120,128]{2,1,0:T(8,128)(2,1)S(1)} all-to-all(bf16[16,120,128]{2,1,0:T(8,128)(2,1)S(1)} %pad_maximum_fusion.2), channel_id=1, replica_groups=mesh['yl'=2,'x'=4,'c'=2,'yh'=4,'z'=8] {'c','z'}, dimensions={0} | all-to-all | bytes 983040 | tf_op jit(solution)/shard_map/all_to_all | solution.py:142
  397.9 1.1 convolution_add_fusion
  (245 shorter events, 22.7 us)
Async XLA Ops:
  7.2 80.4 %all-gather.9.cloned.1.call-start = ((), (), s32[]{:S(2)}) async-start(), calls=%async_computation.20 | async-start | bytes 4456448 | tf_op jit(solution)/shard_map/all_gather | solution.py:69
  12.2 0.9 copy-start.25
  12.2 1.1 copy-start.24
  60.5 29.1 %copy-start.22 = (bf16[16,24,128]{2,1,0:T(8,128)(2,1)}, bf16[16,24,128]{2,1,0:T(8,128)(2,1)S(1)}, u32[]{:S(2)}) copy-start(bf16[16,24,128]{2,1,0:T(8,128)(2,1)S(1)} %reshape.345) | copy-start | bytes 294916
  60.5 7.3 %copy-start.45 = (bf16[24,128]{1,0:T(8,128)(2,1)}, bf16[24,128]{1,0:T(8,128)(2,1)S(1)}, u32[]{:S(2)}) copy-start(bf16[24,128]{1,0:T(8,128)(2,1)S(1)} %slice_bitcast_fusion.2) | copy-start | bytes 18436
  61.3 16.2 %all-to-all-start.2 = ((bf16[32,24,128]{2,1,0:T(8,128)(2,1)}), bf16[32,24,128]{2,1,0:T(8,128)(2,1)S(1)}, u32[]{:S(2)}, u32[]{:S(2)}) async-start(bf16[32,24,128]{2,1,0:T(8,128)(2,1)} %broadcast_in_dim.55), calls=%async_computation.2 | async-start | bytes 393216 | tf_op jit(solution)/shard_map/all_to_all | solution.py:23
  67.9 69.3 %all-gather.11.cloned.1.call-start = ((), (), s32[]{:S(2)}) async-start(), calls=%async_computation.21 | async-start | bytes 6684672 | tf_op jit(solution)/shard_map/all_gather | solution.py:74
  77.5 151.2 %all-gather.13.cloned.1.call-start = ((), (), s32[]{:S(2)}) async-start(), calls=%async_computation.22 | async-start | bytes 8912896 | tf_op jit(solution)/shard_map/all_gather | solution.py:98
  79.6 2.0 copy-start.46
  84.0 5.6 %copy-start.20 = (bf16[128,4096]{1,0:T(8,128)(2,1)}, bf16[128,4096]{1,0:T(8,128)(2,1)S(1)}, u32[]{:S(2)}) copy-start(bf16[128,4096]{1,0:T(8,128)(2,1)S(1)} %constant_dynamic-update-slice_fusion.34) | copy-start | bytes 3145732
  90.1 231.7 %all-gather.15.cloned.1.call-start = ((), (), s32[]{:S(2)}) async-start(), calls=%async_computation.23 | async-start | bytes 17825792 | tf_op jit(solution)/shard_map/all_gather | solution.py:101
  124.5 12.8 %copy-start.4 = (bf16[32,24,128]{2,1,0:T(8,128)(2,1)}, bf16[32,24,128]{2,1,0:T(8,128)(2,1)S(1)}, u32[]{:S(2)}) copy-start(bf16[32,24,128]{2,1,0:T(8,128)(2,1)S(1)} %all_to_all.103) | copy-start | bytes 589828
  125.5 11.7 %copy-start.26 = (bf16[24,128]{1,0:T(8,128)(2,1)}, bf16[24,128]{1,0:T(8,128)(2,1)S(1)}, u32[]{:S(2)}) copy-start(bf16[24,128]{1,0:T(8,128)(2,1)S(1)} %fusion.72) | copy-start | bytes 18436
  126.3 15.7 %all-to-all-start.5 = ((bf16[32,24,128]{2,1,0:T(8,128)(2,1)}), bf16[32,24,128]{2,1,0:T(8,128)(2,1)}, u32[]{:S(2)}, u32[]{:S(2)}) async-start(bf16[32,24,128]{2,1,0:T(8,128)(2,1)} %broadcast_in_dim.58), calls=%async_computation.5 | async-start | bytes 393216 | tf_op jit(solution)/shard_map/all_to_all | solution.py:23
  141.9 21.3 %copy-start.3 = (bf16[1,8,1,16,4096]{4,3,2,1,0:T(8,128)(2,1)S(1)}, bf16[1,8,1,16,4096]{4,3,2,1,0:T(8,128)(2,1)}, u32[]{:S(2)}) copy-start(bf16[1,8,1,16,4096]{4,3,2,1,0:T(8,128)(2,1)} %get-tuple-element.97) | copy-start | bytes 3145732
  143.7 0.6 copy-start.27
  144.3 34.4 %copy-start.1 = (bf16[1,8,1,16,4096]{4,3,2,1,0:T(8,128)(2,1)S(1)}, bf16[1,8,1,16,4096]{4,3,2,1,0:T(8,128)(2,1)}, u32[]{:S(2)}) copy-start(bf16[1,8,1,16,4096]{4,3,2,1,0:T(8,128)(2,1)} %get-tuple-element.96) | copy-start | bytes 3145732
  163.3 16.5 %copy-start.10 = (bf16[32,24,128]{2,1,0:T(8,128)(2,1)}, bf16[32,24,128]{2,1,0:T(8,128)(2,1)S(1)}, u32[]{:S(2)}) copy-start(bf16[32,24,128]{2,1,0:T(8,128)(2,1)S(1)} %all_to_all.104) | copy-start | bytes 589828
  164.3 29.8 %copy-start.28 = (bf16[24,128]{1,0:T(8,128)(2,1)}, bf16[24,128]{1,0:T(8,128)(2,1)S(1)}, u32[]{:S(2)}) copy-start(bf16[24,128]{1,0:T(8,128)(2,1)S(1)} %fusion.74) | copy-start | bytes 18436
  178.7 15.4 %copy-start.6 = (bf16[32,24,128]{2,1,0:T(8,128)(2,1)}, bf16[32,24,128]{2,1,0:T(8,128)(2,1)S(1)}, u32[]{:S(2)}) copy-start(bf16[32,24,128]{2,1,0:T(8,128)(2,1)S(1)} %all_to_all.105) | copy-start | bytes 589828
  179.8 28.7 %copy-start.29 = (bf16[24,128]{1,0:T(8,128)(2,1)}, bf16[24,128]{1,0:T(8,128)(2,1)S(1)}, u32[]{:S(2)}) copy-start(bf16[24,128]{1,0:T(8,128)(2,1)S(1)} %fusion.75) | copy-start | bytes 18436
  193.0 15.5 %copy-start.12 = (bf16[32,24,128]{2,1,0:T(8,128)(2,1)}, bf16[32,24,128]{2,1,0:T(8,128)(2,1)S(1)}, u32[]{:S(2)}) copy-start(bf16[32,24,128]{2,1,0:T(8,128)(2,1)S(1)} %all_to_all.106) | copy-start | bytes 589828
  194.1 28.5 %copy-start.31 = (bf16[24,128]{1,0:T(8,128)(2,1)}, bf16[24,128]{1,0:T(8,128)(2,1)S(1)}, u32[]{:S(2)}) copy-start(bf16[24,128]{1,0:T(8,128)(2,1)S(1)} %fusion.76) | copy-start | bytes 18436
  207.4 15.2 %copy-start.8 = (bf16[32,24,128]{2,1,0:T(8,128)(2,1)}, bf16[32,24,128]{2,1,0:T(8,128)(2,1)S(1)}, u32[]{:S(2)}) copy-start(bf16[32,24,128]{2,1,0:T(8,128)(2,1)S(1)} %all_to_all.107) | copy-start | bytes 589828
  208.5 14.1 %copy-start.33 = (bf16[24,128]{1,0:T(8,128)(2,1)}, bf16[24,128]{1,0:T(8,128)(2,1)S(1)}, u32[]{:S(2)}) copy-start(bf16[24,128]{1,0:T(8,128)(2,1)S(1)} %fusion.77) | copy-start | bytes 18436
  221.5 7.3 %copy-start.14 = (bf16[32,24,128]{2,1,0:T(8,128)(2,1)}, bf16[32,24,128]{2,1,0:T(8,128)(2,1)S(1)}, u32[]{:S(2)}) copy-start(bf16[32,24,128]{2,1,0:T(8,128)(2,1)S(1)} %all_to_all.108) | copy-start | bytes 589828
  222.6 0.6 copy-start.35
  223.9 14.2 %all-to-all-start.11 = ((bf16[32,24,128]{2,1,0:T(8,128)(2,1)}), bf16[32,24,128]{2,1,0:T(8,128)(2,1)}, u32[]{:S(2)}, u32[]{:S(2)}) async-start(bf16[32,24,128]{2,1,0:T(8,128)(2,1)} %broadcast_in_dim.64), calls=%async_computation.11 | async-start | bytes 393216 | tf_op jit(solution)/shard_map/all_to_all | solution.py:23
  238.1 17.5 %copy-start.2 = (bf16[1,8,1,16,4096]{4,3,2,1,0:T(8,128)(2,1)S(1)}, bf16[1,8,1,16,4096]{4,3,2,1,0:T(8,128)(2,1)}, u32[]{:S(2)}) copy-start(bf16[1,8,1,16,4096]{4,3,2,1,0:T(8,128)(2,1)} %get-tuple-element.90) | copy-start | bytes 3145732
  240.0 0.6 copy-start.37
  240.6 29.1 %copy-start = (bf16[1,8,1,16,4096]{4,3,2,1,0:T(8,128)(2,1)S(1)}, bf16[1,8,1,16,4096]{4,3,2,1,0:T(8,128)(2,1)}, u32[]{:S(2)}) copy-start(bf16[1,8,1,16,4096]{4,3,2,1,0:T(8,128)(2,1)} %get-tuple-element.89) | copy-start | bytes 3145732
  255.6 15.2 %copy-start.18 = (bf16[32,24,128]{2,1,0:T(8,128)(2,1)}, bf16[32,24,128]{2,1,0:T(8,128)(2,1)S(1)}, u32[]{:S(2)}) copy-start(bf16[32,24,128]{2,1,0:T(8,128)(2,1)S(1)} %all_to_all.109) | copy-start | bytes 589828
  256.7 14.1 %copy-start.39 = (bf16[24,128]{1,0:T(8,128)(2,1)}, bf16[24,128]{1,0:T(8,128)(2,1)S(1)}, u32[]{:S(2)}) copy-start(bf16[24,128]{1,0:T(8,128)(2,1)S(1)} %fusion.80) | copy-start | bytes 18436
  269.7 1.1 copy-start.16
  270.9 0.6 copy-start.41
  272.2 14.2 %all-to-all-start.14 = ((bf16[32,24,128]{2,1,0:T(8,128)(2,1)}), bf16[32,24,128]{2,1,0:T(8,128)(2,1)}, u32[]{:S(2)}, u32[]{:S(2)}) async-start(bf16[32,24,128]{2,1,0:T(8,128)(2,1)} %broadcast_in_dim.67), calls=%async_computation.14 | async-start | bytes 393216 | tf_op jit(solution)/shard_map/all_to_all | solution.py:23
  288.0 0.6 copy-start.43
  289.3 14.2 %all-to-all-start.15 = ((bf16[32,24,128]{2,1,0:T(8,128)(2,1)}), bf16[32,24,128]{2,1,0:T(8,128)(2,1)}, u32[]{:S(2)}, u32[]{:S(2)}) async-start(bf16[32,24,128]{2,1,0:T(8,128)(2,1)} %broadcast_in_dim.68), calls=%async_computation.15 | async-start | bytes 393216 | tf_op jit(solution)/shard_map/all_to_all | solution.py:23
  293.9 3.7 copy-start.30
  293.9 3.8 copy-start.32
  293.9 4.0 copy-start.34
  293.9 4.1 %copy-start.36 = (bf16[24,128]{1,0:T(8,128)(2,1)S(1)}, bf16[24,128]{1,0:T(8,128)(2,1)}, u32[]{:S(2)}) copy-start(bf16[24,128]{1,0:T(8,128)(2,1)} %copy-done.35) | copy-start | bytes 18436
  293.9 4.3 %copy-start.38 = (bf16[24,128]{1,0:T(8,128)(2,1)S(1)}, bf16[24,128]{1,0:T(8,128)(2,1)}, u32[]{:S(2)}) copy-start(bf16[24,128]{1,0:T(8,128)(2,1)} %copy-done.37) | copy-start | bytes 18436
  293.9 4.4 %copy-start.40 = (bf16[24,128]{1,0:T(8,128)(2,1)S(1)}, bf16[24,128]{1,0:T(8,128)(2,1)}, u32[]{:S(2)}) copy-start(bf16[24,128]{1,0:T(8,128)(2,1)} %copy-done.39) | copy-start | bytes 18436
  294.8 3.7 copy-start.42
  298.2 12.6 %copy-start.44 = (bf16[24,128]{1,0:T(8,128)(2,1)S(1)}, bf16[24,128]{1,0:T(8,128)(2,1)}, u32[]{:S(2)}) copy-start(bf16[24,128]{1,0:T(8,128)(2,1)} %copy-done.43) | copy-start | bytes 18436
  305.9 14.6 %all-to-all-start.16 = ((bf16[32,24,128]{2,1,0:T(8,128)(2,1)}), bf16[32,24,128]{2,1,0:T(8,128)(2,1)}, u32[]{:S(2)}, u32[]{:S(2)}) async-start(bf16[32,24,128]{2,1,0:T(8,128)(2,1)} %broadcast_in_dim.69), calls=%async_computation.16 | async-start | bytes 393216 | tf_op jit(solution)/shard_map/all_to_all | solution.py:23
  312.5 9.2 %copy-start.23 = (f32[24,512]{1,0:T(8,128)S(1)}, f32[24,512]{1,0:T(8,128)}, u32[]{:S(2)}) copy-start(f32[24,512]{1,0:T(8,128)} %convolution_add_fusion.4) | copy-start | bytes 147460
  322.9 15.9 %all-to-all-start.17 = ((f32[32,27,128]{2,1,0:T(8,128)}), f32[32,27,128]{2,1,0:T(8,128)S(1)}, u32[]{:S(2)}, u32[]{:S(2)}) async-start(f32[32,27,128]{2,1,0:T(8,128)} %pad_maximum_fusion.1), calls=%async_computation.17 | async-start | bytes 1048576 | tf_op jit(solution)/shard_map/all_to_all | solution.py:122
  326.8 9.5 %copy-start.5 = (bf16[32,24,128]{2,1,0:T(8,128)(2,1)S(1)}, bf16[32,24,128]{2,1,0:T(8,128)(2,1)}, u32[]{:S(2)}) copy-start(bf16[32,24,128]{2,1,0:T(8,128)(2,1)} %copy-done.4) | copy-start | bytes 589828
  326.8 9.5 %copy-start.11 = (bf16[32,24,128]{2,1,0:T(8,128)(2,1)S(1)}, bf16[32,24,128]{2,1,0:T(8,128)(2,1)}, u32[]{:S(2)}) copy-start(bf16[32,24,128]{2,1,0:T(8,128)(2,1)} %copy-done.10) | copy-start | bytes 589828
  326.8 9.5 %copy-start.13 = (bf16[32,24,128]{2,1,0:T(8,128)(2,1)S(1)}, bf16[32,24,128]{2,1,0:T(8,128)(2,1)}, u32[]{:S(2)}) copy-start(bf16[32,24,128]{2,1,0:T(8,128)(2,1)} %copy-done.12) | copy-start | bytes 589828
  326.8 9.5 %copy-start.15 = (bf16[32,24,128]{2,1,0:T(8,128)(2,1)S(1)}, bf16[32,24,128]{2,1,0:T(8,128)(2,1)}, u32[]{:S(2)}) copy-start(bf16[32,24,128]{2,1,0:T(8,128)(2,1)} %copy-done.14) | copy-start | bytes 589828
  326.8 9.5 %copy-start.19 = (bf16[32,24,128]{2,1,0:T(8,128)(2,1)S(1)}, bf16[32,24,128]{2,1,0:T(8,128)(2,1)}, u32[]{:S(2)}) copy-start(bf16[32,24,128]{2,1,0:T(8,128)(2,1)} %copy-done.18) | copy-start | bytes 589828
  336.4 3.3 copy-start.7
  336.4 3.3 copy-start.9
  336.4 3.3 copy-start.17
  346.0 18.1 %all-to-all-start.18 = ((bf16[32,3,128]{2,1,0:T(4,128)(2,1)}), bf16[32,3,128]{2,1,0:T(4,128)(2,1)S(1)}, u32[]{:S(2)}, u32[]{:S(2)}) async-start(bf16[32,3,128]{2,1,0:T(4,128)(2,1)} %broadcast_in_dim.140), calls=%async_computation.18 | async-start | bytes 65536 | tf_op jit(solution)/shard_map/all_to_all | solution.py:23
  364.3 32.8 %copy-start.21 = (bf16[512,512]{1,0:T(8,128)(2,1)S(1)}, bf16[512,512]{1,0:T(8,128)(2,1)}, u32[]{:S(2)}) copy-start(bf16[512,512]{1,0:T(8,128)(2,1)} %param.13) | copy-start | bytes 1572868
Sparse Core Ops, SparseCore 0:
  35.3 52.1 all-gather.8
  89.7 47.5 all-gather.10
  139.9 57.3 all-gather.12
  199.3 96.8 all-gather.14
